TPU v7x, 32 devices: a whole 2x2x4 slice. The times are simulated.
32 devices in a mesh: groups: 2 (over y), dp: 8 (over z, x), mp: 2 (over core).
Axes of the slice: x: 2, y: 2, z: 4, core: 2. Of those that a mesh axis runs over, the one named last changes fastest.
Arguments:
- tokens: bfloat16 [2048, 4096], P(('groups', 'dp'), 'mp'), parts along dimension 0, may hold values from -6 to 6
- cotangent: bfloat16 [2048, 4096], P(('groups', 'dp'), 'mp'), parts along dimension 0, may hold values from -6 to 6
- gate_spectra: bfloat16 [28, 8, 512], P('mp'), may hold values from -1.5 to 1.5
- up_spectra: bfloat16 [28, 8, 512], P('mp'), may hold values from -1.5 to 1.5
- down_spectra: bfloat16 [8, 28, 512], P('mp'), may hold values from -0.75 to 0.75
Outputs:
- grad_tokens: bfloat16 [2048, 4096], P(('groups', 'dp'), 'mp'), parts along dimension 0
- grad_gate: float32 [56, 8, 512], P(('groups', 'mp')), parts along dimension 0
- grad_up: float32 [56, 8, 512], P(('groups', 'mp')), parts along dimension 0
- grad_down: float32 [16, 28, 512], P(('groups', 'mp')), parts along dimension 0
There are 2 independent parts, one for each index of `groups`. A program takes and returns all parts, laid end to end along the dimension named above; an argument that names none is the same for every part. Nothing has to cross between parts.
All inputs are finite; a program needn't handle non-finite values.
Results may differ from a plain program's by a relative error of at most 0.012.
The roundings to bfloat16 on the way count: a program that leaves them out, or rounds other values in their place, can miss the bound.
Values may be sent and summed in bfloat16 or wider, within the bound.
No kernel may reach another device: no remote copies, remote signals or barrier semaphores. Data moves between devices by JAX's collectives and lax.ppermute only.
A program may use at most 128 MiB of HBM per device.

v0:
```python
import math

import jax
import jax.numpy as jnp
from jax import lax
from jax.sharding import PartitionSpec as P

BLOCK = 512


def transform_tables(block_size):
    half_size = block_size // 2
    positions = jnp.arange(block_size, dtype=jnp.int32)
    frequency = jnp.arange(half_size, dtype=jnp.int32)
    phase_index = positions[:, None] * frequency[None, :] % block_size
    angles = phase_index.astype(jnp.float32) * (2.0 * math.pi / block_size)
    cosine = jnp.cos(angles)
    sine_table = jnp.sin(angles)
    parity = (1 - 2 * (positions % 2)).astype(jnp.float32)
    norm_factor = 1.0 / math.sqrt(block_size)
    forward_table = (
        jnp.concatenate([cosine, parity[:, None], -sine_table[:, 1:]], axis=1) * norm_factor
    )
    doubling = jnp.where(frequency >= 1, 2.0, 1.0).astype(jnp.float32)
    inverse_table = (
        jnp.concatenate(
            [(cosine * doubling[None, :]).T, parity[None, :], -2.0 * sine_table[:, 1:].T], axis=0
        )
        * norm_factor
    )
    return (forward_table.astype(jnp.bfloat16), inverse_table.astype(jnp.bfloat16))


def to_spectra(values, table):
    row_count = values.shape[0]
    blocks = values.reshape(row_count, -1, table.shape[0])
    return jnp.einsum("tbn,nk->kbt", blocks, table, preferred_element_type=jnp.float32).astype(
        jnp.bfloat16
    )


def from_spectra(spectra, table):
    row_count = spectra.shape[2]
    flat = jnp.einsum("kbt,kn->tbn", spectra, table, preferred_element_type=jnp.float32)
    return flat.reshape(row_count, -1)


def product(pattern, left_operand, right_operand):
    return jnp.einsum(pattern, left_operand, right_operand, preferred_element_type=jnp.float32)


def weight_forms(weight):
    half_size = weight.shape[-1] // 2
    leading = jnp.transpose(weight, (2, 0, 1))
    mask_values = (jnp.arange(half_size) >= 1).astype(weight.dtype)[:, None, None]
    real_part = leading[:half_size]
    imag_part = leading[half_size:]
    return (
        real_part,
        imag_part * mask_values,
        real_part * mask_values + imag_part * (1 - mask_values),
    )


def forward_apply(spectra, forms):
    half_size = spectra.shape[0] // 2
    spec_real, spec_imag = (spectra[:half_size], spectra[half_size:])
    real_part, imag_masked, cross_part = forms
    out_real = product("kit,koi->kot", spec_real, real_part) - product(
        "kit,koi->kot", spec_imag, imag_masked
    )
    out_imag = product("kit,koi->kot", spec_real, imag_masked) + product(
        "kit,koi->kot", spec_imag, cross_part
    )
    return jnp.concatenate([out_real, out_imag], axis=0)


def adjoint_apply(spectra, forms):
    half_size = spectra.shape[0] // 2
    spec_real, spec_imag = (spectra[:half_size], spectra[half_size:])
    real_part, imag_masked, cross_part = forms
    out_real = product("kot,koi->kit", spec_real, real_part) + product(
        "kot,koi->kit", spec_imag, imag_masked
    )
    out_imag = product("kot,koi->kit", spec_imag, cross_part) - product(
        "kot,koi->kit", spec_real, imag_masked
    )
    return jnp.concatenate([out_real, out_imag], axis=0)


def weight_grad(source_spec, target_spec):
    half_size = source_spec.shape[0] // 2
    mask_values = (jnp.arange(half_size) >= 1).astype(jnp.float32)[:, None, None]
    source_real, source_imag = (source_spec[:half_size], source_spec[half_size:])
    target_real, target_imag = (target_spec[:half_size], target_spec[half_size:])
    both_real = product("kit,kot->koi", source_real, target_real)
    both_imag = product("kit,kot->koi", source_imag, target_imag)
    real_imag = product("kit,kot->koi", source_real, target_imag)
    imag_real = product("kit,kot->koi", source_imag, target_real)
    grad_real = (1.0 + mask_values) * (both_real + mask_values * both_imag)
    grad_imag = 2.0 * mask_values * (real_imag - imag_real) + (1.0 - mask_values) * both_imag
    return jnp.transpose(jnp.concatenate([grad_real, grad_imag], axis=0), (1, 2, 0))


def swiglu_back(gate_values, up_values, hidden_grad):
    sigmoid_gate = jax.nn.sigmoid(gate_values)
    gate_grad = (
        hidden_grad * up_values * sigmoid_gate * (1.0 + gate_values * (1.0 - sigmoid_gate))
    ).astype(jnp.bfloat16)
    up_grad = (hidden_grad * gate_values * sigmoid_gate).astype(jnp.bfloat16)
    return (gate_grad, up_grad)


def shards(tokens, cotangent, gate_spectra, up_spectra, down_spectra):
    forward_table, inverse_table = transform_tables(BLOCK)
    total_tokens = tokens.shape[0] * lax.axis_size("dp")
    gate_forms = weight_forms(gate_spectra)
    up_forms = weight_forms(up_spectra)
    local_spec = to_spectra(tokens, forward_table)
    token_spec = lax.all_gather(local_spec, "mp", axis=1, tiled=True)
    gate_values = from_spectra(
        forward_apply(token_spec, gate_forms).astype(jnp.bfloat16), inverse_table
    )
    up_values = from_spectra(
        forward_apply(token_spec, up_forms).astype(jnp.bfloat16), inverse_table
    )
    hidden = (gate_values * jax.nn.sigmoid(gate_values) * up_values).astype(jnp.bfloat16)
    hidden_spec = to_spectra(hidden, forward_table)
    cotangent_local = to_spectra(cotangent, forward_table)
    cotangent_spec = lax.all_gather(cotangent_local, "mp", axis=1, tiled=True)
    down_cols = lax.all_to_all(down_spectra, "mp", split_axis=1, concat_axis=0, tiled=True)
    hidden_grad = from_spectra(
        adjoint_apply(cotangent_spec, weight_forms(down_cols)).astype(jnp.bfloat16), inverse_table
    )
    gate_grad, up_grad = swiglu_back(gate_values, up_values, hidden_grad)
    gate_grad_spec = to_spectra(gate_grad, forward_table)
    up_grad_spec = to_spectra(up_grad, forward_table)
    partial_input = adjoint_apply(gate_grad_spec, gate_forms) + adjoint_apply(
        up_grad_spec, up_forms
    )
    input_spec = lax.psum_scatter(
        partial_input.astype(jnp.bfloat16), "mp", scatter_dimension=1, tiled=True
    )
    grad_tokens = from_spectra(input_spec, inverse_table).astype(jnp.bfloat16)
    grad_gate = weight_grad(token_spec, gate_grad_spec)
    grad_up = weight_grad(token_spec, up_grad_spec)
    hidden_all = lax.all_gather(hidden_spec, "mp", axis=1, tiled=True)
    grad_down = weight_grad(hidden_all, cotangent_local)
    grad_gate, grad_up, grad_down = lax.psum((grad_gate, grad_up, grad_down), "dp")
    grad_scale = 1.0 / math.sqrt(total_tokens)
    return (grad_tokens, grad_gate * grad_scale, grad_up * grad_scale, grad_down * grad_scale)


def solution(mesh):
    in_specs = (
        P(("groups", "dp"), "mp"),
        P(("groups", "dp"), "mp"),
        P("mp", None, None),
        P("mp", None, None),
        P("mp", None, None),
    )
    out_specs = (
        P(("groups", "dp"), "mp"),
        P(("groups", "mp"), None, None),
        P(("groups", "mp"), None, None),
        P(("groups", "mp"), None, None),
    )
    return jax.shard_map(shards, mesh=mesh, in_specs=in_specs, out_specs=out_specs, check_vma=False)
```

profile of v0, /device:TPU:0, one launch (start us, length us, event | category | flops | bytes accessed | tf_op | source)
XLA Modules:
  0.0 230.7 jit_solution(4201904417603381097)
XLA Ops:
  7.5 1.9 fusion.142
  9.4 2.6 %fusion.111 = (f32[512,255]{1,0:T(8,128)S(1)}, f32[255,512]{0,1:T(8,128)}) fusion(f32[512,256]{1,0:T(8,128)S(1)} %fusion.94), kind=kLoop, calls=%fused_computation.136 | loop fusion | flops 261120 | bytes 1566720 | tf_op jit(solution)/shard_map/neg | solution.py:22
  14.6 3.5 %all-to-all-start = ((bf16[4,28,512]{2,0,1:T(4,128)(2,1)}), bf16[4,28,512]{2,0,1:T(4,128)(2,1)S(1)}, u32[]{:S(2)}, u32[]{:S(2)}) async-start(bf16[4,28,512]{2,0,1:T(4,128)(2,1)} %param.9), calls=%async_computation | async-start | bytes 229376 | tf_op jit(solution)/shard_map/all_to_all | solution.py:131
  20.1 1.9 fusion.179
  22.9 1.9 fusion.91
  34.6 3.2 %add_convert_fusion.1 = bf16[256,14,128]{2,1,0:T(8,128)(2,1)S(1)} fusion(f32[256,14,128]{2,1,0:T(8,128)S(1)} %fusion.162, bf16[256,8,128]{2,0,1:T(8,128)(2,1)S(1)} %get-tuple-element.31, bf16[512,14,8]{1,2,0:T(8,128)(2,1)S(1)} %bitcast.141, bf16[256]{0:T(256)(128)(2,1)S(1)} %broadcast_subtract_fusion, bf16[256]{0:T(256)(128)(2,1)S(1)} %fusion.167), kind=kOutput, calls=%fused_computation.28 | convolution fusion | flops 8343552 | bytes 3392512 | tf_op jit(solution)/shard_map/kit,koi->kot/dot_general | solution.py:49
  37.8 3.3 %add_convert_fusion = bf16[256,14,128]{2,1,0:T(8,128)(2,1)S(1)} fusion(f32[256,14,128]{2,1,0:T(8,128)S(1)} %fusion.159, bf16[256,8,128]{2,0,1:T(8,128)(2,1)S(1)} %get-tuple-element.31, bf16[512,14,8]{1,2,0:T(8,128)(2,1)S(1)} %bitcast.132, bf16[256]{0:T(256)(128)(2,1)S(1)} %broadcast_subtract_fusion, bf16[256]{0:T(256)(128)(2,1)S(1)} %fusion.167), kind=kOutput, calls=%fused_computation.27 | convolution fusion | flops 8343552 | bytes 3392512 | tf_op jit(solution)/shard_map/kit,koi->kot/dot_general | solution.py:49
  43.6 3.0 %fusion.25 = f32[512,14,128]{2,0,1:T(8,128)} fusion(bf16[512,512,1]{0,1,2:T(8,128)(2,1)S(1)} %copy-done.8, bf16[512,14,128]{2,1,0:T(8,128)(2,1)S(1)} %pad_maximum_fusion.1), kind=kOutput, calls=%fused_computation.40 | convolution fusion | flops 939524096 | bytes 6029312 | tf_op jit(solution)/shard_map/kbt,kn->tbn/dot_general | solution.py:44
  46.5 3.0 %fusion.23 = f32[512,14,128]{2,0,1:T(8,128)} fusion(bf16[512,512,1]{0,1,2:T(8,128)(2,1)S(1)} %copy-done.8, bf16[512,14,128]{2,1,0:T(8,128)(2,1)S(1)} %pad_maximum_fusion.2), kind=kOutput, calls=%fused_computation.38 | convolution fusion | flops 939524096 | bytes 6029312 | tf_op jit(solution)/shard_map/kbt,kn->tbn/dot_general | solution.py:44
  55.3 3.1 %fusion.27 = f32[512,14,128]{2,0,1:T(8,128)} fusion(bf16[512,512,1]{0,1,2:T(8,128)(2,1)S(1)} %copy-done.8, bf16[512,14,128]{2,1,0:T(8,128)(2,1)S(1)} %pad_maximum_fusion), kind=kOutput, calls=%fused_computation.42 | convolution fusion | flops 939524096 | bytes 6029312 | tf_op jit(solution)/shard_map/kbt,kn->tbn/dot_general | solution.py:44
  59.5 2.7 %convert_bitcast_fusion = bf16[512,14,128]{2,0,1:T(8,128)(2,1)} fusion(bf16[512,512,1]{0,1,2:T(8,128)(2,1)S(1)} %copy-done.25, f32[512,14,128]{2,0,1:T(8,128)S(1)} %copy-done.13, f32[512,14,128]{2,0,1:T(8,128)S(1)} %copy-done.11), kind=kOutput, calls=%fused_computation.44 | convolution fusion | flops 945946624 | bytes 9699328 | tf_op jit(solution)/shard_map/tbn,nk->kbt/dot_general | solution.py:37
  62.2 5.8 %convert_bitcast_fusion.1 = bf16[512,14,128]{2,0,1:T(8,128)(2,1)} fusion(bf16[512,512,1]{0,1,2:T(8,128)(2,1)S(1)} %copy-done.25, f32[512,14,128]{2,0,1:T(8,128)} %fusion.23, f32[512,14,128]{2,0,1:T(8,128)} %fusion.27), kind=kOutput, calls=%fused_computation.45 | convolution fusion | flops 945946624 | bytes 9699328 | tf_op jit(solution)/shard_map/tbn,nk->kbt/dot_general | solution.py:37
  69.2 3.6 %convert_bitcast_fusion.2 = bf16[512,14,128]{2,0,1:T(8,128)(2,1)} fusion(bf16[512,512,1]{0,1,2:T(8,128)(2,1)S(1)} %copy-done.25, f32[512,14,128]{2,0,1:T(8,128)S(1)} %copy-done.14, f32[512,14,128]{2,0,1:T(8,128)S(1)} %copy-done.12, f32[512,14,128]{2,0,1:T(8,128)S(1)} %copy-done.15), kind=kOutput, calls=%fused_computation.46 | convolution fusion | flops 949616640 | bytes 13369344 | tf_op jit(solution)/shard_map/tbn,nk->kbt/dot_general | solution.py:37
  77.5 4.1 %fusion.69 = f32[256,8,128]{2,1,0:T(8,128)S(1)} fusion(bf16[256,14,128]{2,0,1:T(8,128)(2,1)S(1)} %get-tuple-element.26, bf16[512,14,8]{1,2,0:T(8,128)(2,1)S(1)} %bitcast.143, bf16[256]{0:T(256)(128)(2,1)S(1)} %broadcast_subtract_fusion, bf16[256]{0:T(256)(128)(2,1)S(1)} %fusion.167), kind=kOutput, calls=%fused_computation.84 | convolution fusion | flops 7426048 | bytes 2081792 | tf_op jit(solution)/shard_map/kot,koi->kit/dot_general | solution.py:49
  81.6 4.1 %fusion.80 = f32[256,8,128]{2,1,0:T(8,128)S(1)} fusion(bf16[256,14,128]{2,0,1:T(8,128)(2,1)S(1)} %get-tuple-element.28, bf16[512,14,8]{1,2,0:T(8,128)(2,1)S(1)} %bitcast.134, bf16[256]{0:T(256)(128)(2,1)S(1)} %broadcast_subtract_fusion, bf16[256]{0:T(256)(128)(2,1)S(1)} %fusion.167), kind=kOutput, calls=%fused_computation.95 | convolution fusion | flops 7426048 | bytes 2081792 | tf_op jit(solution)/shard_map/kot,koi->kit/dot_general | solution.py:49
  90.7 2.2 fusion.67
  95.6 5.0 %fusion.43 = f32[256,14,8]{1,2,0:T(8,128)} fusion(f32[256,14,8]{1,2,0:T(8,128)S(1)} %fusion.67, bf16[256,14,128]{2,0,1:T(8,128)(2,1)S(1)} %get-tuple-element.25, f32[256]{0:T(256)S(1)} %fusion.166, f32[256]{0:T(256)S(1)} %fusion.170, bf16[256,8,128]{2,0,1:T(8,128)(2,1)S(1)} %get-tuple-element.32), kind=kOutput, calls=%fused_computation.54 | convolution fusion | flops 7426048 | bytes 1673216 | tf_op jit(solution)/shard_map/kit,kot->koi/dot_general | solution.py:49
  100.7 5.1 %fusion.42 = f32[256,14,8]{1,2,0:T(8,128)} fusion(f32[256,14,8]{1,2,0:T(8,128)S(1)} %fusion.65, f32[256,14,8]{1,2,0:T(8,128)S(1)} %fusion.67, bf16[256,14,128]{2,0,1:T(8,128)(2,1)S(1)} %get-tuple-element.25, f32[256]{0:T(256)S(1)} %get-tuple-element.38, f32[256]{0:T(256)S(1)} %get-tuple-element.37, bf16[256,8,128]{2,0,1:T(8,128)(2,1)S(1)} %get-tuple-element.31), kind=kOutput, calls=%fused_computation.52 | convolution fusion | flops 7454720 | bytes 1787904 | tf_op jit(solution)/shard_map/kit,kot->koi/dot_general | solution.py:49
  105.8 4.9 %fusion.45 = f32[256,14,8]{1,2,0:T(8,128)} fusion(f32[256,14,8]{1,2,0:T(8,128)S(1)} %fusion.76, f32[256,14,8]{1,2,0:T(8,128)S(1)} %fusion.78, bf16[256,14,128]{2,0,1:T(8,128)(2,1)S(1)} %get-tuple-element.27, f32[256]{0:T(256)S(1)} %get-tuple-element.38, f32[256]{0:T(256)S(1)} %get-tuple-element.37, bf16[256,8,128]{2,0,1:T(8,128)(2,1)S(1)} %get-tuple-element.31), kind=kOutput, calls=%fused_computation.57 | convolution fusion | flops 7454720 | bytes 1787904 | tf_op jit(solution)/shard_map/kit,kot->koi/dot_general | solution.py:49
  110.8 6.0 %fusion.46 = f32[256,14,8]{1,2,0:T(8,128)} fusion(f32[256,14,8]{1,2,0:T(8,128)} %copy-done.9, bf16[256,14,128]{2,0,1:T(8,128)(2,1)S(1)} %get-tuple-element.27, f32[256]{0:T(256)S(1)} %fusion.166, f32[256]{0:T(256)S(1)} %fusion.170, bf16[256,8,128]{2,0,1:T(8,128)(2,1)S(1)} %get-tuple-element.32), kind=kOutput, calls=%fused_computation.59 | convolution fusion | flops 7426048 | bytes 1673216 | tf_op jit(solution)/shard_map/kit,kot->koi/dot_general | solution.py:49
  122.6 2.4 %fusion.174 = (bf16[256,28,128]{2,0,1:T(8,128)(2,1)S(1)}, bf16[256,28,128]{2,0,1:T(8,128)(2,1)S(1)}) fusion(bf16[512,28,128]{2,0,1:T(8,128)(2,1)} %all-gather.8.cloned.1.call-done), kind=kLoop, calls=%fused_computation.214 | loop fusion | bytes 7340032 | tf_op jit(solution)/shard_map/slice | solution.py:94
  127.1 5.5 %fusion.52 = f32[256,4,28]{2,1,0:T(4,128)S(1)} fusion(bf16[256,28,128]{2,0,1:T(8,128)(2,1)S(1)} %get-tuple-element.23, f32[256,4,28]{2,1,0:T(4,128)S(1)} %fusion.17, f32[256]{0:T(256)S(1)} %fusion.166, f32[256]{0:T(256)S(1)} %fusion.170, bf16[256,4,128]{2,0,1:T(8,128)(2,1)S(1)} %copy-done.23), kind=kOutput, calls=%fused_computation.72 | convolution fusion | flops 7426048 | bytes 2328576 | tf_op jit(solution)/shard_map/kit,kot->koi/dot_general | solution.py:49
  134.4 5.7 %fusion.61 = f32[256,4,28]{2,1,0:T(4,128)S(1)} fusion(f32[256,4,28]{2,1,0:T(4,128)S(1)} %fusion.15, bf16[256,28,128]{2,0,1:T(8,128)(2,1)S(1)} %copy-done.20, f32[256,4,28]{2,1,0:T(4,128)S(1)} %copy-done.27, f32[256]{0:T(256)S(1)} %get-tuple-element.38, f32[256]{0:T(256)S(1)} %get-tuple-element.37, bf16[256,4,128]{2,0,1:T(8,128)(2,1)S(1)} %copy-done.22), kind=kOutput, calls=%fused_computation.75 | convolution fusion | flops 7454720 | bytes 2443264 | tf_op jit(solution)/shard_map/kit,kot->koi/dot_general | solution.py:49
  143.6 75.3 %all-reduce.3.cloned.1.call-done = (f32[14,8,512]{2,1,0:T(8,128)}, f32[14,8,512]{2,1,0:T(8,128)}, f32[4,28,512]{2,0,1:T(4,128)}) async-done(((f32[14,8,512]{2,1,0:T(8,128)}, f32[14,8,512]{2,1,0:T(8,128)}, f32[4,28,512]{2,0,1:T(4,128)}), (f32[14,8,512]{2,1,0:T(8,128)}, f32[14,8,512]{2,1,0:T(8,128)}, f32[4,28,512]{2,0,1:T(4,128)})) %all-reduce.3.cloned.1.call-update) | async-done | bytes 688144 | tf_op jit(solution)/shard_map/psum | solution.py:149
  (139 shorter events, 56.4 us)
Async XLA Ops:
  7.2 22.0 %all-gather.6.cloned.1.call-start = ((), (), s32[]{:S(2)}) async-start(), calls=%async_computation.3 | async-start | bytes 1572864 | tf_op jit(solution)/shard_map/all_gather | solution.py:120
  12.6 5.6 %copy-start.30 = (bf16[128,2048]{1,0:T(8,128)(2,1)S(1)}, bf16[128,2048]{1,0:T(8,128)(2,1)}, u32[]{:S(2)}) copy-start(bf16[128,2048]{1,0:T(8,128)(2,1)} %param.6) | copy-start | bytes 1572868
  12.8 6.7 %copy-start.24 = (bf16[512,512,1]{0,1,2:T(8,128)(2,1)}, bf16[512,512,1]{0,1,2:T(8,128)(2,1)S(1)}, u32[]{:S(2)}) copy-start(bf16[512,512,1]{0,1,2:T(8,128)(2,1)S(1)} %fusion.95) | copy-start | bytes 1572868
  14.6 7.4 %copy-start.28 = (bf16[14,8,512]{2,1,0:T(8,128)(2,1)S(1)}, bf16[14,8,512]{2,1,0:T(8,128)(2,1)}, u32[]{:S(2)}) copy-start(bf16[14,8,512]{2,1,0:T(8,128)(2,1)} %param.8) | copy-start | bytes 344068
  14.6 12.0 %all-to-all-start = ((bf16[4,28,512]{2,0,1:T(4,128)(2,1)}), bf16[4,28,512]{2,0,1:T(4,128)(2,1)S(1)}, u32[]{:S(2)}, u32[]{:S(2)}) async-start(bf16[4,28,512]{2,0,1:T(4,128)(2,1)} %param.9), calls=%async_computation | async-start | bytes 229376 | tf_op jit(solution)/shard_map/all_to_all | solution.py:131
  18.1 31.3 %all-gather.4.cloned.1.call-start = ((), (), s32[]{:S(2)}) async-start(), calls=%async_computation.2 | async-start | bytes 1572864 | tf_op jit(solution)/shard_map/all_gather | solution.py:130
  19.5 103.1 %all-gather.8.cloned.1.call-start = ((), (), s32[]{:S(2)}) async-start(), calls=%async_computation.5 | async-start | bytes 5505024 | tf_op jit(solution)/shard_map/all_gather | solution.py:147
  22.0 6.2 %copy-start.18 = (f32[255,512]{0,1:T(8,128)S(1)}, f32[255,512]{0,1:T(8,128)}, u32[]{:S(2)}) copy-start(f32[255,512]{0,1:T(8,128)} %get-tuple-element.36) | copy-start | bytes 1566724
  22.9 11.7 %copy-start.6 = (bf16[14,8,512]{0,1,2:T(8,128)(2,1)}, bf16[14,8,512]{0,1,2:T(8,128)(2,1)S(1)}, u32[]{:S(2)}) copy-start(bf16[14,8,512]{0,1,2:T(8,128)(2,1)S(1)} %copy.134) | copy-start | bytes 344068
  26.6 14.5 %copy-start.4 = (bf16[14,8,512]{0,1,2:T(8,128)(2,1)}, bf16[14,8,512]{0,1,2:T(8,128)(2,1)S(1)}, u32[]{:S(2)}) copy-start(bf16[14,8,512]{0,1,2:T(8,128)(2,1)S(1)} %copy.137) | copy-start | bytes 344068
  54.9 3.5 %copy-start.13 = (f32[512,14,128]{2,0,1:T(8,128)S(1)}, f32[512,14,128]{2,0,1:T(8,128)}, u32[]{:S(2)}) copy-start(f32[512,14,128]{2,0,1:T(8,128)} %fusion.23) | copy-start | bytes 11010052
  55.3 4.2 %copy-start.11 = (f32[512,14,128]{2,0,1:T(8,128)S(1)}, f32[512,14,128]{2,0,1:T(8,128)}, u32[]{:S(2)}) copy-start(f32[512,14,128]{2,0,1:T(8,128)} %fusion.25) | copy-start | bytes 11010052
  55.3 4.2 %copy-start.25 = (bf16[512,512,1]{0,1,2:T(8,128)(2,1)S(1)}, bf16[512,512,1]{0,1,2:T(8,128)(2,1)}, u32[]{:S(2)}) copy-start(bf16[512,512,1]{0,1,2:T(8,128)(2,1)} %copy-done.24) | copy-start | bytes 1572868
  62.2 5.8 %copy-start.12 = (f32[512,14,128]{2,0,1:T(8,128)S(1)}, f32[512,14,128]{2,0,1:T(8,128)}, u32[]{:S(2)}) copy-start(f32[512,14,128]{2,0,1:T(8,128)} %fusion.25) | copy-start | bytes 11010052
  62.2 5.8 %copy-start.14 = (f32[512,14,128]{2,0,1:T(8,128)S(1)}, f32[512,14,128]{2,0,1:T(8,128)}, u32[]{:S(2)}) copy-start(f32[512,14,128]{2,0,1:T(8,128)} %fusion.23) | copy-start | bytes 11010052
  62.2 7.0 %copy-start.15 = (f32[512,14,128]{2,0,1:T(8,128)S(1)}, f32[512,14,128]{2,0,1:T(8,128)}, u32[]{:S(2)}) copy-start(f32[512,14,128]{2,0,1:T(8,128)} %fusion.27) | copy-start | bytes 11010052
  72.8 68.3 %reduce-scatter.2.cloned.1.call-start = ((), (), s32[]{:S(2)}) async-start(), calls=%async_computation.4 | async-start | bytes 1572864 | tf_op jit(solution)/shard_map/reduce_scatter | solution.py:141
  74.9 11.4 %copy-start = (bf16[256,14,128]{2,0,1:T(8,128)(2,1)}, bf16[256,14,128]{2,0,1:T(8,128)(2,1)S(1)}, u32[]{:S(2)}) copy-start(bf16[256,14,128]{2,0,1:T(8,128)(2,1)S(1)} %get-tuple-element.26) | copy-start | bytes 2752516
  75.1 12.7 %copy-start.2 = (bf16[256,14,128]{2,0,1:T(8,128)(2,1)}, bf16[256,14,128]{2,0,1:T(8,128)(2,1)S(1)}, u32[]{:S(2)}) copy-start(bf16[256,14,128]{2,0,1:T(8,128)(2,1)S(1)} %get-tuple-element.28) | copy-start | bytes 2752516
  77.5 4.1 %copy-start.5 = (bf16[14,8,512]{0,1,2:T(8,128)(2,1)S(1)}, bf16[14,8,512]{0,1,2:T(8,128)(2,1)}, u32[]{:S(2)}) copy-start(bf16[14,8,512]{0,1,2:T(8,128)(2,1)} %copy-done.4) | copy-start | bytes 344068
  94.7 11.1 %copy-start.9 = (f32[256,14,8]{1,2,0:T(8,128)}, f32[256,14,8]{1,2,0:T(8,128)S(1)}, u32[]{:S(2)}) copy-start(f32[256,14,8]{1,2,0:T(8,128)S(1)} %fusion.78) | copy-start | bytes 344068
  110.7 108.2 %all-reduce.3.cloned.1.call-start = ((), (), s32[]{:S(2)}) async-start(), calls=%async_computation.6 | async-start | bytes 1376256 | tf_op jit(solution)/shard_map/psum | solution.py:149
  116.8 3.5 %copy-start.16 = (f32[256,14,8]{1,2,0:T(8,128)S(1)}, f32[256,14,8]{1,2,0:T(8,128)}, u32[]{:S(2)}) copy-start(f32[256,14,8]{1,2,0:T(8,128)} %fusion.46) | copy-start | bytes 344068
  116.8 3.9 %copy-start.17 = (f32[256,14,8]{1,2,0:T(8,128)S(1)}, f32[256,14,8]{1,2,0:T(8,128)}, u32[]{:S(2)}) copy-start(f32[256,14,8]{1,2,0:T(8,128)} %fusion.45) | copy-start | bytes 344068
  (13 other events, 22.7 us)
Sparse Core Ops, SparseCore 0:
  14.7 11.7 all-gather.5
  28.1 10.1 all-gather.3
  72.9 15.6 all-gather.7
  110.9 11.1 reduce-scatter.1
  141.2 77.6 all-reduce.2
where the time goes:
time: 235 us; the launch traced here: 231 us
  matrix products  92.9 us (40%)
  waiting for transfers between devices  75.4 us (32%)
  local copies, waits for them, and re-layouts  27.1 us (12%)
  other arithmetic  16.5 us (7%)
  between operations  14.5 us (6%)
  starting transfers between devices  4.23 us (2%)
    psum x1, waiting for transfers between devices, shards(): lax.psum((grad_gate, grad_up, grad_down), 'dp')  75.3 us
    dot_general x32, matrix products, product(): jnp.einsum(pattern, left_operand, right_operand, preferred_element_type=j...  67.8 us
    dot_general x5, matrix products, to_spectra(): jnp.einsum('tbn,nk->kbt', blocks, table, preferred_element_type=jnp.float32)  14.7 us
    unnamed x65, local copies, waits for them, and re-layouts  10.6 us
    dot_general x4, matrix products, from_spectra(): jnp.einsum('kbt,kn->tbn', spectra, table, preferred_element_type=jnp.floa...  10.5 us
  transfers between devices with their start and end apart: 6, of which 1 were waited for; matrix products, arithmetic and copies ran while one was open for 42% of the time, Pallas kernels for 0%

commit v1 on v0

v1 whole, which is shorter than its diff:
```python
import functools
import math

import jax
import jax.numpy as jnp
import numpy as np
from jax import lax
from jax.experimental import pallas as pl
from jax.experimental.pallas import tpu as pltpu
from jax.sharding import PartitionSpec as P

F = 16
LANES = 128
ROWS = 16


def transform_tables(block):
    half = block // 2
    n = np.arange(block)
    k = np.arange(half)
    angles = ((n[:, None] * k[None, :]) % block).astype(np.float32) * np.float32(2.0 * math.pi / block)
    cosine = np.cos(angles.astype(np.float64)).astype(np.float32)
    sine = np.sin(angles.astype(np.float64)).astype(np.float32)
    parity = (1 - 2 * (n % 2)).astype(np.float32)
    norm = np.float32(1.0 / math.sqrt(block))
    forward = np.concatenate([cosine, parity[:, None], -sine[:, 1:]], axis=1) * norm
    doubling = np.where(k >= 1, 2.0, 1.0).astype(np.float32)
    inverse = np.concatenate([(cosine * doubling).T, parity[None, :], -2.0 * sine[:, 1:].T], axis=0) * norm
    order = np.arange(block).reshape(2, half // F, F).transpose(1, 0, 2).reshape(-1)
    return (
        jnp.asarray(forward.T[order], jnp.bfloat16),
        jnp.asarray(inverse.T[:, order], jnp.bfloat16),
    )


def nt_dot(a, b):
    return lax.dot_general(a, b, (((1,), (1,)), ((), ())), preferred_element_type=jnp.float32)


def swap_blocks(tiles):
    tiles = list(tiles)
    lane_block = lax.broadcasted_iota(jnp.int32, tiles[0].shape, 1) // F
    step = len(tiles) // 2
    while step:
        high = (lane_block & step) != 0
        for i in range(len(tiles)):
            if i & step:
                continue
            low_tile, high_tile = tiles[i], tiles[i + step]
            tiles[i] = jnp.where(high, pltpu.roll(high_tile, F * step, 1), low_tile)
            tiles[i + step] = jnp.where(high, high_tile, pltpu.roll(low_tile, LANES - F * step, 1))
        step //= 2
    return tiles


def weight_rows(read, write, conj, groups):
    half = groups * F
    for part in range(half // LANES):
        at = part * LANES
        re = swap_blocks([read(i, at) for i in range(8)])
        im = swap_blocks([read(i, half + at) for i in range(8)])
        for i in range(8):
            g = part * 8 + i
            cross, wim = re[i], im[i]
            if g == 0:
                first = lax.broadcasted_iota(jnp.int32, wim.shape, 1) % F == 0
                cross = jnp.where(first, wim, cross)
                wim = jnp.where(first, 0.0, wim)
            sign = 1.0 if conj else -1.0
            write(g, 0, 0, re[i])
            write(g, 0, 1, sign * wim)
            write(g, 1, 0, -sign * wim)
            write(g, 1, 1, cross)


def diagonal(width):
    row = lax.broadcasted_iota(jnp.int32, (F, width), 0)
    lane = lax.broadcasted_iota(jnp.int32, (F, width), 1)
    return lane % F == row


def main_kernel(groups, fb, x_own, x_other, c_own, c_other, pt_ref, qt_ref, wg_ref, wu_ref, wd_ref,
                d_ref, gg_ref, ug_ref, sx, sc, gs, us, hs, hid, rg, ru, rd, wexp, flat):
    core = lax.axis_index("mp")
    db = 8
    per = db // 2
    block = pt_ref.shape[0]

    for source, target in ((wg_ref, rg), (wu_ref, ru)):
        for tile in range(block // LANES):
            flat[tile] = source[:, tile * LANES : (tile + 1) * LANES].astype(jnp.float32)

        def read(i, at):
            return flat[at // LANES, pl.ds(i, fb, stride=db), :]

        def write(g, ri, tile, rows, target=target):
            target[tile, g * 2 * ROWS + ri * ROWS : g * 2 * ROWS + ri * ROWS + fb, :] = rows

        weight_rows(read, write, False, groups)

    def read_down(o, at):
        return wd_ref[o, :, at : at + LANES].astype(jnp.float32)

    def write_down(g, ri, tile, rows):
        rd[tile, g * 2 * ROWS + ri * ROWS : g * 2 * ROWS + ri * ROWS + fb, :] = rows

    weight_rows(read_down, write_down, True, groups)

    for own, other, target in ((x_own, x_other, sx), (c_own, c_other, sc)):
        for source, first in ((own, core * per), (other, (1 - core) * per)):
            for j in range(0, per, 2):
                pair = jnp.concatenate(
                    [source[:, j * block : (j + 1) * block], source[:, (j + 1) * block : (j + 2) * block]], axis=0
                )
                result = nt_dot(pt_ref[...], pair).astype(jnp.bfloat16)
                for u in range(2):
                    target[:, :, first + j + u] = result[:, u * LANES : (u + 1) * LANES].reshape(groups, 2, F, LANES)

    mask = diagonal(LANES)

    @pl.loop(0, groups)
    def _(g):
        for w, rows in enumerate((rg, ru, rd)):
            for ri in range(2):
                for o in range(fb):
                    at = ((w * 2 + ri) * fb + o) * F
                    for tile in range(2):
                        row = rows[tile, pl.ds(g * 2 * ROWS + ri * ROWS + o, F, stride=0), :]
                        wexp[at : at + F, tile * LANES : (tile + 1) * LANES] = jnp.where(mask, row, 0.0).astype(
                            jnp.bfloat16
                        )
        span = 2 * fb * F
        forward = jnp.dot(
            wexp[0 : 2 * span, :], sx[g].reshape(2 * LANES, LANES), preferred_element_type=jnp.float32
        ).astype(jnp.bfloat16)
        forward = forward.reshape(2, 2, fb, F, LANES)
        back = jnp.dot(
            wexp[2 * span : 3 * span, :], sc[g].reshape(2 * LANES, LANES), preferred_element_type=jnp.float32
        ).astype(jnp.bfloat16)
        back = back.reshape(2, fb, F, LANES)
        for ri in range(2):
            gs[:, g, ri] = forward[0, ri]
            us[:, g, ri] = forward[1, ri]
            hs[:, g, ri] = back[ri]

    for target in (gg_ref, ug_ref, hid):
        target[:, :, fb:] = jnp.zeros((groups, 2, ROWS - fb, F, LANES), jnp.bfloat16)

    @pl.loop(0, fb)
    def _(o):
        spectra = jnp.concatenate([ref[o].reshape(block, LANES) for ref in (gs, us, hs)], axis=1)
        values = jnp.dot(qt_ref[...], spectra, preferred_element_type=jnp.float32)
        gate, up, grad = (values[:, u * LANES : (u + 1) * LANES] for u in range(3))
        sig = 1.0 / (1.0 + jnp.exp(-gate))
        gated = gate * sig
        hidden = (gated * up).astype(jnp.bfloat16)
        gate_grad = (grad * up * sig * (1.0 + gate * (1.0 - sig))).astype(jnp.bfloat16)
        up_grad = (grad * gated).astype(jnp.bfloat16)
        result = jnp.dot(
            pt_ref[...], jnp.concatenate([hidden, gate_grad, up_grad], axis=1), preferred_element_type=jnp.float32
        ).astype(jnp.bfloat16)
        for u, target in enumerate((hid, gg_ref, ug_ref)):
            target[:, :, o] = result[:, u * LANES : (u + 1) * LANES].reshape(groups, 2, F, LANES)

    keep = diagonal(LANES)
    lane = lax.broadcasted_iota(jnp.int32, (F, LANES), 1)
    row = lax.broadcasted_iota(jnp.int32, (F, LANES), 0)

    @pl.loop(0, groups)
    def _(g):
        first = (lane % F == 0) & (row == 0) & (g == 0)
        weight = jnp.where(keep, jnp.where(first, 1.0, 2.0), 0.0)
        weight_pair = jnp.where(first, 0.0, weight)
        weight_first = jnp.where(first, 1.0, 0.0)
        span = 2 * ROWS * F
        for w, (rows, cols, sign) in enumerate(((gg_ref, sx, 1.0), (ug_ref, sx, 1.0), (hid, sc, -1.0))):
            m = nt_dot(rows[g].reshape(span, LANES), cols[g].reshape(2 * LANES, LANES)).reshape(2, ROWS, F, 2 * LANES)
            rr, ri = m[0, :, :, :LANES], m[0, :, :, LANES:]
            ir, ii = m[1, :, :, :LANES], m[1, :, :, LANES:]
            re = jnp.sum(rr * weight + ii * weight_pair, axis=1)
            im = jnp.sum((ir - ri) * (sign * weight_pair) + ii * weight_first, axis=1)
            d_ref[g, w * ROWS : (w + 1) * ROWS, :LANES] = re.astype(jnp.bfloat16)
            d_ref[g, w * ROWS : (w + 1) * ROWS, LANES:] = im.astype(jnp.bfloat16)


def adjoint_kernel(groups, fb, gg_ref, ug_ref, wg_ref, wu_ref, own_ref, other_ref, ra, rb, wexp, part):
    core = lax.axis_index("mp")
    db = 8
    per = db // 2
    for source, target in ((wg_ref, ra), (wu_ref, rb)):
        for upper in range(2):
            def read(o, at, source=source, upper=upper):
                o = upper * 8 + o
                if o >= fb:
                    return jnp.zeros((db, LANES), jnp.float32)
                return source[o, :, at : at + LANES].astype(jnp.float32)

            def write(g, ri, tile, rows, target=target, upper=upper):
                target[tile * 2 + upper, g * 2 * db + ri * db : g * 2 * db + (ri + 1) * db, :] = rows

            weight_rows(read, write, True, groups)
    mask = diagonal(LANES)
    span = 4 * LANES

    @pl.loop(0, groups)
    def _(g):
        for w, rows in enumerate((ra, rb)):
            for r in range(2 * db):
                for tile in range(4):
                    row = rows[tile, pl.ds(g * 2 * db + r, F, stride=0), :]
                    at = w * span + tile * LANES
                    wexp[r * F : (r + 1) * F, at : at + LANES] = jnp.where(mask, row, 0.0).astype(jnp.bfloat16)
        grads = jnp.concatenate([gg_ref[g].reshape(span, LANES), ug_ref[g].reshape(span, LANES)], axis=0)
        part[...] = jnp.dot(wexp[...], grads, preferred_element_type=jnp.float32).reshape(2, db, F, LANES)
        for ri in range(2):
            own_ref[g, ri] = part[ri, pl.ds(core * per, per)]
            other_ref[g, ri] = part[ri, pl.ds((1 - core) * per, per)].astype(jnp.bfloat16)


def input_kernel(own_ref, got_ref, qt_ref, out_ref):
    block = qt_ref.shape[0]
    for j in range(own_ref.shape[2]):
        spectrum = (own_ref[:, :, j] + got_ref[:, :, j].astype(jnp.float32)).astype(jnp.bfloat16)
        values = jnp.dot(qt_ref[...], spectrum.reshape(block, LANES), preferred_element_type=jnp.float32)
        out_ref[:, j * block : (j + 1) * block] = values.T.astype(jnp.bfloat16)


def reduce_kernel(r_ref, sum_ref, keep_ref, send_ref):
    core = lax.axis_index("mp")
    total = r_ref[0].astype(jnp.float32)
    for d in range(1, r_ref.shape[0]):
        total = total + r_ref[d].astype(jnp.float32)
    sum_ref[...] = total[:, : 2 * ROWS].astype(jnp.bfloat16)
    low = lax.broadcasted_iota(jnp.int32, (ROWS, LANES), 1) < LANES // 2
    for g in range(total.shape[0]):
        re, im = total[g, 2 * ROWS :, :LANES], total[g, 2 * ROWS :, LANES:]
        lower = jnp.where(low, re, pltpu.roll(im, LANES // 2, 1))
        upper = jnp.where(low, pltpu.roll(re, LANES // 2, 1), im)
        keep_ref[g] = jnp.where(core == 0, lower, upper).astype(jnp.bfloat16)
        send_ref[g] = jnp.where(core == 0, upper, lower).astype(jnp.bfloat16)


def layout_kernel(scale, fb, s_ref, a_ref, b_ref, gate_ref, up_ref, down_ref, flat):
    groups = s_ref.shape[0]
    half = groups * F
    for w, target in enumerate((gate_ref, up_ref)):
        for ri in range(2):
            for part in range(half // LANES):
                tiles = swap_blocks(
                    [
                        s_ref[part * 8 + i, w * ROWS : (w + 1) * ROWS, ri * LANES : (ri + 1) * LANES].astype(jnp.float32)
                        for i in range(8)
                    ]
                )
                at = ri * half + part * LANES
                for i in range(8):
                    flat[pl.ds(i, fb, stride=8), :] = tiles[i][:fb] * scale
                target[:, at : at + LANES] = flat[...]
    outputs = down_ref.shape[0]
    for h, source in enumerate((a_ref, b_ref)):
        for part in range(half // LANES):
            tiles = swap_blocks([source[part * 8 + i].astype(jnp.float32) for i in range(8)])
            for ri in range(2):
                at = ri * half + part * LANES
                for o in range(outputs):
                    down_ref[o, h * fb : (h + 1) * fb, at : at + LANES] = tiles[ri * outputs + o][:fb] * scale


def params(mib):
    return pltpu.CompilerParams(vmem_limit_bytes=mib << 20)


VMEM = pl.BlockSpec(memory_space=pltpu.VMEM)


def call(kernel, out_shape, args, scratch=(), mib=16, flops=0, moved=0):
    return pl.pallas_call(
        kernel,
        out_shape=out_shape,
        in_specs=[VMEM] * len(args),
        out_specs=jax.tree.map(lambda _: VMEM, out_shape),
        scratch_shapes=list(scratch),
        compiler_params=params(mib),
        cost_estimate=pl.CostEstimate(flops=flops, bytes_accessed=moved, transcendentals=0),
    )(*args)


def shards(tokens, cotangent, gate_spectra, up_spectra, down_spectra):
    n_dp = lax.axis_size("dp")
    core = lax.axis_index("mp")
    swap = [(0, 1), (1, 0)]
    fb, db, block = gate_spectra.shape
    assert db == 8 and fb <= ROWS and tokens.shape[0] == LANES and lax.axis_size("mp") == 2
    groups = block // 2 // F
    per = db // 2
    bf16, f32 = jnp.bfloat16, jnp.float32
    shape = jax.ShapeDtypeStruct
    pt, qt = transform_tables(block)

    tokens_other = lax.ppermute(tokens, "mp", swap)
    cotangent_other = lax.ppermute(cotangent, "mp", swap)
    down = down_spectra.reshape(per, 2, fb, block)
    down_own = jnp.where(core == 0, down[:, 0], down[:, 1])
    down_got = lax.ppermute(jnp.where(core == 0, down[:, 1], down[:, 0]), "mp", swap)
    down_all = jnp.where(
        core == 0, jnp.concatenate([down_own, down_got], 0), jnp.concatenate([down_got, down_own], 0)
    )
    wg = gate_spectra.reshape(fb * db, block)
    wu = up_spectra.reshape(fb * db, block)

    spec = shape((groups, 2, ROWS, F, LANES), bf16)
    d_all, gg, ug = call(
        functools.partial(main_kernel, groups, fb),
        (shape((groups, 3 * ROWS, 2 * LANES), bf16), spec, spec),
        (tokens, tokens_other, cotangent, cotangent_other, pt, qt, wg, wu, down_all),
        [pltpu.VMEM((groups, 2, db, F, LANES), bf16)] * 2
        + [pltpu.VMEM((fb, groups, 2, F, LANES), bf16)] * 3
        + [pltpu.VMEM(spec.shape, bf16)]
        + [pltpu.VMEM((2, groups * 2 * ROWS, LANES), f32)] * 3
        + [pltpu.VMEM((3 * 2 * fb * F, 2 * LANES), bf16), pltpu.VMEM((block // LANES, fb * db, LANES), f32)],
        mib=40,
        flops=10**10,
        moved=10**7,
    )

    if groups % n_dp == 0:
        share = groups // n_dp
        got = lax.all_to_all(d_all.reshape(n_dp, share, 3 * ROWS, 2 * LANES), "dp", 0, 0, tiled=True)
    else:
        share = groups
        got = lax.psum(d_all.astype(f32), "dp")[None]

    own, other = call(
        functools.partial(adjoint_kernel, groups, fb),
        (shape((groups, 2, per, F, LANES), f32), shape((groups, 2, per, F, LANES), bf16)),
        (gg, ug, gate_spectra, up_spectra),
        [pltpu.VMEM((4, groups * 2 * db, LANES), f32)] * 2
        + [pltpu.VMEM((2 * LANES, 8 * LANES), bf16), pltpu.VMEM((2, db, F, LANES), f32)],
        flops=2 * 10**9,
        moved=10**7,
    )
    partner = lax.ppermute(other, "mp", swap)
    grad_tokens = call(
        input_kernel, shape(tokens.shape, bf16), (own, partner, qt), flops=5 * 10**8, moved=4 * 10**6
    )

    total, keep, send = call(
        reduce_kernel,
        (
            shape((share, 2 * ROWS, 2 * LANES), bf16),
            shape((share, ROWS, LANES), bf16),
            shape((share, ROWS, LANES), bf16),
        ),
        (got,),
        moved=10**6,
    )
    partner_rows = lax.ppermute(send, "mp", swap)
    lower = jnp.where(core == 0, keep, partner_rows)
    upper = jnp.where(core == 0, partner_rows, keep)
    if groups % n_dp == 0:
        packed = jnp.concatenate([total, jnp.concatenate([lower, upper], axis=-1)], axis=1)
        every = jnp.broadcast_to(packed[None], (n_dp,) + packed.shape)
        packed = lax.all_to_all(every, "dp", 0, 0, tiled=True).reshape(groups, 3 * ROWS, 2 * LANES)
    else:
        packed = jnp.concatenate([total, jnp.concatenate([lower, upper], axis=-1)], axis=1)
    scale = 1.0 / math.sqrt(tokens.shape[0] * n_dp)
    gate_grad, up_grad, down_grad = call(
        functools.partial(layout_kernel, scale, fb),
        (shape((fb * db, block), f32), shape((fb * db, block), f32), shape((per, 2 * fb, block), f32)),
        (packed[:, : 2 * ROWS], packed[:, 2 * ROWS :, :LANES], packed[:, 2 * ROWS :, LANES:]),
        [pltpu.VMEM((fb * db, LANES), f32)],
        moved=10**6,
    )
    return (grad_tokens, gate_grad.reshape(fb, db, block), up_grad.reshape(fb, db, block), down_grad)


def solution(mesh):
    in_specs = (
        P(("groups", "dp"), "mp"),
        P(("groups", "dp"), "mp"),
        P("mp", None, None),
        P("mp", None, None),
        P("mp", None, None),
    )
    out_specs = (
        P(("groups", "dp"), "mp"),
        P(("groups", "mp"), None, None),
        P(("groups", "mp"), None, None),
        P(("groups", "mp"), None, None),
    )
    return jax.shard_map(shards, mesh=mesh, in_specs=in_specs, out_specs=out_specs, check_vma=False)
```

time: 235 us -> 77.7 us (0.33); the launches traced: 231 us -> 77.1 us
  matrix products: 92.9 us -> 0 us
  waiting for transfers between devices: 75.4 us -> 5.1 us
  Pallas kernels: 0 us -> 35.4 us
  blocking collectives: 0 us -> 19.4 us
  other arithmetic: 16.5 us -> 0.07 us
  local copies, waits for them, and re-layouts: 27.1 us -> 11.4 us
  between operations: 14.5 us -> 0.75 us
    dot_general x41 -> x0, matrix products: 92.9 us -> none  [the longest x32 67.8 us: product(): jnp.einsum(pattern, left_operand, right_operand, preferred_element_type=j...]
    psum x1 -> x0, waiting for transfers between devices: 75.3 us -> none  [shards(): lax.psum((grad_gate, grad_up, grad_down), 'dp')]
    pallas_call x0 -> x5, Pallas kernels: none -> 35.4 us  [call(): pl.pallas_call(kernel, out_shape=out_shape, in_specs=[VMEM] * len(args),...]
    all_to_all x0 -> x1, blocking collectives: none -> 19.4 us  [shards(): lax.all_to_all(d_all.reshape(n_dp, share, 3 * ROWS, 2 * LANES), 'dp', 0,...]
    slice x6 -> x3, local copies, waits for them, and re-layouts: 8.83 us -> 0.93 us  [the longest x1 0.89 us: shards(): down_own = jnp.where(core == 0, down[:, 0], down[:, 1])]
    mul x6 -> x0, other arithmetic: 7.14 us -> none  [the longest x1 1.92 us: transform_tables(): cosine * doubling[None, :]]
    ppermute x0 -> x5, waiting for transfers between devices: none -> 3.98 us  [the longest x1 1.73 us: shards(): partner = lax.ppermute(other, 'mp', swap)]
    neg x1 -> x0, other arithmetic: 2.6 us -> none  [transform_tables(): -sine_table[:, 1:]]
  transfers between devices with their start and end apart: 6 -> 6, of which waited for: 1 -> 4; matrix products, arithmetic and copies ran while one was open for 42% -> 1% of each run, Pallas kernels for 0% -> 10%
where the time goes in v1:
time: 77.7 us; the launch traced here: 77.1 us
  Pallas kernels  35.4 us (46%)
  blocking collectives  19.4 us (25%)
  local copies, waits for them, and re-layouts  11.4 us (15%)
  waiting for transfers between devices  5.1 us (7%)
  starting transfers between devices  4.89 us (6%)
    pallas_call x5, Pallas kernels, call(): pl.pallas_call(kernel, out_shape=out_shape, in_specs=[VMEM] * len(args),...  35.4 us
    all_to_all x1, blocking collectives, shards(): lax.all_to_all(d_all.reshape(n_dp, share, 3 * ROWS, 2 * LANES), 'dp', 0,...  19.4 us
    unnamed x23, local copies, waits for them, and re-layouts  9.72 us
    all_to_all x1, starting transfers between devices, shards(): lax.all_to_all(every, 'dp', 0, 0, tiled=True)  3.45 us
    ppermute x1, waiting for transfers between devices, shards(): partner = lax.ppermute(other, 'mp', swap)  1.73 us
  transfers between devices with their start and end apart: 6, of which 4 were waited for; matrix products, arithmetic and copies ran while one was open for 1% of the time, Pallas kernels for 10%

profile of v1, /device:TPU:0, one launch (start us, length us, event | category | flops | bytes accessed | tf_op | source)
XLA Modules:
  0.0 77.1 jit_solution(7723322807371041868)
XLA Ops:
  0.6 0.6 collective-permute-start
  1.3 0.9 %fusion.1 = (bf16[4,1,14,512]{3,0,2,1:T(4,128)(2,1)S(1)}, bf16[4,1,14,512]{3,0,2,1:T(4,128)(2,1)S(1)}) fusion(bf16[4,2,14,512]{3,0,2,1:T(4,128)(2,1)} %bitcast.16), kind=kLoop, calls=%fused_computation.7 | loop fusion | bytes 229376 | tf_op jit(solution)/shard_map/slice | solution.py:303
  2.2 0.5 collective-permute-start.2
  2.7 1.1 %collective-permute-done.2 = bf16[4,14,512]{2,1,0:T(8,128)(2,1)S(1)} collective-permute-done((bf16[4,14,512]{2,1,0:T(8,128)(2,1)S(1)}, bf16[4,14,512]{2,1,0:T(8,128)(2,1)S(1)}, u32[]{:S(2)}, u32[]{:S(2)}) %collective-permute-start.2) | collective-permute-done | bytes 57376 | tf_op jit(solution)/shard_map/ppermute | solution.py:304
  3.8 1.0 %copy-done = bf16[512,512]{1,0:T(8,128)(2,1)S(1)} copy-done((bf16[512,512]{1,0:T(8,128)(2,1)S(1)}, bf16[512,512]{1,0:T(8,128)(2,1)}, u32[]{:S(2)}) %copy-start) | copy-done | bytes 524312
  4.9 1.0 %copy-done.2 = bf16[128,2048]{1,0:T(8,128)(2,1)S(1)} copy-done((bf16[128,2048]{1,0:T(8,128)(2,1)S(1)}, bf16[128,2048]{1,0:T(8,128)(2,1)}, u32[]{:S(2)}) %copy-start.2) | copy-done | bytes 524312
  5.9 1.0 %copy-done.3 = bf16[128,2048]{1,0:T(8,128)(2,1)S(1)} copy-done((bf16[128,2048]{1,0:T(8,128)(2,1)S(1)}, bf16[128,2048]{1,0:T(8,128)(2,1)}, u32[]{:S(2)}) %copy-start.3) | copy-done | bytes 524312
  7.0 0.9 %copy-done.4 = bf16[14,8,512]{2,1,0:T(8,128)(2,1)S(1)} copy-done((bf16[14,8,512]{2,1,0:T(8,128)(2,1)S(1)}, bf16[14,8,512]{2,1,0:T(8,128)(2,1)}, u32[]{:S(2)}) %copy-start.4) | copy-done | bytes 114712
  7.9 0.9 %copy-done.6 = bf16[14,8,512]{2,1,0:T(8,128)(2,1)S(1)} copy-done((bf16[14,8,512]{2,1,0:T(8,128)(2,1)S(1)}, bf16[14,8,512]{2,1,0:T(8,128)(2,1)}, u32[]{:S(2)}) %copy-start.6) | copy-done | bytes 114712
  8.8 1.0 %copy-done.8 = bf16[512,512]{1,0:T(8,128)(2,1)S(1)} copy-done((bf16[512,512]{1,0:T(8,128)(2,1)S(1)}, bf16[512,512]{1,0:T(8,128)(2,1)}, u32[]{:S(2)}) %copy-start.8) | copy-done | bytes 524312
  9.8 26.0 %shard_map.102 = (bf16[16,48,256]{2,1,0:T(8,128)(2,1)S(1)}, bf16[16,2,16,16,128]{4,3,2,1,0:T(8,128)(2,1)S(1)}, bf16[16,2,16,16,128]{4,3,2,1,0:T(8,128)(2,1)S(1)}) custom-call(bf16[128,2048]{1,0:T(8,128)(2,1)S(1)} %copy-done.2, bf16[128,2048]{1,0:T(8,128)(2,1)S(1)} %collective-permute-done.x_other, bf16[128,2048]{1,0:T(8,128)(2,1)S(1)} %copy-done.3, ...), custom_call_target="tpu_custom_call" | custom-call | flops 10000000000 | bytes 10000000 | tf_op jit(solution)/shard_map/pallas_call | solution.py:277
  35.8 1.3 %copy-done.9 = bf16[16,2,16,16,128]{4,3,2,1,0:T(8,128)(2,1)} copy-done((bf16[16,2,16,16,128]{4,3,2,1,0:T(8,128)(2,1)}, bf16[16,2,16,16,128]{4,3,2,1,0:T(8,128)(2,1)S(1)}, u32[]{:S(2)}) %copy-start.9) | copy-done | bytes 2097176
  37.1 19.4 %all_to_all.10.r_ref = bf16[8,2,48,256]{3,2,1,0:T(8,128)(2,1)S(1)} all-to-all(bf16[8,2,48,256]{3,2,1,0:T(8,128)(2,1)S(1)} %bitcast.11), channel_id=1, replica_groups=mesh['groups'=2,'dp'=8,'mp'=2] {'dp'}, dimensions={0} | all-to-all | bytes 786432 | tf_op jit(solution)/shard_map/all_to_all | solution.py:328
  56.7 1.2 %collective-permute-done.4 = bf16[2,16,128]{2,1,0:T(8,128)(2,1)S(1)} collective-permute-done((bf16[2,16,128]{2,1,0:T(8,128)(2,1)S(1)}, bf16[2,16,128]{2,1,0:T(8,128)(2,1)S(1)}, u32[]{:S(2)}, u32[]{:S(2)}) %collective-permute-start.4) | collective-permute-done | bytes 8224 | tf_op jit(solution)/shard_map/ppermute | solution.py:357
  57.9 0.8 %broadcast_in_dim.2 = bf16[8,2,48,256]{3,2,1,0:T(8,128)(2,1)} broadcast(bf16[2,48,256]{2,1,0:T(8,128)(2,1)S(1)} %maximum_maximum_fusion), dimensions={1,2,3} | broadcast | bytes 442368 | tf_op jit(solution)/shard_map/broadcast_in_dim | solution.py:362
  58.7 3.5 %all-to-all-start.1 = ((bf16[8,2,48,256]{3,2,1,0:T(8,128)(2,1)}), bf16[8,2,48,256]{3,2,1,0:T(8,128)(2,1)S(1)}, u32[]{:S(2)}, u32[]{:S(2)}) async-start(bf16[8,2,48,256]{3,2,1,0:T(8,128)(2,1)} %broadcast_in_dim.2), calls=%async_computation.1 | async-start | bytes 786432 | tf_op jit(solution)/shard_map/all_to_all | solution.py:363
  62.2 1.6 %copy-done.10 = bf16[16,2,16,16,128]{4,3,2,1,0:T(8,128)(2,1)S(1)} copy-done((bf16[16,2,16,16,128]{4,3,2,1,0:T(8,128)(2,1)S(1)}, bf16[16,2,16,16,128]{4,3,2,1,0:T(8,128)(2,1)}, u32[]{:S(2)}) %copy-start.10) | copy-done | bytes 2097176
  63.7 5.9 %shard_map.103 = (f32[16,2,4,16,128]{4,3,2,1,0:T(8,128)S(1)}, bf16[16,2,4,16,128]{4,3,2,1,0:T(8,128)(2,1)S(1)}) custom-call(bf16[16,2,16,16,128]{4,3,2,1,0:T(8,128)(2,1)S(1)} %get-tuple-element.15.gg_ref, bf16[16,2,16,16,128]{4,3,2,1,0:T(8,128)(2,1)S(1)} %copy-done.10, bf16[14,8,512]{2,1,0:T(8,128)(2,1)S(1)} %copy-done.5, bf16[14,8,512]{2,1,0:T(8,128)(2,1)S(1)} %copy-done.7), custom_call_target="tpu_custom_call" | custom-call | flops 2000000000 | bytes 10000000 | tf_op jit(solution)/shard_map/pallas_call | solution.py:277
  69.6 0.2 collective-permute-start.3
  69.9 1.7 %collective-permute-done.3.got_ref = bf16[16,2,4,16,128]{4,3,2,1,0:T(8,128)(2,1)S(1)} collective-permute-done((bf16[16,2,4,16,128]{4,3,2,1,0:T(8,128)(2,1)S(1)}, bf16[16,2,4,16,128]{4,3,2,1,0:T(8,128)(2,1)S(1)}, u32[]{:S(2)}, u32[]{:S(2)}) %collective-permute-start.3) | collective-permute-done | bytes 524320 | tf_op jit(solution)/shard_map/ppermute | solution.py:342
  71.6 1.6 %shard_map.104 = bf16[128,2048]{1,0:T(8,128)(2,1)} custom-call(f32[16,2,4,16,128]{4,3,2,1,0:T(8,128)S(1)} %get-tuple-element.17.own_ref, bf16[16,2,4,16,128]{4,3,2,1,0:T(8,128)(2,1)S(1)} %collective-permute-done.3.got_ref, bf16[512,512]{1,0:T(8,128)(2,1)S(1)} %copy-done.1), custom_call_target="tpu_custom_call" | custom-call | flops 500000000 | bytes 4000000 | tf_op jit(solution)/shard_map/pallas_call | solution.py:277
  73.2 1.1 %all-to-all-done.1 = bf16[8,2,48,256]{3,2,1,0:T(8,128)(2,1)S(1)} async-done(((bf16[8,2,48,256]{3,2,1,0:T(8,128)(2,1)}), bf16[8,2,48,256]{3,2,1,0:T(8,128)(2,1)S(1)}, u32[]{:S(2)}, u32[]{:S(2)}) %all-to-all-start.1) | async-done | bytes 393248 | tf_op jit(solution)/shard_map/all_to_all | solution.py:363
  74.4 1.8 %shard_map.106 = (f32[112,512]{1,0:T(8,128)}, f32[112,512]{1,0:T(8,128)}, f32[4,28,512]{2,1,0:T(8,128)S(1)}) custom-call(bf16[16,32,256]{2,1,0:T(8,128)(2,1)S(1)} %slice.24.s_ref, bf16[16,16,128]{2,1,0:T(8,128)(2,1)S(1)} %get-tuple-element.35.a_ref, bf16[16,16,128]{2,1,0:T(8,128)(2,1)S(1)} %get-tuple-element.34.b_ref), custom_call_target="tpu_custom_call" | custom-call | bytes 1000000 | tf_op jit(solution)/shard_map/pallas_call | solution.py:277
  76.2 0.8 %copy.14 = f32[4,28,512]{2,0,1:T(4,128)} copy(f32[4,28,512]{2,1,0:T(8,128)S(1)} %get-tuple-element.33) | data formatting | bytes 458752
  (25 shorter events, 0.4 us)
Async XLA Ops:
  0.6 3.2 %collective-permute-start = (bf16[128,2048]{1,0:T(8,128)(2,1)}, bf16[128,2048]{1,0:T(8,128)(2,1)S(1)}, u32[]{:S(2)}, u32[]{:S(2)}) collective-permute-start(bf16[128,2048]{1,0:T(8,128)(2,1)} %x_own.1), channel_id=1, source_target_pairs={{0,1},{1,0},{2,3},{3,2},{4,5},{5,4},{6,7},{7,6},{8,9},{9,8},{10,11... | collective-permute-start | bytes 1572872 | tf_op jit(solution)/shard_map/ppermute | solution.py:300
  1.2 2.6 %collective-permute-start.1 = (bf16[128,2048]{1,0:T(8,128)(2,1)}, bf16[128,2048]{1,0:T(8,128)(2,1)S(1)}, u32[]{:S(2)}, u32[]{:S(2)}) collective-permute-start(bf16[128,2048]{1,0:T(8,128)(2,1)} %c_own.1), channel_id=1, source_target_pairs={{0,1},{1,0},{2,3},{3,2},{4,5},{5,4},{6,7},{7,6},{8,9},{9,8},{10,11... | collective-permute-start | bytes 1572872 | tf_op jit(solution)/shard_map/ppermute | solution.py:301
  2.2 1.6 %collective-permute-start.2 = (bf16[4,14,512]{2,1,0:T(8,128)(2,1)S(1)}, bf16[4,14,512]{2,1,0:T(8,128)(2,1)S(1)}, u32[]{:S(2)}, u32[]{:S(2)}) collective-permute-start(bf16[4,14,512]{2,1,0:T(8,128)(2,1)S(1)} %get-tuple-element.37), channel_id=1, source_target_pairs={{0,1},{1,0},{2,3},{3,2},{4,5},{5,4},{6,7},{7,6},{8,9},{9,8},{10,11... | collective-permute-start | bytes 172040 | tf_op jit(solution)/shard_map/ppermute | solution.py:304
  3.8 1.0 %copy-start = (bf16[512,512]{1,0:T(8,128)(2,1)S(1)}, bf16[512,512]{1,0:T(8,128)(2,1)}, u32[]{:S(2)}) copy-start(bf16[512,512]{1,0:T(8,128)(2,1)} %constant.11.clone.qt_ref) | copy-start | bytes 1572868
  4.9 1.0 %copy-start.2 = (bf16[128,2048]{1,0:T(8,128)(2,1)S(1)}, bf16[128,2048]{1,0:T(8,128)(2,1)}, u32[]{:S(2)}) copy-start(bf16[128,2048]{1,0:T(8,128)(2,1)} %x_own.1) | copy-start | bytes 1572868
  5.9 1.0 %copy-start.3 = (bf16[128,2048]{1,0:T(8,128)(2,1)S(1)}, bf16[128,2048]{1,0:T(8,128)(2,1)}, u32[]{:S(2)}) copy-start(bf16[128,2048]{1,0:T(8,128)(2,1)} %c_own.1) | copy-start | bytes 1572868
  7.0 0.9 %copy-start.4 = (bf16[14,8,512]{2,1,0:T(8,128)(2,1)S(1)}, bf16[14,8,512]{2,1,0:T(8,128)(2,1)}, u32[]{:S(2)}) copy-start(bf16[14,8,512]{2,1,0:T(8,128)(2,1)} %wg_ref.1) | copy-start | bytes 344068
  7.9 0.9 %copy-start.6 = (bf16[14,8,512]{2,1,0:T(8,128)(2,1)S(1)}, bf16[14,8,512]{2,1,0:T(8,128)(2,1)}, u32[]{:S(2)}) copy-start(bf16[14,8,512]{2,1,0:T(8,128)(2,1)} %wu_ref.1) | copy-start | bytes 344068
  8.8 1.0 %copy-start.8 = (bf16[512,512]{1,0:T(8,128)(2,1)S(1)}, bf16[512,512]{1,0:T(8,128)(2,1)}, u32[]{:S(2)}) copy-start(bf16[512,512]{1,0:T(8,128)(2,1)} %constant.10.clone.pt_ref) | copy-start | bytes 1572868
  35.8 1.3 %copy-start.9 = (bf16[16,2,16,16,128]{4,3,2,1,0:T(8,128)(2,1)}, bf16[16,2,16,16,128]{4,3,2,1,0:T(8,128)(2,1)S(1)}, u32[]{:S(2)}) copy-start(bf16[16,2,16,16,128]{4,3,2,1,0:T(8,128)(2,1)S(1)} %get-tuple-element.16.ug_ref) | copy-start | bytes 6291460
  37.1 25.0 %copy-start.5 = (bf16[14,8,512]{2,1,0:T(8,128)(2,1)S(1)}, bf16[14,8,512]{2,1,0:T(8,128)(2,1)}, u32[]{:S(2)}) copy-start(bf16[14,8,512]{2,1,0:T(8,128)(2,1)} %wg_ref.1) | copy-start | bytes 344068
  37.1 25.0 %copy-start.7 = (bf16[14,8,512]{2,1,0:T(8,128)(2,1)S(1)}, bf16[14,8,512]{2,1,0:T(8,128)(2,1)}, u32[]{:S(2)}) copy-start(bf16[14,8,512]{2,1,0:T(8,128)(2,1)} %wu_ref.1) | copy-start | bytes 344068
  56.6 1.2 %collective-permute-start.4 = (bf16[2,16,128]{2,1,0:T(8,128)(2,1)S(1)}, bf16[2,16,128]{2,1,0:T(8,128)(2,1)S(1)}, u32[]{:S(2)}, u32[]{:S(2)}) collective-permute-start(bf16[2,16,128]{2,1,0:T(8,128)(2,1)S(1)} %get-tuple-element.22), channel_id=1, source_target_pairs={{0,1},{1,0},{2,3},{3,2},{4,5},{5,4},{6,7},{7,6},{8,9},{9,8},{10,11... | collective-permute-start | bytes 24584 | tf_op jit(solution)/shard_map/ppermute | solution.py:357
  58.7 15.7 %all-to-all-start.1 = ((bf16[8,2,48,256]{3,2,1,0:T(8,128)(2,1)}), bf16[8,2,48,256]{3,2,1,0:T(8,128)(2,1)S(1)}, u32[]{:S(2)}, u32[]{:S(2)}) async-start(bf16[8,2,48,256]{3,2,1,0:T(8,128)(2,1)} %broadcast_in_dim.2), calls=%async_computation.1 | async-start | bytes 786432 | tf_op jit(solution)/shard_map/all_to_all | solution.py:363
  62.2 1.6 %copy-start.10 = (bf16[16,2,16,16,128]{4,3,2,1,0:T(8,128)(2,1)S(1)}, bf16[16,2,16,16,128]{4,3,2,1,0:T(8,128)(2,1)}, u32[]{:S(2)}) copy-start(bf16[16,2,16,16,128]{4,3,2,1,0:T(8,128)(2,1)} %copy-done.9) | copy-start | bytes 6291460
  63.7 7.9 %copy-start.1 = (bf16[512,512]{1,0:T(8,128)(2,1)S(1)}, bf16[512,512]{1,0:T(8,128)(2,1)}, u32[]{:S(2)}) copy-start(bf16[512,512]{1,0:T(8,128)(2,1)} %constant.11.clone.qt_ref) | copy-start | bytes 1572868
  69.6 2.0 %collective-permute-start.3 = (bf16[16,2,4,16,128]{4,3,2,1,0:T(8,128)(2,1)S(1)}, bf16[16,2,4,16,128]{4,3,2,1,0:T(8,128)(2,1)S(1)}, u32[]{:S(2)}, u32[]{:S(2)}) collective-permute-start(bf16[16,2,4,16,128]{4,3,2,1,0:T(8,128)(2,1)S(1)} %get-tuple-element.18), channel_id=1, source_target_pairs={{0,1},{1,0},{2,3},{3,2},{4,5},{5,4},{6,7},{7,6},{8,9},{9,8},{10,11... | collective-permute-start | bytes 1572872 | tf_op jit(solution)/shard_map/ppermute | solution.py:342

commit v2 on v1

--- a/solution.py
+++ b/solution.py
@@ -79,12 +79,22 @@
     return lane % F == row
 
 
-def main_kernel(groups, fb, x_own, x_other, c_own, c_other, pt_ref, qt_ref, wg_ref, wu_ref, wd_ref,
-                d_ref, gg_ref, ug_ref, sx, sc, gs, us, hs, hid, rg, ru, rd, wexp, flat):
+def main_kernel(groups, fb, wg_in, wu_in, wd_in, pt_in, x_own_in, c_own_in, x_other_in, c_other_in, qt_in,
+                d_ref, gg_out, ug_out, wg_ref, wu_ref, wd_ref, pt_ref, x_own, c_own, x_other, c_other, qt_ref,
+                sx, sc, gs, us, hs, hid, gg_ref, ug_ref, rg, ru, rd, wexp, flat, in_sem, out_sem):
     core = lax.axis_index("mp")
     db = 8
     per = db // 2
     block = pt_ref.shape[0]
+    pairs = (
+        (wg_in, wg_ref), (wu_in, wu_ref), (wd_in, wd_ref), (pt_in, pt_ref), (x_own_in, x_own), (c_own_in, c_own),
+        (x_other_in, x_other), (c_other_in, c_other), (qt_in, qt_ref),
+    )
+    copies = [pltpu.make_async_copy(src, dst, in_sem.at[n]) for n, (src, dst) in enumerate(pairs)]
+    for copy in copies:
+        copy.start()
+    for copy in copies[:3]:
+        copy.wait()
 
     for source, target in ((wg_ref, rg), (wu_ref, ru)):
         for tile in range(block // LANES):
@@ -106,8 +116,10 @@
 
     weight_rows(read_down, write_down, True, groups)
 
-    for own, other, target in ((x_own, x_other, sx), (c_own, c_other, sc)):
-        for source, first in ((own, core * per), (other, (1 - core) * per)):
+    copies[3].wait()
+    for half, first in enumerate((core * per, (1 - core) * per)):
+        for u, (source, target) in enumerate((((x_own, x_other)[half], sx), ((c_own, c_other)[half], sc))):
+            copies[4 + 2 * half + u].wait()
             for j in range(0, per, 2):
                 pair = jnp.concatenate(
                     [source[:, j * block : (j + 1) * block], source[:, (j + 1) * block : (j + 2) * block]], axis=0
@@ -143,6 +155,7 @@
             us[:, g, ri] = forward[1, ri]
             hs[:, g, ri] = back[ri]
 
+    copies[8].wait()
     for target in (gg_ref, ug_ref, hid):
         target[:, :, fb:] = jnp.zeros((groups, 2, ROWS - fb, F, LANES), jnp.bfloat16)
 
@@ -162,6 +175,11 @@
         for u, target in enumerate((hid, gg_ref, ug_ref)):
             target[:, :, o] = result[:, u * LANES : (u + 1) * LANES].reshape(groups, 2, F, LANES)
 
+    stores = [
+        pltpu.make_async_copy(src, dst, out_sem.at[n]) for n, (src, dst) in enumerate(((gg_ref, gg_out), (ug_ref, ug_out)))
+    ]
+    for copy in stores:
+        copy.start()
     keep = diagonal(LANES)
     lane = lax.broadcasted_iota(jnp.int32, (F, LANES), 1)
     row = lax.broadcasted_iota(jnp.int32, (F, LANES), 0)
@@ -182,11 +200,32 @@
             d_ref[g, w * ROWS : (w + 1) * ROWS, :LANES] = re.astype(jnp.bfloat16)
             d_ref[g, w * ROWS : (w + 1) * ROWS, LANES:] = im.astype(jnp.bfloat16)
 
-
-def adjoint_kernel(groups, fb, gg_ref, ug_ref, wg_ref, wu_ref, own_ref, other_ref, ra, rb, wexp, part):
+    for copy in stores:
+        copy.wait()
+
+
+def adjoint_kernel(groups, fb, wg_in, wu_in, gg_in, ug_in, own_ref, other_ref, wg_ref, wu_ref, gg_ref, ug_ref,
+                   ra, rb, wexp, part, in_sem, g_sem):
     core = lax.axis_index("mp")
     db = 8
     per = db // 2
+    weights = [
+        pltpu.make_async_copy(src, dst, in_sem.at[n]) for n, (src, dst) in enumerate(((wg_in, wg_ref), (wu_in, wu_ref)))
+    ]
+
+    def group_copies(g):
+        return [
+            pltpu.make_async_copy(src.at[g], dst.at[g], g_sem.at[n, g])
+            for n, (src, dst) in enumerate(((gg_in, gg_ref), (ug_in, ug_ref)))
+        ]
+
+    for copy in weights:
+        copy.start()
+    for g in range(groups):
+        for copy in group_copies(g):
+            copy.start()
+    for copy in weights:
+        copy.wait()
     for source, target in ((wg_ref, ra), (wu_ref, rb)):
         for upper in range(2):
             def read(o, at, source=source, upper=upper):
@@ -210,6 +249,8 @@
                     row = rows[tile, pl.ds(g * 2 * db + r, F, stride=0), :]
                     at = w * span + tile * LANES
                     wexp[r * F : (r + 1) * F, at : at + LANES] = jnp.where(mask, row, 0.0).astype(jnp.bfloat16)
+        for copy in group_copies(g):
+            copy.wait()
         grads = jnp.concatenate([gg_ref[g].reshape(span, LANES), ug_ref[g].reshape(span, LANES)], axis=0)
         part[...] = jnp.dot(wexp[...], grads, preferred_element_type=jnp.float32).reshape(2, db, F, LANES)
         for ri in range(2):
@@ -225,24 +266,29 @@
         out_ref[:, j * block : (j + 1) * block] = values.T.astype(jnp.bfloat16)
 
 
-def reduce_kernel(r_ref, sum_ref, keep_ref, send_ref):
-    core = lax.axis_index("mp")
+def reduce_kernel(r_ref, out_ref):
     total = r_ref[0].astype(jnp.float32)
     for d in range(1, r_ref.shape[0]):
         total = total + r_ref[d].astype(jnp.float32)
-    sum_ref[...] = total[:, : 2 * ROWS].astype(jnp.bfloat16)
+    total = total.astype(jnp.bfloat16)
+    for d in range(out_ref.shape[0]):
+        out_ref[d] = total
+
+
+def pack_kernel(s_ref, keep_ref, send_ref):
+    core = lax.axis_index("mp")
     low = lax.broadcasted_iota(jnp.int32, (ROWS, LANES), 1) < LANES // 2
-    for g in range(total.shape[0]):
-        re, im = total[g, 2 * ROWS :, :LANES], total[g, 2 * ROWS :, LANES:]
+    for g in range(s_ref.shape[0]):
+        re = s_ref[g, 2 * ROWS :, :LANES].astype(jnp.float32)
+        im = s_ref[g, 2 * ROWS :, LANES:].astype(jnp.float32)
         lower = jnp.where(low, re, pltpu.roll(im, LANES // 2, 1))
         upper = jnp.where(low, pltpu.roll(re, LANES // 2, 1), im)
         keep_ref[g] = jnp.where(core == 0, lower, upper).astype(jnp.bfloat16)
         send_ref[g] = jnp.where(core == 0, upper, lower).astype(jnp.bfloat16)
 
 
-def layout_kernel(scale, fb, s_ref, a_ref, b_ref, gate_ref, up_ref, down_ref, flat):
-    groups = s_ref.shape[0]
-    half = groups * F
+def layout_kernel(scale, fb, s_ref, gate_ref, up_ref, flat):
+    half = s_ref.shape[0] * F
     for w, target in enumerate((gate_ref, up_ref)):
         for ri in range(2):
             for part in range(half // LANES):
@@ -256,14 +302,19 @@
                 for i in range(8):
                     flat[pl.ds(i, fb, stride=8), :] = tiles[i][:fb] * scale
                 target[:, at : at + LANES] = flat[...]
-    outputs = down_ref.shape[0]
-    for h, source in enumerate((a_ref, b_ref)):
+
+
+def down_layout_kernel(scale, fb, keep_ref, got_ref, down_ref):
+    core = lax.axis_index("mp")
+    half = keep_ref.shape[0] * F
+    outputs = down_ref.shape[1]
+    for source, h in ((keep_ref, core), (got_ref, 1 - core)):
         for part in range(half // LANES):
             tiles = swap_blocks([source[part * 8 + i].astype(jnp.float32) for i in range(8)])
             for ri in range(2):
                 at = ri * half + part * LANES
                 for o in range(outputs):
-                    down_ref[o, h * fb : (h + 1) * fb, at : at + LANES] = tiles[ri * outputs + o][:fb] * scale
+                    down_ref[pl.ds(h * fb, fb), o, at : at + LANES] = tiles[ri * outputs + o][:fb] * scale
 
 
 def params(mib):
@@ -271,14 +322,15 @@
 
 
 VMEM = pl.BlockSpec(memory_space=pltpu.VMEM)
-
-
-def call(kernel, out_shape, args, scratch=(), mib=16, flops=0, moved=0):
+HBM = pl.BlockSpec(memory_space=pltpu.HBM)
+
+
+def call(kernel, out_shape, args, scratch=(), mib=16, flops=0, moved=0, in_specs=None, out_specs=None):
     return pl.pallas_call(
         kernel,
         out_shape=out_shape,
-        in_specs=[VMEM] * len(args),
-        out_specs=jax.tree.map(lambda _: VMEM, out_shape),
+        in_specs=in_specs or [VMEM] * len(args),
+        out_specs=out_specs or jax.tree.map(lambda _: VMEM, out_shape),
         scratch_shapes=list(scratch),
         compiler_params=params(mib),
         cost_estimate=pl.CostEstimate(flops=flops, bytes_accessed=moved, transcendentals=0),
@@ -309,21 +361,27 @@
     wu = up_spectra.reshape(fb * db, block)
 
     spec = shape((groups, 2, ROWS, F, LANES), bf16)
+    inputs = (wg, wu, down_all, pt, tokens, cotangent, tokens_other, cotangent_other, qt)
     d_all, gg, ug = call(
         functools.partial(main_kernel, groups, fb),
         (shape((groups, 3 * ROWS, 2 * LANES), bf16), spec, spec),
-        (tokens, tokens_other, cotangent, cotangent_other, pt, qt, wg, wu, down_all),
-        [pltpu.VMEM((groups, 2, db, F, LANES), bf16)] * 2
+        inputs,
+        [pltpu.VMEM(a.shape, a.dtype) for a in inputs]
+        + [pltpu.VMEM((groups, 2, db, F, LANES), bf16)] * 2
         + [pltpu.VMEM((fb, groups, 2, F, LANES), bf16)] * 3
-        + [pltpu.VMEM(spec.shape, bf16)]
+        + [pltpu.VMEM(spec.shape, bf16)] * 3
         + [pltpu.VMEM((2, groups * 2 * ROWS, LANES), f32)] * 3
-        + [pltpu.VMEM((3 * 2 * fb * F, 2 * LANES), bf16), pltpu.VMEM((block // LANES, fb * db, LANES), f32)],
-        mib=40,
+        + [pltpu.VMEM((3 * 2 * fb * F, 2 * LANES), bf16), pltpu.VMEM((block // LANES, fb * db, LANES), f32)]
+        + [pltpu.SemaphoreType.DMA((len(inputs),)), pltpu.SemaphoreType.DMA((2,))],
+        mib=63,
         flops=10**10,
         moved=10**7,
-    )
-
-    if groups % n_dp == 0:
+        in_specs=[HBM] * len(inputs),
+        out_specs=(VMEM, HBM, HBM),
+    )
+
+    direct = groups % n_dp == 0
+    if direct:
         share = groups // n_dp
         got = lax.all_to_all(d_all.reshape(n_dp, share, 3 * ROWS, 2 * LANES), "dp", 0, 0, tiled=True)
     else:
@@ -333,44 +391,42 @@
     own, other = call(
         functools.partial(adjoint_kernel, groups, fb),
         (shape((groups, 2, per, F, LANES), f32), shape((groups, 2, per, F, LANES), bf16)),
-        (gg, ug, gate_spectra, up_spectra),
-        [pltpu.VMEM((4, groups * 2 * db, LANES), f32)] * 2
-        + [pltpu.VMEM((2 * LANES, 8 * LANES), bf16), pltpu.VMEM((2, db, F, LANES), f32)],
+        (gate_spectra, up_spectra, gg, ug),
+        [pltpu.VMEM(gate_spectra.shape, bf16)] * 2
+        + [pltpu.VMEM(spec.shape, bf16)] * 2
+        + [pltpu.VMEM((4, groups * 2 * db, LANES), f32)] * 2
+        + [pltpu.VMEM((2 * LANES, 8 * LANES), bf16), pltpu.VMEM((2, db, F, LANES), f32)]
+        + [pltpu.SemaphoreType.DMA((2,)), pltpu.SemaphoreType.DMA((2, groups))],
+        mib=63,
         flops=2 * 10**9,
         moved=10**7,
-    )
+        in_specs=[HBM] * 4,
+    )
+    total = call(reduce_kernel, shape((n_dp if direct else 1, share, 3 * ROWS, 2 * LANES), bf16), (got,), moved=10**6)
+    total, own, other = lax.optimization_barrier((total, own, other))
     partner = lax.ppermute(other, "mp", swap)
     grad_tokens = call(
         input_kernel, shape(tokens.shape, bf16), (own, partner, qt), flops=5 * 10**8, moved=4 * 10**6
     )
-
-    total, keep, send = call(
-        reduce_kernel,
-        (
-            shape((share, 2 * ROWS, 2 * LANES), bf16),
-            shape((share, ROWS, LANES), bf16),
-            shape((share, ROWS, LANES), bf16),
-        ),
-        (got,),
-        moved=10**6,
-    )
+    if direct:
+        total = lax.all_to_all(total, "dp", 0, 0, tiled=True)
+    total = total.reshape(groups, 3 * ROWS, 2 * LANES)
+    keep, send = call(pack_kernel, (shape((groups, ROWS, LANES), bf16),) * 2, (total,), moved=10**5)
     partner_rows = lax.ppermute(send, "mp", swap)
-    lower = jnp.where(core == 0, keep, partner_rows)
-    upper = jnp.where(core == 0, partner_rows, keep)
-    if groups % n_dp == 0:
-        packed = jnp.concatenate([total, jnp.concatenate([lower, upper], axis=-1)], axis=1)
-        every = jnp.broadcast_to(packed[None], (n_dp,) + packed.shape)
-        packed = lax.all_to_all(every, "dp", 0, 0, tiled=True).reshape(groups, 3 * ROWS, 2 * LANES)
-    else:
-        packed = jnp.concatenate([total, jnp.concatenate([lower, upper], axis=-1)], axis=1)
     scale = 1.0 / math.sqrt(tokens.shape[0] * n_dp)
-    gate_grad, up_grad, down_grad = call(
+    gate_grad, up_grad = call(
         functools.partial(layout_kernel, scale, fb),
-        (shape((fb * db, block), f32), shape((fb * db, block), f32), shape((per, 2 * fb, block), f32)),
-        (packed[:, : 2 * ROWS], packed[:, 2 * ROWS :, :LANES], packed[:, 2 * ROWS :, LANES:]),
+        (shape((fb * db, block), f32),) * 2,
+        (total,),
         [pltpu.VMEM((fb * db, LANES), f32)],
         moved=10**6,
     )
+    down_grad = call(
+        functools.partial(down_layout_kernel, scale, fb),
+        shape((2 * fb, per, block), f32),
+        (keep, partner_rows),
+        moved=10**6,
+    ).transpose(1, 0, 2)
     return (grad_tokens, gate_grad.reshape(fb, db, block), up_grad.reshape(fb, db, block), down_grad)
 
 

time: 77.7 us -> 76 us (0.978)
  blocking collectives: 19.4 us -> 0 us
  Pallas kernels: 35.4 us -> 45.5 us
  local copies, waits for them, and re-layouts: 11.4 us -> 1.69 us
  waiting for transfers between devices: 5.1 us -> 13.7 us
  starting transfers between devices: 4.89 us -> 13.3 us
    all_to_all x1 -> x0, blocking collectives: 19.4 us -> none  [shards(): lax.all_to_all(d_all.reshape(n_dp, share, 3 * ROWS, 2 * LANES), 'dp', 0,...]
    all_to_all x1 -> x2, waiting for transfers between devices: 1.12 us -> 12.6 us  [the longest x1 11.5 us: shards(): total = lax.all_to_all(total, 'dp', 0, 0, tiled=True)]
    pallas_call x5 -> x7, Pallas kernels: 35.4 us -> 45.5 us  [call(): pl.pallas_call(kernel, out_shape=out_shape, in_specs=in_specs or [VMEM] *...]
    unnamed x23 -> x6, local copies, waits for them, and re-layouts: 9.72 us -> 0.8 us
    all_to_all x1 -> x2, starting transfers between devices: 3.45 us -> 12.1 us  [the longest x1 7.17 us: shards(): lax.all_to_all(d_all.reshape(n_dp, share, 3 * ROWS, 2 * LANES), 'dp', 0,...]
    ppermute x1, waiting for transfers between devices: 1.73 us -> 0.01 us  [shards(): partner = lax.ppermute(other, 'mp', swap)]
    ppermute x1, waiting for transfers between devices: 1.16 us -> 0.01 us  [shards(): partner_rows = lax.ppermute(send, 'mp', swap)]
    broadcast_in_dim x1 -> x0, local copies, waits for them, and re-layouts: 0.78 us -> none  [shards(): every = jnp.broadcast_to(packed[None], (n_dp,) + packed.shape)]
  transfers between devices with their start and end apart: 6 -> 7, of which waited for: 4 -> 3; matrix products, arithmetic and copies ran while one was open for 1% -> 2% of each run, Pallas kernels for 10% -> 18%
where the time goes in v2:
time: 76 us; the launch traced here: 75.7 us
  Pallas kernels  45.5 us (60%)
  waiting for transfers between devices  13.7 us (18%)
  starting transfers between devices  13.3 us (18%)
  local copies, waits for them, and re-layouts  1.69 us (2%)
    pallas_call x7, Pallas kernels, call(): pl.pallas_call(kernel, out_shape=out_shape, in_specs=in_specs or [VMEM] *...  45.5 us
    all_to_all x1, waiting for transfers between devices, shards(): total = lax.all_to_all(total, 'dp', 0, 0, tiled=True)  11.5 us
    all_to_all x1, starting transfers between devices, shards(): lax.all_to_all(d_all.reshape(n_dp, share, 3 * ROWS, 2 * LANES), 'dp', 0,...  7.17 us
    all_to_all x1, starting transfers between devices, shards(): total = lax.all_to_all(total, 'dp', 0, 0, tiled=True)  4.93 us
  transfers between devices with their start and end apart: 7, of which 3 were waited for; matrix products, arithmetic and copies ran while one was open for 2% of the time, Pallas kernels for 18%

profile of v2, /device:TPU:0, one launch (start us, length us, event | category | flops | bytes accessed | tf_op | source)
XLA Modules:
  0.0 75.7 jit_solution(16759933232505760084)
XLA Ops:
  0.6 0.6 collective-permute-start.1
  1.2 0.1 collective-permute-start.2
  1.3 0.9 %fusion = (bf16[4,1,14,512]{3,0,2,1:T(4,128)(2,1)S(1)}, bf16[4,1,14,512]{3,0,2,1:T(4,128)(2,1)S(1)}) fusion(bf16[4,2,14,512]{3,0,2,1:T(4,128)(2,1)} %bitcast.16), kind=kLoop, calls=%fused_computation.3 | loop fusion | bytes 229376 | tf_op jit(solution)/shard_map/slice | solution.py:355
  2.2 0.5 collective-permute-start
  2.7 1.1 %collective-permute-done = bf16[4,14,512]{2,1,0:T(8,128)(2,1)S(1)} collective-permute-done((bf16[4,14,512]{2,1,0:T(8,128)(2,1)S(1)}, bf16[4,14,512]{2,1,0:T(8,128)(2,1)S(1)}, u32[]{:S(2)}, u32[]{:S(2)}) %collective-permute-start) | collective-permute-done | bytes 57376 | tf_op jit(solution)/shard_map/ppermute | solution.py:356
  3.8 0.7 maximum_select_fusion.wd_in
  4.5 0.0 collective-permute-done.1.x_other_in
  4.5 0.0 collective-permute-done.2.c_other_in
  4.5 0.8 %copy-done.2 = bf16[128,2048]{1,0:T(8,128)(2,1)} copy-done((bf16[128,2048]{1,0:T(8,128)(2,1)}, bf16[128,2048]{1,0:T(8,128)(2,1)S(1)}, u32[]{:S(2)}) %copy-start.2) | copy-done | bytes 524312
  5.3 29.8 %shard_map.102 = (bf16[16,48,256]{2,1,0:T(8,128)(2,1)}, bf16[16,2,16,16,128]{4,3,2,1,0:T(8,128)(2,1)}, bf16[16,2,16,16,128]{4,3,2,1,0:T(8,128)(2,1)}) custom-call(bf16[112,512]{1,0:T(8,128)(2,1)} %bitcast.19, bf16[112,512]{1,0:T(8,128)(2,1)} %bitcast.20, bf16[8,14,512]{2,1,0:T(8,128)(2,1)} %maximum_select_fusion.wd_in, ...), custom_call_target="tpu_custom_call" | custom-call | flops 10000000000 | bytes 10000000 | tf_op jit(solution)/shard_map/pallas_call | solution.py:329
  35.1 7.2 %all-to-all-start = ((bf16[8,2,48,256]{3,2,1,0:T(8,128)(2,1)}), bf16[8,2,48,256]{3,2,1,0:T(8,128)(2,1)S(1)}, u32[]{:S(2)}, u32[]{:S(2)}) async-start(bf16[8,2,48,256]{3,2,1,0:T(8,128)(2,1)} %bitcast.14), calls=%async_computation | async-start | bytes 786432 | tf_op jit(solution)/shard_map/all_to_all | solution.py:386
  42.2 10.9 %shard_map.104 = (f32[16,2,4,16,128]{4,3,2,1,0:T(8,128)}, bf16[16,2,4,16,128]{4,3,2,1,0:T(8,128)(2,1)}) custom-call(bf16[14,8,512]{2,1,0:T(8,128)(2,1)} %wg_in.1, bf16[14,8,512]{2,1,0:T(8,128)(2,1)} %wu_in.1, bf16[16,2,16,16,128]{4,3,2,1,0:T(8,128)(2,1)} %get-tuple-element.17.gg_in, bf16[16,2,16,16,128]{4,3,2,1,0:T(8,128)(2,1)} %get-tuple-element.18.ug_in), custom_call_target="tpu_custom_call" | custom-call | flops 2000000000 | bytes 10000000 | tf_op jit(solution)/shard_map/pallas_call | solution.py:329
  53.1 0.0 copy-start.1
  53.1 1.1 %all-to-all-done.r_ref = bf16[8,2,48,256]{3,2,1,0:T(8,128)(2,1)S(1)} async-done(((bf16[8,2,48,256]{3,2,1,0:T(8,128)(2,1)}), bf16[8,2,48,256]{3,2,1,0:T(8,128)(2,1)S(1)}, u32[]{:S(2)}, u32[]{:S(2)}) %all-to-all-start) | async-done | bytes 393248 | tf_op jit(solution)/shard_map/all_to_all | solution.py:386
  54.2 0.8 %shard_map.103 = bf16[8,2,48,256]{3,2,1,0:T(8,128)(2,1)} custom-call(bf16[8,2,48,256]{3,2,1,0:T(8,128)(2,1)S(1)} %all-to-all-done.r_ref), custom_call_target="tpu_custom_call" | custom-call | bytes 1000000 | tf_op jit(solution)/shard_map/pallas_call | solution.py:329
  55.0 4.9 %all-to-all-start.1 = ((bf16[8,2,48,256]{3,2,1,0:T(8,128)(2,1)}), bf16[8,2,48,256]{3,2,1,0:T(8,128)(2,1)S(1)}, u32[]{:S(2)}, u32[]{:S(2)}) async-start(bf16[8,2,48,256]{3,2,1,0:T(8,128)(2,1)} %shard_map.103), calls=%async_computation.1 | async-start | bytes 786432 | tf_op jit(solution)/shard_map/all_to_all | solution.py:412
  60.0 0.0 collective-permute-start.3
  60.0 11.5 %all-to-all-done.1 = bf16[8,2,48,256]{3,2,1,0:T(8,128)(2,1)S(1)} async-done(((bf16[8,2,48,256]{3,2,1,0:T(8,128)(2,1)}), bf16[8,2,48,256]{3,2,1,0:T(8,128)(2,1)S(1)}, u32[]{:S(2)}, u32[]{:S(2)}) %all-to-all-start.1) | async-done | bytes 393248 | tf_op jit(solution)/shard_map/all_to_all | solution.py:412
  71.5 0.1 shard_map.107
  71.6 0.1 collective-permute-start.4
  71.7 1.6 %shard_map.105 = bf16[128,2048]{1,0:T(8,128)(2,1)} custom-call(f32[16,2,4,16,128]{4,3,2,1,0:T(8,128)S(1)} %copy-done, bf16[16,2,4,16,128]{4,3,2,1,0:T(8,128)(2,1)S(1)} %collective-permute-done.3.got_ref, bf16[512,512]{1,0:T(8,128)(2,1)S(1)} %copy-done.1), custom_call_target="tpu_custom_call" | custom-call | flops 500000000 | bytes 4000000 | tf_op jit(solution)/shard_map/pallas_call | solution.py:329
  73.3 1.3 %shard_map.106 = (f32[112,512]{1,0:T(8,128)}, f32[112,512]{1,0:T(8,128)}) custom-call(bf16[16,48,256]{2,1,0:T(8,128)(2,1)S(1)} %bitcast.13), custom_call_target="tpu_custom_call" | custom-call | bytes 1000000 | tf_op jit(solution)/shard_map/pallas_call | solution.py:329
  74.6 0.0 collective-permute-done.4.got_ref
  74.6 1.1 %shard_map.108 = f32[28,4,512]{2,1,0:T(4,128)} custom-call(bf16[16,16,128]{2,1,0:T(8,128)(2,1)S(1)} %get-tuple-element.26.keep_ref, bf16[16,16,128]{2,1,0:T(8,128)(2,1)S(1)} %collective-permute-done.4.got_ref), custom_call_target="tpu_custom_call" | custom-call | bytes 1000000 | tf_op jit(solution)/shard_map/pallas_call | solution.py:329
  (6 shorter events, 0.0 us)
Async XLA Ops:
  0.6 3.9 %collective-permute-start.1 = (bf16[128,2048]{1,0:T(8,128)(2,1)}, bf16[128,2048]{1,0:T(8,128)(2,1)S(1)}, u32[]{:S(2)}, u32[]{:S(2)}) collective-permute-start(bf16[128,2048]{1,0:T(8,128)(2,1)} %x_own_in.1), channel_id=1, source_target_pairs={{0,1},{1,0},{2,3},{3,2},{4,5},{5,4},{6,7},{7,6},{8,9},{9,8},{10,11... | collective-permute-start | bytes 1572872 | tf_op jit(solution)/shard_map/ppermute | solution.py:352
  1.2 3.3 %collective-permute-start.2 = (bf16[128,2048]{1,0:T(8,128)(2,1)}, bf16[128,2048]{1,0:T(8,128)(2,1)}, u32[]{:S(2)}, u32[]{:S(2)}) collective-permute-start(bf16[128,2048]{1,0:T(8,128)(2,1)} %c_own_in.1), channel_id=1, source_target_pairs={{0,1},{1,0},{2,3},{3,2},{4,5},{5,4},{6,7},{7,6},{8,9},{9,8},{10,11... | collective-permute-start | bytes 1572872 | tf_op jit(solution)/shard_map/ppermute | solution.py:353
  2.2 1.6 %collective-permute-start = (bf16[4,14,512]{2,1,0:T(8,128)(2,1)S(1)}, bf16[4,14,512]{2,1,0:T(8,128)(2,1)S(1)}, u32[]{:S(2)}, u32[]{:S(2)}) collective-permute-start(bf16[4,14,512]{2,1,0:T(8,128)(2,1)S(1)} %get-tuple-element.29), channel_id=1, source_target_pairs={{0,1},{1,0},{2,3},{3,2},{4,5},{5,4},{6,7},{7,6},{8,9},{9,8},{10,11... | collective-permute-start | bytes 172040 | tf_op jit(solution)/shard_map/ppermute | solution.py:356
  4.5 0.8 %copy-start.2 = (bf16[128,2048]{1,0:T(8,128)(2,1)}, bf16[128,2048]{1,0:T(8,128)(2,1)S(1)}, u32[]{:S(2)}) copy-start(bf16[128,2048]{1,0:T(8,128)(2,1)S(1)} %collective-permute-done.1.x_other_in) | copy-start | bytes 1572868
  35.1 19.1 %all-to-all-start = ((bf16[8,2,48,256]{3,2,1,0:T(8,128)(2,1)}), bf16[8,2,48,256]{3,2,1,0:T(8,128)(2,1)S(1)}, u32[]{:S(2)}, u32[]{:S(2)}) async-start(bf16[8,2,48,256]{3,2,1,0:T(8,128)(2,1)} %bitcast.14), calls=%async_computation | async-start | bytes 786432 | tf_op jit(solution)/shard_map/all_to_all | solution.py:386
  53.1 18.6 %copy-start = (f32[16,2,4,16,128]{4,3,2,1,0:T(8,128)S(1)}, f32[16,2,4,16,128]{4,3,2,1,0:T(8,128)}, u32[]{:S(2)}) copy-start(f32[16,2,4,16,128]{4,3,2,1,0:T(8,128)} %get-tuple-element.21.own_ref) | copy-start | bytes 3145732
  53.1 18.6 %copy-start.1 = (bf16[512,512]{1,0:T(8,128)(2,1)S(1)}, bf16[512,512]{1,0:T(8,128)(2,1)}, u32[]{:S(2)}) copy-start(bf16[512,512]{1,0:T(8,128)(2,1)} %constant.11.clone.qt_in.qt_ref) | copy-start | bytes 1572868
  55.0 16.5 %all-to-all-start.1 = ((bf16[8,2,48,256]{3,2,1,0:T(8,128)(2,1)}), bf16[8,2,48,256]{3,2,1,0:T(8,128)(2,1)S(1)}, u32[]{:S(2)}, u32[]{:S(2)}) async-start(bf16[8,2,48,256]{3,2,1,0:T(8,128)(2,1)} %shard_map.103), calls=%async_computation.1 | async-start | bytes 786432 | tf_op jit(solution)/shard_map/all_to_all | solution.py:412
  60.0 11.7 %collective-permute-start.3 = (bf16[16,2,4,16,128]{4,3,2,1,0:T(8,128)(2,1)}, bf16[16,2,4,16,128]{4,3,2,1,0:T(8,128)(2,1)S(1)}, u32[]{:S(2)}, u32[]{:S(2)}) collective-permute-start(bf16[16,2,4,16,128]{4,3,2,1,0:T(8,128)(2,1)} %get-tuple-element.22), channel_id=1, source_target_pairs={{0,1},{1,0},{2,3},{3,2},{4,5},{5,4},{6,7},{7,6},{8,9},{9,8},{10,11... | collective-permute-start | bytes 1572872 | tf_op jit(solution)/shard_map/ppermute | solution.py:407
  71.6 3.0 %collective-permute-start.4 = (bf16[16,16,128]{2,1,0:T(8,128)(2,1)S(1)}, bf16[16,16,128]{2,1,0:T(8,128)(2,1)S(1)}, u32[]{:S(2)}, u32[]{:S(2)}) collective-permute-start(bf16[16,16,128]{2,1,0:T(8,128)(2,1)S(1)} %get-tuple-element.27), channel_id=1, source_target_pairs={{0,1},{1,0},{2,3},{3,2},{4,5},{5,4},{6,7},{7,6},{8,9},{9,8},{10,11... | collective-permute-start | bytes 196616 | tf_op jit(solution)/shard_map/ppermute | solution.py:415

commit v3 on v2

--- a/solution.py
+++ b/solution.py
@@ -73,41 +73,71 @@
             write(g, 1, 1, cross)
 
 
-def diagonal(width):
-    row = lax.broadcasted_iota(jnp.int32, (F, width), 0)
-    lane = lax.broadcasted_iota(jnp.int32, (F, width), 1)
-    return lane % F == row
-
-
-def main_kernel(groups, fb, wg_in, wu_in, wd_in, pt_in, x_own_in, c_own_in, x_other_in, c_other_in, qt_in,
-                d_ref, gg_out, ug_out, wg_ref, wu_ref, wd_ref, pt_ref, x_own, c_own, x_other, c_other, qt_ref,
-                sx, sc, gs, us, hs, hid, gg_ref, ug_ref, rg, ru, rd, wexp, flat, in_sem, out_sem):
+def diagonal():
+    row = lax.broadcasted_iota(jnp.int32, (F, LANES), 0)
+    lane = lax.broadcasted_iota(jnp.int32, (F, LANES), 1)
+    return jnp.where(lane % F == row, 1.0, 0.0).astype(jnp.bfloat16)
+
+
+def spread(rows, tiles, base, count, mask):
+    return jnp.concatenate(
+        [
+            jnp.concatenate(
+                [rows[tile, pl.ds(base + r, F, stride=0), :].astype(jnp.bfloat16) * mask for tile in range(tiles)],
+                axis=1,
+            )
+            for r in range(count)
+        ],
+        axis=0,
+    )
+
+
+def main_kernel(groups, fb, wg_in, wu_in, pt_in, x_own_in, c_own_in, wd_own_in, wd_other_in, x_other_in, c_other_in,
+                qt_in, d_ref, gg_out, ug_out, wg_ref, wu_ref, pt_ref, x_own, c_own, wd_ref, x_other, c_other, qt_ref,
+                sx, sc, gs, us, hs, hid, gg_ref, ug_ref, rg, ru, rd, flat, in_sem, out_sem):
     core = lax.axis_index("mp")
     db = 8
     per = db // 2
     block = pt_ref.shape[0]
     pairs = (
-        (wg_in, wg_ref), (wu_in, wu_ref), (wd_in, wd_ref), (pt_in, pt_ref), (x_own_in, x_own), (c_own_in, c_own),
+        (wg_in, wg_ref), (wu_in, wu_ref), (pt_in, pt_ref), (x_own_in, x_own), (c_own_in, c_own),
+        (wd_own_in, wd_ref.at[pl.ds(core * per, per)]), (wd_other_in, wd_ref.at[pl.ds((1 - core) * per, per)]),
         (x_other_in, x_other), (c_other_in, c_other), (qt_in, qt_ref),
     )
     copies = [pltpu.make_async_copy(src, dst, in_sem.at[n]) for n, (src, dst) in enumerate(pairs)]
     for copy in copies:
         copy.start()
-    for copy in copies[:3]:
+
+    def to_spectra(source, target, first):
+        for j in range(0, per, 2):
+            pair = jnp.concatenate(
+                [source[:, j * block : (j + 1) * block], source[:, (j + 1) * block : (j + 2) * block]], axis=0
+            )
+            result = nt_dot(pt_ref[...], pair).astype(jnp.bfloat16)
+            for u in range(2):
+                target[:, :, first + j + u] = result[:, u * LANES : (u + 1) * LANES].reshape(groups, 2, F, LANES)
+
+    for copy in copies[:5]:
         copy.wait()
-
-    for source, target in ((wg_ref, rg), (wu_ref, ru)):
+    to_spectra(x_own, sx, core * per)
+    to_spectra(c_own, sc, core * per)
+    for n, (source, target) in enumerate(((wg_ref, rg), (wu_ref, ru))):
         for tile in range(block // LANES):
-            flat[tile] = source[:, tile * LANES : (tile + 1) * LANES].astype(jnp.float32)
-
-        def read(i, at):
-            return flat[at // LANES, pl.ds(i, fb, stride=db), :]
+            flat[n, tile] = source[:, tile * LANES : (tile + 1) * LANES].astype(jnp.float32)
+
+        def read(i, at, n=n):
+            return flat[n, at // LANES, pl.ds(i, fb, stride=db), :]
 
         def write(g, ri, tile, rows, target=target):
             target[tile, g * 2 * ROWS + ri * ROWS : g * 2 * ROWS + ri * ROWS + fb, :] = rows
 
         weight_rows(read, write, False, groups)
 
+    for copy in copies[5:9]:
+        copy.wait()
+    to_spectra(x_other, sx, (1 - core) * per)
+    to_spectra(c_other, sc, (1 - core) * per)
+
     def read_down(o, at):
         return wd_ref[o, :, at : at + LANES].astype(jnp.float32)
 
@@ -115,97 +145,106 @@
         rd[tile, g * 2 * ROWS + ri * ROWS : g * 2 * ROWS + ri * ROWS + fb, :] = rows
 
     weight_rows(read_down, write_down, True, groups)
-
-    copies[3].wait()
-    for half, first in enumerate((core * per, (1 - core) * per)):
-        for u, (source, target) in enumerate((((x_own, x_other)[half], sx), ((c_own, c_other)[half], sc))):
-            copies[4 + 2 * half + u].wait()
-            for j in range(0, per, 2):
-                pair = jnp.concatenate(
-                    [source[:, j * block : (j + 1) * block], source[:, (j + 1) * block : (j + 2) * block]], axis=0
-                )
-                result = nt_dot(pt_ref[...], pair).astype(jnp.bfloat16)
-                for u in range(2):
-                    target[:, :, first + j + u] = result[:, u * LANES : (u + 1) * LANES].reshape(groups, 2, F, LANES)
-
-    mask = diagonal(LANES)
+    for target in (gg_ref, ug_ref):
+        target[:, :, fb:] = jnp.zeros((groups, 2, ROWS - fb, F, LANES), jnp.bfloat16)
+
+    mask = diagonal()
+    span = fb * F
 
     @pl.loop(0, groups)
     def _(g):
-        for w, rows in enumerate((rg, ru, rd)):
+        for rows, source, target in ((rg, sx, gs), (ru, sx, us), (rd, sc, hs)):
+            spectrum = source[g].reshape(2 * LANES, LANES)
             for ri in range(2):
-                for o in range(fb):
-                    at = ((w * 2 + ri) * fb + o) * F
-                    for tile in range(2):
-                        row = rows[tile, pl.ds(g * 2 * ROWS + ri * ROWS + o, F, stride=0), :]
-                        wexp[at : at + F, tile * LANES : (tile + 1) * LANES] = jnp.where(mask, row, 0.0).astype(
-                            jnp.bfloat16
-                        )
-        span = 2 * fb * F
-        forward = jnp.dot(
-            wexp[0 : 2 * span, :], sx[g].reshape(2 * LANES, LANES), preferred_element_type=jnp.float32
-        ).astype(jnp.bfloat16)
-        forward = forward.reshape(2, 2, fb, F, LANES)
-        back = jnp.dot(
-            wexp[2 * span : 3 * span, :], sc[g].reshape(2 * LANES, LANES), preferred_element_type=jnp.float32
-        ).astype(jnp.bfloat16)
-        back = back.reshape(2, fb, F, LANES)
-        for ri in range(2):
-            gs[:, g, ri] = forward[0, ri]
-            us[:, g, ri] = forward[1, ri]
-            hs[:, g, ri] = back[ri]
-
-    copies[8].wait()
-    for target in (gg_ref, ug_ref, hid):
-        target[:, :, fb:] = jnp.zeros((groups, 2, ROWS - fb, F, LANES), jnp.bfloat16)
-
-    @pl.loop(0, fb)
-    def _(o):
-        spectra = jnp.concatenate([ref[o].reshape(block, LANES) for ref in (gs, us, hs)], axis=1)
+                result = jnp.dot(
+                    spread(rows, 2, g * 2 * ROWS + ri * ROWS, fb, mask), spectrum, preferred_element_type=jnp.float32
+                )
+                target[:, g, ri] = result.astype(jnp.bfloat16).reshape(fb, F, LANES)
+
+    copies[9].wait()
+
+    @pl.loop(0, fb // 2)
+    def _(pair):
+        spectra = jnp.concatenate(
+            [ref[2 * pair + u].reshape(block, LANES) for u in range(2) for ref in (gs, us, hs)], axis=1
+        )
         values = jnp.dot(qt_ref[...], spectra, preferred_element_type=jnp.float32)
-        gate, up, grad = (values[:, u * LANES : (u + 1) * LANES] for u in range(3))
-        sig = 1.0 / (1.0 + jnp.exp(-gate))
-        gated = gate * sig
-        hidden = (gated * up).astype(jnp.bfloat16)
-        gate_grad = (grad * up * sig * (1.0 + gate * (1.0 - sig))).astype(jnp.bfloat16)
-        up_grad = (grad * gated).astype(jnp.bfloat16)
-        result = jnp.dot(
-            pt_ref[...], jnp.concatenate([hidden, gate_grad, up_grad], axis=1), preferred_element_type=jnp.float32
-        ).astype(jnp.bfloat16)
-        for u, target in enumerate((hid, gg_ref, ug_ref)):
-            target[:, :, o] = result[:, u * LANES : (u + 1) * LANES].reshape(groups, 2, F, LANES)
+        sides = []
+        for u in range(2):
+            gate, up, grad = (values[:, (3 * u + v) * LANES : (3 * u + v + 1) * LANES] for v in range(3))
+            sig = 1.0 / (1.0 + jnp.exp(-gate))
+            gated = gate * sig
+            sides.append((gated * up).astype(jnp.bfloat16))
+            sides.append((grad * up * sig * (1.0 + gate * (1.0 - sig))).astype(jnp.bfloat16))
+            sides.append((grad * gated).astype(jnp.bfloat16))
+        result = jnp.dot(pt_ref[...], jnp.concatenate(sides, axis=1), preferred_element_type=jnp.float32)
+        result = result.astype(jnp.bfloat16)
+        for u in range(2):
+            for v, target in enumerate((hid, gg_ref, ug_ref)):
+                at = (3 * u + v) * LANES
+                target[:, :, 2 * pair + u] = result[:, at : at + LANES].reshape(groups, 2, F, LANES)
 
     stores = [
         pltpu.make_async_copy(src, dst, out_sem.at[n]) for n, (src, dst) in enumerate(((gg_ref, gg_out), (ug_ref, ug_out)))
     ]
     for copy in stores:
         copy.start()
-    keep = diagonal(LANES)
-    lane = lax.broadcasted_iota(jnp.int32, (F, LANES), 1)
-    row = lax.broadcasted_iota(jnp.int32, (F, LANES), 0)
+    lane = lax.broadcasted_iota(jnp.int32, (8, LANES), 1)
+    row = lax.broadcasted_iota(jnp.int32, (8, LANES), 0)
+    low = lane % F < 8
 
     @pl.loop(0, groups)
     def _(g):
-        first = (lane % F == 0) & (row == 0) & (g == 0)
-        weight = jnp.where(keep, jnp.where(first, 1.0, 2.0), 0.0)
-        weight_pair = jnp.where(first, 0.0, weight)
-        weight_first = jnp.where(first, 1.0, 0.0)
-        span = 2 * ROWS * F
-        for w, (rows, cols, sign) in enumerate(((gg_ref, sx, 1.0), (ug_ref, sx, 1.0), (hid, sc, -1.0))):
-            m = nt_dot(rows[g].reshape(span, LANES), cols[g].reshape(2 * LANES, LANES)).reshape(2, ROWS, F, 2 * LANES)
-            rr, ri = m[0, :, :, :LANES], m[0, :, :, LANES:]
-            ir, ii = m[1, :, :, :LANES], m[1, :, :, LANES:]
-            re = jnp.sum(rr * weight + ii * weight_pair, axis=1)
-            im = jnp.sum((ir - ri) * (sign * weight_pair) + ii * weight_first, axis=1)
-            d_ref[g, w * ROWS : (w + 1) * ROWS, :LANES] = re.astype(jnp.bfloat16)
-            d_ref[g, w * ROWS : (w + 1) * ROWS, LANES:] = im.astype(jnp.bfloat16)
+        first = (lane % F == 0) & (g == 0)
+        for w, (rows, cols, sign) in enumerate(((gg_ref, sx, 1), (ug_ref, sx, 1), (hid, sc, -1))):
+            m = nt_dot(rows[g, :, :fb].reshape(2 * span, LANES), cols[g].reshape(2 * LANES, LANES))
+            re, im = [], []
+            for upper in range(0, fb, 8):
+                re_tile = jnp.zeros((8, LANES), jnp.float32)
+                im_tile = jnp.zeros((8, LANES), jnp.float32)
+                for o in range(upper, min(upper + 8, fb)):
+                    def part(a, b, o=o, m=m):
+                        at = a * span + o * F
+                        lanes = slice(b * LANES, (b + 1) * LANES)
+                        return jnp.where(low, m[at : at + 8, lanes], m[at + 8 : at + F, lanes])
+
+                    rr, ri, ir, ii = part(0, 0), part(0, 1), part(1, 0), part(1, 1)
+                    cross = ir - ri if sign > 0 else ri - ir
+                    turn = o - upper
+                    here = (row - lane) % 8 == turn
+                    both = rr + jnp.where(first, 0.0, ii)
+                    cross = jnp.where(first, ii, cross)
+                    if turn:
+                        both, cross = pltpu.roll(both, turn, 0), pltpu.roll(cross, turn, 0)
+                    re_tile = jnp.where(here, both, re_tile)
+                    im_tile = jnp.where(here, cross, im_tile)
+                re.append(re_tile)
+                im.append(im_tile)
+            d_ref[g, w * ROWS : (w + 1) * ROWS, :LANES] = jnp.concatenate(re, axis=0).astype(jnp.bfloat16)
+            d_ref[g, w * ROWS : (w + 1) * ROWS, LANES:] = jnp.concatenate(im, axis=0).astype(jnp.bfloat16)
 
     for copy in stores:
         copy.wait()
 
 
+def straight(tile):
+    halves = []
+    lane = lax.broadcasted_iota(jnp.int32, (8, LANES), 1)
+    for at in range(0, tile.shape[0], 8):
+        half = tile[at : at + 8]
+        for bit in (1, 2, 4):
+            half = jnp.where((lane & bit) != 0, pltpu.roll(half, 8 - bit, 0), half)
+        halves.append(half)
+    return jnp.concatenate(halves, axis=0)
+
+
+def factor(scale, part):
+    lane = lax.broadcasted_iota(jnp.int32, (1, LANES), 1)
+    return jnp.where((lane == 0) & (part == 0), scale, 2.0 * scale)
+
+
 def adjoint_kernel(groups, fb, wg_in, wu_in, gg_in, ug_in, own_ref, other_ref, wg_ref, wu_ref, gg_ref, ug_ref,
-                   ra, rb, wexp, part, in_sem, g_sem):
+                   ra, rb, part, in_sem, g_sem):
     core = lax.axis_index("mp")
     db = 8
     per = db // 2
@@ -238,21 +277,16 @@
                 target[tile * 2 + upper, g * 2 * db + ri * db : g * 2 * db + (ri + 1) * db, :] = rows
 
             weight_rows(read, write, True, groups)
-    mask = diagonal(LANES)
+    mask = diagonal()
     span = 4 * LANES
 
     @pl.loop(0, groups)
     def _(g):
-        for w, rows in enumerate((ra, rb)):
-            for r in range(2 * db):
-                for tile in range(4):
-                    row = rows[tile, pl.ds(g * 2 * db + r, F, stride=0), :]
-                    at = w * span + tile * LANES
-                    wexp[r * F : (r + 1) * F, at : at + LANES] = jnp.where(mask, row, 0.0).astype(jnp.bfloat16)
         for copy in group_copies(g):
             copy.wait()
+        rows = jnp.concatenate([spread(ref, 4, g * 2 * db, 2 * db, mask) for ref in (ra, rb)], axis=1)
         grads = jnp.concatenate([gg_ref[g].reshape(span, LANES), ug_ref[g].reshape(span, LANES)], axis=0)
-        part[...] = jnp.dot(wexp[...], grads, preferred_element_type=jnp.float32).reshape(2, db, F, LANES)
+        part[...] = jnp.dot(rows, grads, preferred_element_type=jnp.float32).reshape(2, db, F, LANES)
         for ri in range(2):
             own_ref[g, ri] = part[ri, pl.ds(core * per, per)]
             other_ref[g, ri] = part[ri, pl.ds((1 - core) * per, per)].astype(jnp.bfloat16)
@@ -294,13 +328,17 @@
             for part in range(half // LANES):
                 tiles = swap_blocks(
                     [
-                        s_ref[part * 8 + i, w * ROWS : (w + 1) * ROWS, ri * LANES : (ri + 1) * LANES].astype(jnp.float32)
+                        straight(
+                            s_ref[part * 8 + i, w * ROWS : (w + 1) * ROWS, ri * LANES : (ri + 1) * LANES].astype(
+                                jnp.float32
+                            )
+                        )
                         for i in range(8)
                     ]
                 )
                 at = ri * half + part * LANES
                 for i in range(8):
-                    flat[pl.ds(i, fb, stride=8), :] = tiles[i][:fb] * scale
+                    flat[pl.ds(i, fb, stride=8), :] = tiles[i][:fb] * factor(scale, part)
                 target[:, at : at + LANES] = flat[...]
 
 
@@ -310,11 +348,13 @@
     outputs = down_ref.shape[1]
     for source, h in ((keep_ref, core), (got_ref, 1 - core)):
         for part in range(half // LANES):
-            tiles = swap_blocks([source[part * 8 + i].astype(jnp.float32) for i in range(8)])
+            tiles = swap_blocks([straight(source[part * 8 + i].astype(jnp.float32)) for i in range(8)])
             for ri in range(2):
                 at = ri * half + part * LANES
                 for o in range(outputs):
-                    down_ref[pl.ds(h * fb, fb), o, at : at + LANES] = tiles[ri * outputs + o][:fb] * scale
+                    down_ref[pl.ds(h * fb, fb), o, at : at + LANES] = tiles[ri * outputs + o][:fb] * factor(
+                        scale, part
+                    )
 
 
 def params(mib):
@@ -342,7 +382,7 @@
     core = lax.axis_index("mp")
     swap = [(0, 1), (1, 0)]
     fb, db, block = gate_spectra.shape
-    assert db == 8 and fb <= ROWS and tokens.shape[0] == LANES and lax.axis_size("mp") == 2
+    assert db == 8 and fb <= ROWS and fb % 2 == 0 and tokens.shape[0] == LANES and lax.axis_size("mp") == 2
     groups = block // 2 // F
     per = db // 2
     bf16, f32 = jnp.bfloat16, jnp.float32
@@ -354,24 +394,23 @@
     down = down_spectra.reshape(per, 2, fb, block)
     down_own = jnp.where(core == 0, down[:, 0], down[:, 1])
     down_got = lax.ppermute(jnp.where(core == 0, down[:, 1], down[:, 0]), "mp", swap)
-    down_all = jnp.where(
-        core == 0, jnp.concatenate([down_own, down_got], 0), jnp.concatenate([down_got, down_own], 0)
-    )
     wg = gate_spectra.reshape(fb * db, block)
     wu = up_spectra.reshape(fb * db, block)
 
     spec = shape((groups, 2, ROWS, F, LANES), bf16)
-    inputs = (wg, wu, down_all, pt, tokens, cotangent, tokens_other, cotangent_other, qt)
+    inputs = (wg, wu, pt, tokens, cotangent, down_own, down_got, tokens_other, cotangent_other, qt)
+    buffers = [shape(a.shape, bf16) for a in (wg, wu, pt, tokens, cotangent)]
+    buffers += [shape((db, fb, block), bf16)] + [shape(a.shape, bf16) for a in (tokens_other, cotangent_other, qt)]
     d_all, gg, ug = call(
         functools.partial(main_kernel, groups, fb),
         (shape((groups, 3 * ROWS, 2 * LANES), bf16), spec, spec),
         inputs,
-        [pltpu.VMEM(a.shape, a.dtype) for a in inputs]
+        [pltpu.VMEM(a.shape, a.dtype) for a in buffers]
         + [pltpu.VMEM((groups, 2, db, F, LANES), bf16)] * 2
         + [pltpu.VMEM((fb, groups, 2, F, LANES), bf16)] * 3
         + [pltpu.VMEM(spec.shape, bf16)] * 3
         + [pltpu.VMEM((2, groups * 2 * ROWS, LANES), f32)] * 3
-        + [pltpu.VMEM((3 * 2 * fb * F, 2 * LANES), bf16), pltpu.VMEM((block // LANES, fb * db, LANES), f32)]
+        + [pltpu.VMEM((2, block // LANES, fb * db, LANES), f32)]
         + [pltpu.SemaphoreType.DMA((len(inputs),)), pltpu.SemaphoreType.DMA((2,))],
         mib=63,
         flops=10**10,
@@ -395,7 +434,7 @@
         [pltpu.VMEM(gate_spectra.shape, bf16)] * 2
         + [pltpu.VMEM(spec.shape, bf16)] * 2
         + [pltpu.VMEM((4, groups * 2 * db, LANES), f32)] * 2
-        + [pltpu.VMEM((2 * LANES, 8 * LANES), bf16), pltpu.VMEM((2, db, F, LANES), f32)]
+        + [pltpu.VMEM((2, db, F, LANES), f32)]
         + [pltpu.SemaphoreType.DMA((2,)), pltpu.SemaphoreType.DMA((2, groups))],
         mib=63,
         flops=2 * 10**9,
@@ -403,11 +442,11 @@
         in_specs=[HBM] * 4,
     )
     total = call(reduce_kernel, shape((n_dp if direct else 1, share, 3 * ROWS, 2 * LANES), bf16), (got,), moved=10**6)
-    total, own, other = lax.optimization_barrier((total, own, other))
     partner = lax.ppermute(other, "mp", swap)
     grad_tokens = call(
         input_kernel, shape(tokens.shape, bf16), (own, partner, qt), flops=5 * 10**8, moved=4 * 10**6
     )
+    total, grad_tokens = lax.optimization_barrier((total, grad_tokens))
     if direct:
         total = lax.all_to_all(total, "dp", 0, 0, tiled=True)
     total = total.reshape(groups, 3 * ROWS, 2 * LANES)

time: 76 us -> 70.3 us (0.925)
  blocking collectives: 0 us -> 18.1 us
  waiting for transfers between devices: 13.7 us -> 3.02 us
  Pallas kernels: 45.5 us -> 36.1 us
  starting transfers between devices: 13.3 us -> 8.36 us
  local copies, waits for them, and re-layouts: 1.69 us -> 2.92 us
    all_to_all x0 -> x1, blocking collectives: none -> 18.1 us  [shards(): total = lax.all_to_all(total, 'dp', 0, 0, tiled=True)]
    all_to_all x1 -> x0, waiting for transfers between devices: 11.5 us -> none  [shards(): total = lax.all_to_all(total, 'dp', 0, 0, tiled=True)]
    pallas_call x7, Pallas kernels: 45.5 us -> 36.1 us  [call(): pl.pallas_call(kernel, out_shape=out_shape, in_specs=in_specs or [VMEM] *...]
    all_to_all x1 -> x0, starting transfers between devices: 4.93 us -> none  [shards(): total = lax.all_to_all(total, 'dp', 0, 0, tiled=True)]
    ppermute x1, waiting for transfers between devices: 0.01 us -> 2.11 us  [shards(): partner = lax.ppermute(other, 'mp', swap)]
    unnamed x6 -> x8, local copies, waits for them, and re-layouts: 0.8 us -> 2.03 us
    all_to_all x1, waiting for transfers between devices: 1.08 us -> 0.01 us  [shards(): lax.all_to_all(d_all.reshape(n_dp, share, 3 * ROWS, 2 * LANES), 'dp', 0,...]
  transfers between devices with their start and end apart: 7 -> 6, of which waited for: 3 -> 2; matrix products, arithmetic and copies ran while one was open for 2% -> 2% of each run, Pallas kernels for 18% -> 18%
where the time goes in v3:
time: 70.3 us; the launch traced here: 69.9 us
  Pallas kernels  36.1 us (51%)
  blocking collectives  18.1 us (26%)
  starting transfers between devices  8.36 us (12%)
  waiting for transfers between devices  3.02 us (4%)
  local copies, waits for them, and re-layouts  2.92 us (4%)
    pallas_call x7, Pallas kernels, call(): pl.pallas_call(kernel, out_shape=out_shape, in_specs=in_specs or [VMEM] *...  36.1 us
    all_to_all x1, blocking collectives, shards(): total = lax.all_to_all(total, 'dp', 0, 0, tiled=True)  18.1 us
    all_to_all x1, starting transfers between devices, shards(): lax.all_to_all(d_all.reshape(n_dp, share, 3 * ROWS, 2 * LANES), 'dp', 0,...  7.15 us
    ppermute x1, waiting for transfers between devices, shards(): partner = lax.ppermute(other, 'mp', swap)  2.11 us
    unnamed x8, local copies, waits for them, and re-layouts  2.03 us
  transfers between devices with their start and end apart: 6, of which 2 were waited for; matrix products, arithmetic and copies ran while one was open for 2% of the time, Pallas kernels for 18%

profile of v3, /device:TPU:0, one launch (start us, length us, event | category | flops | bytes accessed | tf_op | source)
XLA Modules:
  0.0 69.9 jit_solution(7133363583276361539)
XLA Ops:
  0.6 0.6 collective-permute-start.1
  1.2 0.1 collective-permute-start.2
  1.3 0.9 %fusion = (bf16[4,1,14,512]{3,0,2,1:T(4,128)(2,1)S(1)}, bf16[4,1,14,512]{3,0,2,1:T(4,128)(2,1)S(1)}) fusion(bf16[4,2,14,512]{3,0,2,1:T(4,128)(2,1)} %bitcast.16), kind=kLoop, calls=%fused_computation.2 | loop fusion | bytes 229376 | tf_op jit(solution)/shard_map/slice | solution.py:395
  2.2 0.7 select_bitcast_fusion
  2.8 0.4 collective-permute-start
  3.2 0.9 %collective-permute-done.wd_other_in = bf16[4,14,512]{2,1,0:T(8,128)(2,1)S(1)} collective-permute-done((bf16[4,14,512]{2,1,0:T(8,128)(2,1)S(1)}, bf16[4,14,512]{2,1,0:T(8,128)(2,1)S(1)}, u32[]{:S(2)}, u32[]{:S(2)}) %collective-permute-start) | collective-permute-done | bytes 57376 | tf_op jit(solution)/shard_map/ppermute | solution.py:396
  4.2 0.0 collective-permute-done.1.x_other_in
  4.2 0.6 copy-done.3
  4.8 0.2 copy-done.2
  5.0 22.5 %shard_map.102 = (bf16[16,48,256]{2,1,0:T(8,128)(2,1)}, bf16[16,2,16,16,128]{4,3,2,1,0:T(8,128)(2,1)}, bf16[16,2,16,16,128]{4,3,2,1,0:T(8,128)(2,1)}) custom-call(bf16[112,512]{1,0:T(8,128)(2,1)} %bitcast.19, bf16[112,512]{1,0:T(8,128)(2,1)} %bitcast.20, bf16[512,512]{1,0:T(8,128)(2,1)} %constant.10.clone.pt_in, bf16[128,2048]{1,0:T(8,128)(2,1)} %x_own_in.1, ...), custom_call_target="tpu_custom_call" | custom-call | flops 10000000000 | bytes 10000000 | tf_op jit(solution)/shard_map/pallas_call | solution.py:369
  27.5 7.1 %all-to-all-start = ((bf16[8,2,48,256]{3,2,1,0:T(8,128)(2,1)}), bf16[8,2,48,256]{3,2,1,0:T(8,128)(2,1)S(1)}, u32[]{:S(2)}, u32[]{:S(2)}) async-start(bf16[8,2,48,256]{3,2,1,0:T(8,128)(2,1)} %bitcast.14), calls=%async_computation | async-start | bytes 786432 | tf_op jit(solution)/shard_map/all_to_all | solution.py:425
  34.7 9.5 %shard_map.104 = (f32[16,2,4,16,128]{4,3,2,1,0:T(8,128)}, bf16[16,2,4,16,128]{4,3,2,1,0:T(8,128)(2,1)}) custom-call(bf16[14,8,512]{2,1,0:T(8,128)(2,1)} %wg_in.1, bf16[14,8,512]{2,1,0:T(8,128)(2,1)} %wu_in.1, bf16[16,2,16,16,128]{4,3,2,1,0:T(8,128)(2,1)} %get-tuple-element.16.gg_in, bf16[16,2,16,16,128]{4,3,2,1,0:T(8,128)(2,1)} %get-tuple-element.17.ug_in), custom_call_target="tpu_custom_call" | custom-call | flops 2000000000 | bytes 10000000 | tf_op jit(solution)/shard_map/pallas_call | solution.py:369
  44.2 0.1 collective-permute-start.3
  44.2 2.1 %collective-permute-done.3.got_ref = bf16[16,2,4,16,128]{4,3,2,1,0:T(8,128)(2,1)S(1)} collective-permute-done((bf16[16,2,4,16,128]{4,3,2,1,0:T(8,128)(2,1)}, bf16[16,2,4,16,128]{4,3,2,1,0:T(8,128)(2,1)S(1)}, u32[]{:S(2)}, u32[]{:S(2)}) %collective-permute-start.3) | collective-permute-done | bytes 524320 | tf_op jit(solution)/shard_map/ppermute | solution.py:445
  46.4 1.2 %copy-done = f32[16,2,4,16,128]{4,3,2,1,0:T(8,128)S(1)} copy-done((f32[16,2,4,16,128]{4,3,2,1,0:T(8,128)S(1)}, f32[16,2,4,16,128]{4,3,2,1,0:T(8,128)}, u32[]{:S(2)}) %copy-start) | copy-done | bytes 1048600
  47.6 1.6 %shard_map.105 = bf16[128,2048]{1,0:T(8,128)(2,1)} custom-call(f32[16,2,4,16,128]{4,3,2,1,0:T(8,128)S(1)} %copy-done, bf16[16,2,4,16,128]{4,3,2,1,0:T(8,128)(2,1)S(1)} %collective-permute-done.3.got_ref, bf16[512,512]{1,0:T(8,128)(2,1)S(1)} %copy-done.1), custom_call_target="tpu_custom_call" | custom-call | flops 500000000 | bytes 4000000 | tf_op jit(solution)/shard_map/pallas_call | solution.py:369
  49.2 0.0 all-to-all-done.r_ref
  49.2 0.1 shard_map.103
  49.2 18.1 %all_to_all.10 = bf16[8,2,48,256]{3,2,1,0:T(8,128)(2,1)S(1)} all-to-all(bf16[8,2,48,256]{3,2,1,0:T(8,128)(2,1)S(1)} %shard_map.103), channel_id=1, replica_groups=mesh['groups'=2,'dp'=8,'mp'=2] {'dp'}, dimensions={0} | all-to-all | bytes 786432 | tf_op jit(solution)/shard_map/all_to_all | solution.py:451
  67.4 0.1 shard_map.107
  67.5 0.1 collective-permute-start.4
  67.6 1.3 %shard_map.106 = (f32[112,512]{1,0:T(8,128)}, f32[112,512]{1,0:T(8,128)}) custom-call(bf16[16,48,256]{2,1,0:T(8,128)(2,1)S(1)} %bitcast.13), custom_call_target="tpu_custom_call" | custom-call | bytes 1000000 | tf_op jit(solution)/shard_map/pallas_call | solution.py:369
  68.9 0.0 collective-permute-done.4.got_ref
  68.9 1.1 %shard_map.108 = f32[28,4,512]{2,1,0:T(4,128)} custom-call(bf16[16,16,128]{2,1,0:T(8,128)(2,1)S(1)} %get-tuple-element.24.keep_ref, bf16[16,16,128]{2,1,0:T(8,128)(2,1)S(1)} %collective-permute-done.4.got_ref), custom_call_target="tpu_custom_call" | custom-call | bytes 1000000 | tf_op jit(solution)/shard_map/pallas_call | solution.py:369
  (6 shorter events, 0.0 us)
Async XLA Ops:
  0.6 3.5 %collective-permute-start.1 = (bf16[128,2048]{1,0:T(8,128)(2,1)}, bf16[128,2048]{1,0:T(8,128)(2,1)S(1)}, u32[]{:S(2)}, u32[]{:S(2)}) collective-permute-start(bf16[128,2048]{1,0:T(8,128)(2,1)} %x_own_in.1), channel_id=1, source_target_pairs={{0,1},{1,0},{2,3},{3,2},{4,5},{5,4},{6,7},{7,6},{8,9},{9,8},{10,11... | collective-permute-start | bytes 1572872 | tf_op jit(solution)/shard_map/ppermute | solution.py:392
  1.2 3.0 %collective-permute-start.2 = (bf16[128,2048]{1,0:T(8,128)(2,1)}, bf16[128,2048]{1,0:T(8,128)(2,1)}, u32[]{:S(2)}, u32[]{:S(2)}) collective-permute-start(bf16[128,2048]{1,0:T(8,128)(2,1)} %c_own_in.1), channel_id=1, source_target_pairs={{0,1},{1,0},{2,3},{3,2},{4,5},{5,4},{6,7},{7,6},{8,9},{9,8},{10,11... | collective-permute-start | bytes 1572872 | tf_op jit(solution)/shard_map/ppermute | solution.py:393
  2.8 1.3 %collective-permute-start = (bf16[4,14,512]{2,1,0:T(8,128)(2,1)S(1)}, bf16[4,14,512]{2,1,0:T(8,128)(2,1)S(1)}, u32[]{:S(2)}, u32[]{:S(2)}) collective-permute-start(bf16[4,14,512]{2,1,0:T(8,128)(2,1)S(1)} %get-tuple-element.26), channel_id=1, source_target_pairs={{0,1},{1,0},{2,3},{3,2},{4,5},{5,4},{6,7},{7,6},{8,9},{9,8},{10,11... | collective-permute-start | bytes 172040 | tf_op jit(solution)/shard_map/ppermute | solution.py:396
  4.2 0.6 copy-start.3
  4.2 0.8 %copy-start.2 = (bf16[128,2048]{1,0:T(8,128)(2,1)}, bf16[128,2048]{1,0:T(8,128)(2,1)S(1)}, u32[]{:S(2)}) copy-start(bf16[128,2048]{1,0:T(8,128)(2,1)S(1)} %collective-permute-done.1.x_other_in) | copy-start | bytes 1572868
  27.5 21.7 %all-to-all-start = ((bf16[8,2,48,256]{3,2,1,0:T(8,128)(2,1)}), bf16[8,2,48,256]{3,2,1,0:T(8,128)(2,1)S(1)}, u32[]{:S(2)}, u32[]{:S(2)}) async-start(bf16[8,2,48,256]{3,2,1,0:T(8,128)(2,1)} %bitcast.14), calls=%async_computation | async-start | bytes 786432 | tf_op jit(solution)/shard_map/all_to_all | solution.py:425
  34.7 11.7 %copy-start.1 = (bf16[512,512]{1,0:T(8,128)(2,1)S(1)}, bf16[512,512]{1,0:T(8,128)(2,1)}, u32[]{:S(2)}) copy-start(bf16[512,512]{1,0:T(8,128)(2,1)} %constant.11.clone.qt_in.qt_ref) | copy-start | bytes 1572868
  44.2 2.2 %collective-permute-start.3 = (bf16[16,2,4,16,128]{4,3,2,1,0:T(8,128)(2,1)}, bf16[16,2,4,16,128]{4,3,2,1,0:T(8,128)(2,1)S(1)}, u32[]{:S(2)}, u32[]{:S(2)}) collective-permute-start(bf16[16,2,4,16,128]{4,3,2,1,0:T(8,128)(2,1)} %get-tuple-element.19), channel_id=1, source_target_pairs={{0,1},{1,0},{2,3},{3,2},{4,5},{5,4},{6,7},{7,6},{8,9},{9,8},{10,11... | collective-permute-start | bytes 1572872 | tf_op jit(solution)/shard_map/ppermute | solution.py:445
  46.4 1.2 %copy-start = (f32[16,2,4,16,128]{4,3,2,1,0:T(8,128)S(1)}, f32[16,2,4,16,128]{4,3,2,1,0:T(8,128)}, u32[]{:S(2)}) copy-start(f32[16,2,4,16,128]{4,3,2,1,0:T(8,128)} %get-tuple-element.18.own_ref) | copy-start | bytes 3145732
  67.5 1.4 %collective-permute-start.4 = (bf16[16,16,128]{2,1,0:T(8,128)(2,1)S(1)}, bf16[16,16,128]{2,1,0:T(8,128)(2,1)S(1)}, u32[]{:S(2)}, u32[]{:S(2)}) collective-permute-start(bf16[16,16,128]{2,1,0:T(8,128)(2,1)S(1)} %get-tuple-element.25), channel_id=1, source_target_pairs={{0,1},{1,0},{2,3},{3,2},{4,5},{5,4},{6,7},{7,6},{8,9},{9,8},{10,11... | collective-permute-start | bytes 196616 | tf_op jit(solution)/shard_map/ppermute | solution.py:454

commit v4 on v3

v4 whole, which is shorter than its diff:
```python
import functools
import math

import jax
import jax.numpy as jnp
import numpy as np
from jax import lax
from jax.experimental import pallas as pl
from jax.experimental.pallas import tpu as pltpu
from jax.sharding import PartitionSpec as P

F = 8
PAIR = 2 * F
LANES = 128
ROWS = 16


def transform_tables(block):
    half = block // 2
    n = np.arange(block)
    k = np.arange(half)
    angles = ((n[:, None] * k[None, :]) % block).astype(np.float32) * np.float32(2.0 * math.pi / block)
    cosine = np.cos(angles.astype(np.float64)).astype(np.float32)
    sine = np.sin(angles.astype(np.float64)).astype(np.float32)
    parity = (1 - 2 * (n % 2)).astype(np.float32)
    norm = np.float32(1.0 / math.sqrt(block))
    forward = np.concatenate([cosine, parity[:, None], -sine[:, 1:]], axis=1) * norm
    doubling = np.where(k >= 1, 2.0, 1.0).astype(np.float32)
    inverse = np.concatenate([(cosine * doubling).T, parity[None, :], -2.0 * sine[:, 1:].T], axis=0) * norm
    order = np.arange(block).reshape(2, half // PAIR, PAIR).transpose(1, 0, 2).reshape(-1)
    extra = np.zeros((16, half), np.float32)
    inverse_cos = np.concatenate([inverse[:half, :half].T, extra], axis=0)
    inverse_cos[half] = inverse[:half, half]
    inverse_sin = inverse[half:, :half].T.copy()
    inverse_sin[:, 0] = 0.0
    forward_cos = np.concatenate([forward[:half, :half].T, extra], axis=0)
    forward_cos[half] = forward[:half, half]
    forward_sin = forward[:half, half:].T.copy()
    forward_sin[0] = 0.0
    tables = (forward.T[order], inverse.T[:, order], inverse_cos, inverse_sin, forward_cos, forward_sin)
    return [jnp.asarray(table, jnp.bfloat16) for table in tables]


def nt_dot(a, b):
    return lax.dot_general(a, b, (((1,), (1,)), ((), ())), preferred_element_type=jnp.float32)


def dot(a, b):
    return jnp.dot(a, b, preferred_element_type=jnp.float32)


def swap_blocks(tiles):
    tiles = list(tiles)
    lane_block = lax.broadcasted_iota(jnp.int32, tiles[0].shape, 1) // F
    step = len(tiles) // 2
    while step:
        high = (lane_block & step) != 0
        for i in range(len(tiles)):
            if i & step:
                continue
            low_tile, high_tile = tiles[i], tiles[i + step]
            tiles[i] = jnp.where(high, pltpu.roll(high_tile, F * step, 1), low_tile)
            tiles[i + step] = jnp.where(high, high_tile, pltpu.roll(low_tile, LANES - F * step, 1))
        step //= 2
    return tiles


def weight_rows(read, write, conj, half):
    for part in range(half // LANES):
        at = part * LANES
        tiles = swap_blocks([read(i, at) for i in range(8)] + [read(i, half + at) for i in range(8)])
        for i, tile in enumerate(tiles):
            lane = lax.broadcasted_iota(jnp.int32, tile.shape, 1)
            left = lane < LANES // 2
            turned = pltpu.roll(tile, LANES // 2, 1)
            if conj:
                real, imag = tile, jnp.where(left, -turned, turned)
            else:
                real, imag = jnp.where(left, tile, -tile), turned
            if part == 0 and i == 0:
                first = lane % F == 0
                real = jnp.where(first & ~left, 0.0, real)
                imag = jnp.where(first, jnp.where(left, 0.0, tile), imag)
            write(part * 16 + i, 0, real)
            write(part * 16 + i, 1, imag)


def adjoint_rows(read, write, half):
    for part in range(half // LANES):
        at = part * LANES
        re = swap_blocks([read(o, at) for o in range(16)])
        im = swap_blocks([read(o, half + at) for o in range(16)])
        for i in range(16):
            cross, wim = re[i], im[i]
            if part == 0 and i == 0:
                first = lax.broadcasted_iota(jnp.int32, wim.shape, 1) % F == 0
                cross = jnp.where(first, wim, cross)
                wim = jnp.where(first, 0.0, wim)
            write(part * 16 + i, 0, 0, re[i])
            write(part * 16 + i, 0, 1, wim)
            write(part * 16 + i, 1, 0, -wim)
            write(part * 16 + i, 1, 1, cross)


def diagonal():
    row = lax.broadcasted_iota(jnp.int32, (PAIR, LANES), 0)
    lane = lax.broadcasted_iota(jnp.int32, (PAIR, LANES), 1)
    return jnp.where(lane % F == row % F, 1.0, 0.0).astype(jnp.bfloat16)


def spread(read, count, mask):
    return jnp.concatenate(
        [jnp.concatenate([read(r), read(r + 1)], axis=0).astype(jnp.bfloat16) * mask for r in range(0, count, 2)], axis=0
    )


def blocks(first, second):
    zero = jnp.zeros_like(first)
    return jnp.concatenate(
        [jnp.concatenate([first, zero], axis=1), jnp.concatenate([zero, second], axis=1)], axis=0
    )


def side_by_side(values):
    return jnp.concatenate([values[..., :LANES], values[..., LANES:]], axis=-2)


def swiglu_back(gate, up, grad):
    sig = 1.0 / (1.0 + jnp.exp(-gate))
    gated = gate * sig
    return (
        (gated * up).astype(jnp.bfloat16),
        (grad * up * sig * (1.0 + gate * (1.0 - sig))).astype(jnp.bfloat16),
        (grad * gated).astype(jnp.bfloat16),
    )


def main_kernel(fb, norm, wg_in, wu_in, pt_in, x_own_in, c_own_in, wd_own_in, wd_other_in, x_other_in, c_other_in,
                qc_in, qs_in, pc_in, ps_in, d_ref, own_ref, other_ref, wg_ref, wu_ref, pt_ref, x_own, c_own, wd_ref,
                x_other, c_other, qc_ref, qs_ref, pc_ref, ps_ref, sx, sc, gs, us, hs, hid, gg, ug, rg, ru, rd, ra, rb,
                flat, part, in_sem):
    core = lax.axis_index("mp")
    db = 8
    per = db // 2
    block = pt_ref.shape[0]
    half = block // 2
    pairs = half // PAIR
    arrays = (
        (wg_in, wg_ref), (wu_in, wu_ref), (pt_in, pt_ref), (x_own_in, x_own), (c_own_in, c_own),
        (wd_own_in, wd_ref.at[pl.ds(core * per, per)]), (wd_other_in, wd_ref.at[pl.ds((1 - core) * per, per)]),
        (x_other_in, x_other), (c_other_in, c_other),
        (qc_in, qc_ref), (qs_in, qs_ref), (pc_in, pc_ref), (ps_in, ps_ref),
    )
    copies = [pltpu.make_async_copy(src, dst, in_sem.at[n]) for n, (src, dst) in enumerate(arrays)]
    for copy in copies:
        copy.start()

    def to_spectra(source, target, first):
        for j in range(0, per, 2):
            pair = jnp.concatenate(
                [source[:, j * block : (j + 1) * block], source[:, (j + 1) * block : (j + 2) * block]], axis=0
            )
            result = nt_dot(pt_ref[...], pair).reshape(pairs, 2, 2, F, 2 * LANES)
            target[:, :, :, first // 2 + j // 2] = side_by_side(result).astype(jnp.bfloat16)

    for copy in copies[:5]:
        copy.wait()
    to_spectra(x_own, sx, core * per)
    to_spectra(c_own, sc, core * per)
    for n, (source, target, adjoint) in enumerate(((wg_ref, rg, ra), (wu_ref, ru, rb))):
        for tile in range(block // LANES):
            for o in range(fb):
                flat[n, tile, o * db : (o + 1) * db] = source[o, :, tile * LANES : (tile + 1) * LANES].astype(jnp.float32)

        def read(i, at, n=n):
            return flat[n, at // LANES, pl.ds(i, fb, stride=db), :]

        def write(group, ri, rows, target=target):
            at = (group * 2 + ri) * ROWS
            target[at : at + fb, :] = rows

        weight_rows(read, write, False, half)

        def read_adjoint(o, at, n=n):
            if o >= fb:
                return jnp.zeros((db, LANES), jnp.float32)
            return flat[n, at // LANES, o * db : (o + 1) * db, :]

        def write_adjoint(group, ri, tile, rows, adjoint=adjoint):
            at = (group * 2 + ri) * db
            adjoint[tile, at : at + db, :] = rows

        adjoint_rows(read_adjoint, write_adjoint, half)

    for copy in copies[5:9]:
        copy.wait()
    to_spectra(x_other, sx, (1 - core) * per)
    to_spectra(c_other, sc, (1 - core) * per)

    def read_down(o, at):
        return wd_ref[o, :, at : at + LANES].astype(jnp.float32)

    def write_down(group, ri, rows):
        at = (group * 2 + ri) * ROWS
        rd[at : at + fb, :] = rows

    weight_rows(read_down, write_down, True, half)
    if fb < ROWS:
        for target in (gg, ug):
            target[:, :, :, fb // 2 :] = jnp.zeros((pairs, 2, 2, (ROWS - fb) // 2, PAIR, LANES), jnp.bfloat16)

    mask = diagonal()

    def both_groups(ref, g):
        return blocks(*(ref[g, :, h].reshape(LANES, LANES) for h in range(2)))

    @pl.loop(0, pairs)
    def _(g):
        for source, weights in ((sx, ((rg, gs), (ru, us))), (sc, ((rd, hs),))):
            spectrum = both_groups(source, g)
            for rows, target in weights:
                left = jnp.concatenate(
                    [
                        jnp.concatenate(
                            [
                                spread(
                                    lambda o, h=h, ri=ri, rows=rows: rows[
                                        pl.ds(((2 * g + h) * 2 + ri) * ROWS + o, F, stride=0), :
                                    ],
                                    fb,
                                    mask,
                                )
                                for h in range(2)
                            ],
                            axis=1,
                        )
                        for ri in range(2)
                    ],
                    axis=0,
                )
                result = side_by_side(dot(left, spectrum).reshape(2, fb, F, 2 * LANES)).astype(jnp.bfloat16)
                for ri in range(2):
                    target[:, g, ri] = result[ri]

    for copy in copies[9:]:
        copy.wait()
    top = lax.broadcasted_iota(jnp.int32, (F, LANES), 0)
    signed = jnp.where(top % 2 == 0, norm, -norm)

    def set_row(values, row):
        return jnp.concatenate([jnp.where(top == 0, row, values[:F]), values[F:]], axis=0)

    def add_tile(values, tile):
        return (values.reshape(-1, F, LANES) + tile[None]).reshape(values.shape)

    @pl.loop(0, fb // 2)
    def _(pair):
        sources = [(ref, 2 * pair + u) for u in range(2) for ref in (gs, us, hs)]
        re = jnp.concatenate([ref[o, :, 0].reshape(half, LANES) for ref, o in sources], axis=1)
        im = jnp.concatenate([ref[o, :, 1].reshape(half, LANES) for ref, o in sources], axis=1)
        even = dot(qc_ref[...], re)
        odd = dot(qs_ref[...], im)
        near, far = [], []
        for v in range(len(sources)):
            lanes = slice(v * LANES, (v + 1) * LANES)
            last = im[:PAIR, lanes].astype(jnp.float32)[:1]
            shared = add_tile(even[:half, lanes], last * signed)
            near.append(shared + odd[:, lanes])
            far.append(set_row(shared - odd[:, lanes], even[half : half + 1, lanes] + last * norm))
        sums, differences, middles = [], [], []
        for u in range(2):
            for a, b in zip(swiglu_back(*near[3 * u : 3 * u + 3]), swiglu_back(*far[3 * u : 3 * u + 3])):
                a, b = a.astype(jnp.float32), b.astype(jnp.float32)
                middles.append(b[:1])
                sums.append(set_row(a + b, a[:1]).astype(jnp.bfloat16))
                differences.append((a - b).astype(jnp.bfloat16))
        re = dot(pc_ref[...], jnp.concatenate(sums, axis=1))
        im = dot(ps_ref[...], jnp.concatenate(differences, axis=1))
        for v, target in enumerate((hid, gg, ug)):
            real, imag = [], []
            for u in range(2):
                at = (3 * u + v) * LANES
                middle = middles[3 * u + v]
                real.append(add_tile(re[:half, at : at + LANES], middle * signed))
                imag.append(set_row(im[:, at : at + LANES], re[half : half + 1, at : at + LANES] + middle * norm))
            for ri, two in enumerate((real, imag)):
                two = [values.reshape(pairs, 2, F, LANES) for values in two]
                target[:, ri, :, pair] = jnp.concatenate(two, axis=2).astype(jnp.bfloat16)

    lane = lax.broadcasted_iota(jnp.int32, (F, LANES), 1)
    left = lane < LANES // 2

    @pl.loop(0, pairs)
    def _(g):
        for w, (rows, cols, sign) in enumerate(((gg, sx, 1), (ug, sx, 1), (hid, sc, -1))):
            two = jnp.concatenate([rows[g, :, h, : fb // 2].reshape(2 * fb * F, LANES) for h in range(2)], axis=1)
            m = nt_dot(two, both_groups(cols, g))
            for h in range(2):
                result = []
                for upper in range(0, fb, 8):
                    sums = [jnp.zeros((F, LANES), jnp.float32)] * 2
                    for o in range(upper, min(upper + 8, fb)):
                        turn = o - upper
                        here = (top - lane) % 8 == turn
                        for q in range(2):
                            tile = m[(q * fb + o) * F : (q * fb + o + 1) * F, h * LANES : (h + 1) * LANES]
                            sums[q] = jnp.where(here, pltpu.roll(tile, turn, 0) if turn else tile, sums[q])
                    same = jnp.where(left, sums[0], sums[1])
                    cross = jnp.where(left, sums[1], sums[0])
                    turned = pltpu.roll(cross, LANES // 2, 1)
                    both = jnp.where(
                        left, same + pltpu.roll(same, LANES // 2, 1), turned - cross if sign > 0 else cross - turned
                    )
                    if h == 0:
                        both = jnp.where((lane % F == 0) & (g == 0), same, both)
                    result.append(both)
                d_ref[g, w * ROWS : (w + 1) * ROWS, h * LANES : (h + 1) * LANES] = jnp.concatenate(
                    result, axis=0
                ).astype(jnp.bfloat16)
        spectrum = jnp.concatenate([blocks(*(ref[g, :, h].reshape(2 * LANES, LANES) for h in range(2))) for ref in (gg, ug)])
        weights = jnp.concatenate(
            [
                spread(
                    lambda r, h=h, tile=tile, ref=ref: ref[
                        tile, pl.ds((2 * g + h) * 2 * db + r, F, stride=0), :
                    ],
                    2 * db,
                    mask,
                )
                for ref in (ra, rb)
                for h in range(2)
                for tile in range(2)
            ],
            axis=1,
        )
        part[...] = side_by_side(dot(weights, spectrum).reshape(2, db, F, 2 * LANES))
        for ri in range(2):
            own_ref[g, ri] = part[ri, pl.ds(core * per, per)]
            other_ref[g, ri] = part[ri, pl.ds((1 - core) * per, per)].astype(jnp.bfloat16)


def input_kernel(own_ref, got_ref, qt_ref, out_ref):
    block = qt_ref.shape[0]
    for j in range(own_ref.shape[2]):
        spectrum = (own_ref[:, :, j] + got_ref[:, :, j].astype(jnp.float32)).astype(jnp.bfloat16)
        values = dot(qt_ref[...], spectrum.reshape(block, LANES))
        out_ref[:, j * block : (j + 1) * block] = values.T.astype(jnp.bfloat16)


def reduce_kernel(r_ref, out_ref):
    total = r_ref[0].astype(jnp.float32)
    for d in range(1, r_ref.shape[0]):
        total = total + r_ref[d].astype(jnp.float32)
    total = total.astype(jnp.bfloat16)
    for d in range(out_ref.shape[0]):
        out_ref[d] = total


def straight(tile):
    halves = []
    lane = lax.broadcasted_iota(jnp.int32, (8, LANES), 1)
    for at in range(0, tile.shape[0], 8):
        half = tile[at : at + 8]
        for bit in (1, 2, 4):
            half = jnp.where((lane & bit) != 0, pltpu.roll(half, 8 - bit, 0), half)
        halves.append(half)
    return jnp.concatenate(halves, axis=0)


def entries(source, rows, part):
    tiles = []
    for i in range(16):
        lanes = slice((i % 2) * LANES, (i % 2 + 1) * LANES)
        tiles.append(straight(source[part * 8 + i // 2, rows, lanes].astype(jnp.float32)))
    return swap_blocks(tiles)


def factor(scale, part):
    lane = lax.broadcasted_iota(jnp.int32, (1, LANES), 1)
    return jnp.where((lane == 0) & (part == 0), scale, 2.0 * scale)


def layout_kernel(scale, fb, s_ref, gate_ref, up_ref, flat):
    half = s_ref.shape[0] * PAIR
    for w, target in enumerate((gate_ref, up_ref)):
        for part in range(half // LANES):
            tiles = entries(s_ref, slice(w * ROWS, (w + 1) * ROWS), part)
            for ri in range(2):
                at = ri * half + part * LANES
                for i in range(8):
                    flat[w, ri, pl.ds(i, fb, stride=8), :] = tiles[8 * ri + i][:fb] * factor(scale, part)
                target[:, at : at + LANES] = flat[w, ri]


def down_layout_kernel(scale, fb, own_ref, got_ref, down_ref):
    core = lax.axis_index("mp")
    half = own_ref.shape[0] * PAIR
    outputs = down_ref.shape[1]
    for source, h in ((own_ref, core), (got_ref, 1 - core)):
        for part in range(half // LANES):
            tiles = entries(source, slice(0, ROWS), part)
            for ri in range(2):
                at = ri * half + part * LANES
                for o in range(outputs):
                    rows = jnp.where(core == 0, tiles[8 * ri + o], tiles[8 * ri + outputs + o])
                    down_ref[pl.ds(h * fb, fb), o, at : at + LANES] = rows[:fb] * factor(scale, part)


def params(mib):
    return pltpu.CompilerParams(vmem_limit_bytes=mib << 20)


VMEM = pl.BlockSpec(memory_space=pltpu.VMEM)
HBM = pl.BlockSpec(memory_space=pltpu.HBM)


def call(kernel, out_shape, args, scratch=(), mib=16, flops=0, moved=0, in_specs=None, out_specs=None):
    return pl.pallas_call(
        kernel,
        out_shape=out_shape,
        in_specs=in_specs or [VMEM] * len(args),
        out_specs=out_specs or jax.tree.map(lambda _: VMEM, out_shape),
        scratch_shapes=list(scratch),
        compiler_params=params(mib),
        cost_estimate=pl.CostEstimate(flops=flops, bytes_accessed=moved, transcendentals=0),
    )(*args)


def shards(tokens, cotangent, gate_spectra, up_spectra, down_spectra):
    n_dp = lax.axis_size("dp")
    core = lax.axis_index("mp")
    swap = [(0, 1), (1, 0)]
    fb, db, block = gate_spectra.shape
    assert db == 8 and fb <= ROWS and fb % 2 == 0 and tokens.shape[0] == LANES and lax.axis_size("mp") == 2
    half = block // 2
    pairs = half // PAIR
    groups = half // F
    per = db // 2
    bf16, f32 = jnp.bfloat16, jnp.float32
    shape = jax.ShapeDtypeStruct
    pt, qt, qc, qs, pc, ps = transform_tables(block)
    norm = float(np.asarray(1.0 / math.sqrt(block), jnp.bfloat16))

    tokens_other = lax.ppermute(tokens, "mp", swap)
    cotangent_other = lax.ppermute(cotangent, "mp", swap)
    down = down_spectra.reshape(per, 2, fb, block)
    down_own = jnp.where(core == 0, down[:, 0], down[:, 1])
    down_got = lax.ppermute(jnp.where(core == 0, down[:, 1], down[:, 0]), "mp", swap)

    inputs = (
        gate_spectra, up_spectra, pt, tokens, cotangent, down_own, down_got, tokens_other, cotangent_other, qc, qs, pc, ps
    )
    buffers = [shape((db, fb, block), bf16) if n == 5 else a for n, a in enumerate(inputs) if n != 6]
    d_all, own, other = call(
        functools.partial(main_kernel, fb, norm),
        (
            shape((pairs, 3 * ROWS, 2 * LANES), bf16),
            shape((pairs, 2, per, PAIR, LANES), f32),
            shape((pairs, 2, per, PAIR, LANES), bf16),
        ),
        inputs,
        [pltpu.VMEM(a.shape, bf16) for a in buffers]
        + [pltpu.VMEM((pairs, 2, 2, db // 2, PAIR, LANES), bf16)] * 2
        + [pltpu.VMEM((fb, pairs, 2, PAIR, LANES), bf16)] * 3
        + [pltpu.VMEM((pairs, 2, 2, ROWS // 2, PAIR, LANES), bf16)] * 3
        + [pltpu.VMEM((groups * 2 * ROWS, LANES), f32)] * 3
        + [pltpu.VMEM((2, groups * 2 * db, LANES), f32)] * 2
        + [pltpu.VMEM((2, block // LANES, fb * db, LANES), f32), pltpu.VMEM((2, db, PAIR, LANES), f32)]
        + [pltpu.SemaphoreType.DMA((len(inputs),))],
        mib=63,
        flops=10**10,
        moved=10**7,
        in_specs=[HBM] * len(inputs),
    )

    direct = pairs % n_dp == 0
    if direct:
        share = pairs // n_dp
        got = lax.all_to_all(d_all.reshape(n_dp, share, 3 * ROWS, 2 * LANES), "dp", 0, 0, tiled=True)
    else:
        share = pairs
        got = lax.psum(d_all.astype(f32), "dp")[None]
    partner = lax.ppermute(other, "mp", swap)
    grad_tokens = call(
        input_kernel, shape(tokens.shape, bf16), (own, partner, qt), flops=5 * 10**8, moved=4 * 10**6
    )

    total = call(reduce_kernel, shape((n_dp if direct else 1, share, 3 * ROWS, 2 * LANES), bf16), (got,), moved=10**6)
    total, grad_tokens = lax.optimization_barrier((total, grad_tokens))
    if direct:
        total = lax.all_to_all(total, "dp", 0, 0, tiled=True)
    total = total.reshape(pairs, 3 * ROWS, 2 * LANES)
    down_sums = total[:, 2 * ROWS :]
    partner_sums = lax.ppermute(down_sums, "mp", swap)
    scale = 1.0 / math.sqrt(tokens.shape[0] * n_dp)
    gate_grad, up_grad = call(
        functools.partial(layout_kernel, scale, fb),
        (shape((fb * db, block), f32),) * 2,
        (total,),
        [pltpu.VMEM((2, 2, fb * db, LANES), f32)],
        moved=10**6,
    )
    down_grad = call(
        functools.partial(down_layout_kernel, scale, fb),
        shape((2 * fb, per, block), f32),
        (down_sums, partner_sums),
        moved=10**6,
    ).transpose(1, 0, 2)
    return (grad_tokens, gate_grad.reshape(fb, db, block), up_grad.reshape(fb, db, block), down_grad)


def solution(mesh):
    in_specs = (
        P(("groups", "dp"), "mp"),
        P(("groups", "dp"), "mp"),
        P("mp", None, None),
        P("mp", None, None),
        P("mp", None, None),
    )
    out_specs = (
        P(("groups", "dp"), "mp"),
        P(("groups", "mp"), None, None),
        P(("groups", "mp"), None, None),
        P(("groups", "mp"), None, None),
    )
    return jax.shard_map(shards, mesh=mesh, in_specs=in_specs, out_specs=out_specs, check_vma=False)
```

time: 70.3 us -> 67.7 us (0.963)
  Pallas kernels: 36.1 us -> 28.9 us
  waiting for transfers between devices: 3.02 us -> 10 us
  blocking collectives: 18.1 us -> 15.7 us
    pallas_call x7 -> x5, Pallas kernels: 36.1 us -> 28.9 us  [call(): pl.pallas_call(kernel, out_shape=out_shape, in_specs=in_specs or [VMEM] *...]
    all_to_all x1, waiting for transfers between devices: 0.01 us -> 7 us  [shards(): lax.all_to_all(d_all.reshape(n_dp, share, 3 * ROWS, 2 * LANES), 'dp', 0,...]
    all_to_all x1, blocking collectives: 18.1 us -> 15.7 us  [shards(): total = lax.all_to_all(total, 'dp', 0, 0, tiled=True)]
  transfers between devices with their start and end apart: 6 -> 6, of which waited for: 2 -> 3; matrix products, arithmetic and copies ran while one was open for 2% -> 2% of each run, Pallas kernels for 18% -> 4%
where the time goes in v4:
time: 67.7 us; the launch traced here: 67.3 us
  Pallas kernels  28.9 us (43%)
  blocking collectives  15.7 us (23%)
  waiting for transfers between devices  10 us (15%)
  starting transfers between devices  8.46 us (12%)
  local copies, waits for them, and re-layouts  2.93 us (4%)
  between operations  0.68 us (1%)
    pallas_call x5, Pallas kernels, call(): pl.pallas_call(kernel, out_shape=out_shape, in_specs=in_specs or [VMEM] *...  28.9 us
    all_to_all x1, blocking collectives, shards(): total = lax.all_to_all(total, 'dp', 0, 0, tiled=True)  15.7 us
    all_to_all x1, starting transfers between devices, shards(): lax.all_to_all(d_all.reshape(n_dp, share, 3 * ROWS, 2 * LANES), 'dp', 0,...  7.31 us
    all_to_all x1, waiting for transfers between devices, shards(): lax.all_to_all(d_all.reshape(n_dp, share, 3 * ROWS, 2 * LANES), 'dp', 0,...  7 us
    ppermute x1, waiting for transfers between devices, shards(): partner = lax.ppermute(other, 'mp', swap)  2.11 us
    unnamed x8, local copies, waits for them, and re-layouts  2.04 us
  transfers between devices with their start and end apart: 6, of which 3 were waited for; matrix products, arithmetic and copies ran while one was open for 2% of the time, Pallas kernels for 4%

profile of v4, /device:TPU:0, one launch (start us, length us, event | category | flops | bytes accessed | tf_op | source)
XLA Modules:
  0.0 67.3 jit_solution(6239626543500047209)
XLA Ops:
  0.6 0.6 collective-permute-start.1
  1.2 0.1 collective-permute-start.2
  1.3 0.9 %fusion = (bf16[4,1,14,512]{3,0,2,1:T(4,128)(2,1)S(1)}, bf16[4,1,14,512]{3,0,2,1:T(4,128)(2,1)S(1)}) fusion(bf16[4,2,14,512]{3,0,2,1:T(4,128)(2,1)} %bitcast.14), kind=kLoop, calls=%fused_computation.2 | loop fusion | bytes 229376 | tf_op jit(solution)/shard_map/slice | solution.py:447
  2.2 0.7 select_bitcast_fusion
  2.8 0.4 collective-permute-start
  3.2 0.9 %collective-permute-done.wd_other_in = bf16[4,14,512]{2,1,0:T(8,128)(2,1)S(1)} collective-permute-done((bf16[4,14,512]{2,1,0:T(8,128)(2,1)S(1)}, bf16[4,14,512]{2,1,0:T(8,128)(2,1)S(1)}, u32[]{:S(2)}, u32[]{:S(2)}) %collective-permute-start) | collective-permute-done | bytes 57376 | tf_op jit(solution)/shard_map/ppermute | solution.py:448
  4.2 0.0 collective-permute-done.1.x_other_in
  4.2 0.0 collective-permute-done.2.c_other_in
  4.2 0.6 copy-done.3
  4.8 0.2 copy-done.2
  5.0 24.4 %shard_map.138 = (bf16[16,48,256]{2,1,0:T(8,128)(2,1)}, f32[16,2,4,16,128]{4,3,2,1,0:T(8,128)}, bf16[16,2,4,16,128]{4,3,2,1,0:T(8,128)(2,1)}) custom-call(bf16[14,8,512]{2,1,0:T(8,128)(2,1)} %wg_in.1, bf16[14,8,512]{2,1,0:T(8,128)(2,1)} %wu_in.1, bf16[512,512]{1,0:T(8,128)(2,1)} %constant.18.clone.pt_in, bf16[128,2048]{1,0:T(8,128)(2,1)} %x_own_in.1, ...), custom_call_target="tpu_custom_call" | custom-call | flops 10000000000 | bytes 10000000 | tf_op jit(solution)/shard_map/pallas_call | solution.py:418
  29.4 0.0 copy-start.1
  29.4 7.3 %all-to-all-start = ((bf16[8,2,48,256]{3,2,1,0:T(8,128)(2,1)}), bf16[8,2,48,256]{3,2,1,0:T(8,128)(2,1)S(1)}, u32[]{:S(2)}, u32[]{:S(2)}) async-start(bf16[8,2,48,256]{3,2,1,0:T(8,128)(2,1)} %bitcast.12), calls=%async_computation | async-start | bytes 786432 | tf_op jit(solution)/shard_map/all_to_all | solution.py:479
  36.7 0.0 collective-permute-start.3
  36.7 2.1 %collective-permute-done.3.got_ref = bf16[16,2,4,16,128]{4,3,2,1,0:T(8,128)(2,1)S(1)} collective-permute-done((bf16[16,2,4,16,128]{4,3,2,1,0:T(8,128)(2,1)}, bf16[16,2,4,16,128]{4,3,2,1,0:T(8,128)(2,1)S(1)}, u32[]{:S(2)}, u32[]{:S(2)}) %collective-permute-start.3) | collective-permute-done | bytes 524320 | tf_op jit(solution)/shard_map/ppermute | solution.py:483
  38.8 1.2 %copy-done = f32[16,2,4,16,128]{4,3,2,1,0:T(8,128)S(1)} copy-done((f32[16,2,4,16,128]{4,3,2,1,0:T(8,128)S(1)}, f32[16,2,4,16,128]{4,3,2,1,0:T(8,128)}, u32[]{:S(2)}) %copy-start) | copy-done | bytes 1048600
  40.0 1.6 %shard_map.140 = bf16[128,2048]{1,0:T(8,128)(2,1)} custom-call(f32[16,2,4,16,128]{4,3,2,1,0:T(8,128)S(1)} %copy-done, bf16[16,2,4,16,128]{4,3,2,1,0:T(8,128)(2,1)S(1)} %collective-permute-done.3.got_ref, bf16[512,512]{1,0:T(8,128)(2,1)S(1)} %copy-done.1), custom_call_target="tpu_custom_call" | custom-call | flops 500000000 | bytes 4000000 | tf_op jit(solution)/shard_map/pallas_call | solution.py:418
  41.7 7.0 %all-to-all-done.r_ref = bf16[8,2,48,256]{3,2,1,0:T(8,128)(2,1)S(1)} async-done(((bf16[8,2,48,256]{3,2,1,0:T(8,128)(2,1)}), bf16[8,2,48,256]{3,2,1,0:T(8,128)(2,1)S(1)}, u32[]{:S(2)}, u32[]{:S(2)}) %all-to-all-start) | async-done | bytes 393248 | tf_op jit(solution)/shard_map/all_to_all | solution.py:479
  48.7 0.1 shard_map.139
  48.7 15.7 %all_to_all.10 = bf16[8,2,48,256]{3,2,1,0:T(8,128)(2,1)S(1)} all-to-all(bf16[8,2,48,256]{3,2,1,0:T(8,128)(2,1)S(1)} %shard_map.139), channel_id=1, replica_groups=mesh['groups'=2,'dp'=8,'mp'=2] {'dp'}, dimensions={0} | all-to-all | bytes 786432 | tf_op jit(solution)/shard_map/all_to_all | solution.py:491
  64.4 0.1 collective-permute-start.4
  64.5 1.4 %shard_map.141 = (f32[112,512]{1,0:T(8,128)}, f32[112,512]{1,0:T(8,128)}) custom-call(bf16[16,48,256]{2,1,0:T(8,128)(2,1)S(1)} %bitcast.11), custom_call_target="tpu_custom_call" | custom-call | bytes 1000000 | tf_op jit(solution)/shard_map/pallas_call | solution.py:418
  65.9 0.0 collective-permute-done.4.got_ref
  65.9 1.4 %shard_map.142 = f32[28,4,512]{2,1,0:T(4,128)} custom-call(bf16[16,16,256]{2,1,0:T(8,128)(2,1)S(1)} %slice.16.own_ref, bf16[16,16,256]{2,1,0:T(8,128)(2,1)S(1)} %collective-permute-done.4.got_ref), custom_call_target="tpu_custom_call" | custom-call | bytes 1000000 | tf_op jit(solution)/shard_map/pallas_call | solution.py:418
  (5 shorter events, 0.0 us)
Async XLA Ops:
  0.6 3.5 %collective-permute-start.1 = (bf16[128,2048]{1,0:T(8,128)(2,1)}, bf16[128,2048]{1,0:T(8,128)(2,1)S(1)}, u32[]{:S(2)}, u32[]{:S(2)}) collective-permute-start(bf16[128,2048]{1,0:T(8,128)(2,1)} %x_own_in.1), channel_id=1, source_target_pairs={{0,1},{1,0},{2,3},{3,2},{4,5},{5,4},{6,7},{7,6},{8,9},{9,8},{10,11... | collective-permute-start | bytes 1572872 | tf_op jit(solution)/shard_map/ppermute | solution.py:444
  1.2 3.0 %collective-permute-start.2 = (bf16[128,2048]{1,0:T(8,128)(2,1)}, bf16[128,2048]{1,0:T(8,128)(2,1)}, u32[]{:S(2)}, u32[]{:S(2)}) collective-permute-start(bf16[128,2048]{1,0:T(8,128)(2,1)} %c_own_in.1), channel_id=1, source_target_pairs={{0,1},{1,0},{2,3},{3,2},{4,5},{5,4},{6,7},{7,6},{8,9},{9,8},{10,11... | collective-permute-start | bytes 1572872 | tf_op jit(solution)/shard_map/ppermute | solution.py:445
  2.8 1.3 %collective-permute-start = (bf16[4,14,512]{2,1,0:T(8,128)(2,1)S(1)}, bf16[4,14,512]{2,1,0:T(8,128)(2,1)S(1)}, u32[]{:S(2)}, u32[]{:S(2)}) collective-permute-start(bf16[4,14,512]{2,1,0:T(8,128)(2,1)S(1)} %get-tuple-element.18), channel_id=1, source_target_pairs={{0,1},{1,0},{2,3},{3,2},{4,5},{5,4},{6,7},{7,6},{8,9},{9,8},{10,11... | collective-permute-start | bytes 172040 | tf_op jit(solution)/shard_map/ppermute | solution.py:448
  4.2 0.6 copy-start.3
  4.2 0.8 %copy-start.2 = (bf16[128,2048]{1,0:T(8,128)(2,1)}, bf16[128,2048]{1,0:T(8,128)(2,1)S(1)}, u32[]{:S(2)}) copy-start(bf16[128,2048]{1,0:T(8,128)(2,1)S(1)} %collective-permute-done.1.x_other_in) | copy-start | bytes 1572868
  29.4 9.5 %copy-start.1 = (bf16[512,512]{1,0:T(8,128)(2,1)S(1)}, bf16[512,512]{1,0:T(8,128)(2,1)}, u32[]{:S(2)}) copy-start(bf16[512,512]{1,0:T(8,128)(2,1)} %constant.19.clone.qt_ref) | copy-start | bytes 1572868
  29.4 19.3 %all-to-all-start = ((bf16[8,2,48,256]{3,2,1,0:T(8,128)(2,1)}), bf16[8,2,48,256]{3,2,1,0:T(8,128)(2,1)S(1)}, u32[]{:S(2)}, u32[]{:S(2)}) async-start(bf16[8,2,48,256]{3,2,1,0:T(8,128)(2,1)} %bitcast.12), calls=%async_computation | async-start | bytes 786432 | tf_op jit(solution)/shard_map/all_to_all | solution.py:479
  36.7 2.1 %collective-permute-start.3 = (bf16[16,2,4,16,128]{4,3,2,1,0:T(8,128)(2,1)}, bf16[16,2,4,16,128]{4,3,2,1,0:T(8,128)(2,1)S(1)}, u32[]{:S(2)}, u32[]{:S(2)}) collective-permute-start(bf16[16,2,4,16,128]{4,3,2,1,0:T(8,128)(2,1)} %get-tuple-element.13), channel_id=1, source_target_pairs={{0,1},{1,0},{2,3},{3,2},{4,5},{5,4},{6,7},{7,6},{8,9},{9,8},{10,11... | collective-permute-start | bytes 1572872 | tf_op jit(solution)/shard_map/ppermute | solution.py:483
  38.8 1.2 %copy-start = (f32[16,2,4,16,128]{4,3,2,1,0:T(8,128)S(1)}, f32[16,2,4,16,128]{4,3,2,1,0:T(8,128)}, u32[]{:S(2)}) copy-start(f32[16,2,4,16,128]{4,3,2,1,0:T(8,128)} %get-tuple-element.12.own_ref) | copy-start | bytes 3145732
  64.4 1.5 %collective-permute-start.4 = (bf16[16,16,256]{2,1,0:T(8,128)(2,1)S(1)}, bf16[16,16,256]{2,1,0:T(8,128)(2,1)S(1)}, u32[]{:S(2)}, u32[]{:S(2)}) collective-permute-start(bf16[16,16,256]{2,1,0:T(8,128)(2,1)S(1)} %slice.16.own_ref), channel_id=1, source_target_pairs={{0,1},{1,0},{2,3},{3,2},{4,5},{5,4},{6,7},{7,6},{8,9},{9,8},{10,11... | collective-permute-start | bytes 393224 | tf_op jit(solution)/shard_map/ppermute | solution.py:494

commit v5 on v4

--- a/solution.py
+++ b/solution.py
@@ -29,15 +29,13 @@
     inverse = np.concatenate([(cosine * doubling).T, parity[None, :], -2.0 * sine[:, 1:].T], axis=0) * norm
     order = np.arange(block).reshape(2, half // PAIR, PAIR).transpose(1, 0, 2).reshape(-1)
     extra = np.zeros((16, half), np.float32)
-    inverse_cos = np.concatenate([inverse[:half, :half].T, extra], axis=0)
-    inverse_cos[half] = inverse[:half, half]
-    inverse_sin = inverse[half:, :half].T.copy()
-    inverse_sin[:, 0] = 0.0
+    folded = np.concatenate([np.arange(half), [half], np.arange(block - 1, half, -1)])
     forward_cos = np.concatenate([forward[:half, :half].T, extra], axis=0)
     forward_cos[half] = forward[:half, half]
     forward_sin = forward[:half, half:].T.copy()
     forward_sin[0] = 0.0
-    tables = (forward.T[order], inverse.T[:, order], inverse_cos, inverse_sin, forward_cos, forward_sin)
+    natural = inverse.T[:, order]
+    tables = (forward.T[order], natural, natural[folded], forward_cos, forward_sin)
     return [jnp.asarray(table, jnp.bfloat16) for table in tables]
 
 
@@ -128,17 +126,18 @@
 def swiglu_back(gate, up, grad):
     sig = 1.0 / (1.0 + jnp.exp(-gate))
     gated = gate * sig
+    slope = sig + gated * (1.0 - sig)
     return (
         (gated * up).astype(jnp.bfloat16),
-        (grad * up * sig * (1.0 + gate * (1.0 - sig))).astype(jnp.bfloat16),
+        (grad * up * slope).astype(jnp.bfloat16),
         (grad * gated).astype(jnp.bfloat16),
     )
 
 
 def main_kernel(fb, norm, wg_in, wu_in, pt_in, x_own_in, c_own_in, wd_own_in, wd_other_in, x_other_in, c_other_in,
-                qc_in, qs_in, pc_in, ps_in, d_ref, own_ref, other_ref, wg_ref, wu_ref, pt_ref, x_own, c_own, wd_ref,
-                x_other, c_other, qc_ref, qs_ref, pc_ref, ps_ref, sx, sc, gs, us, hs, hid, gg, ug, rg, ru, rd, ra, rb,
-                flat, part, in_sem):
+                qf_in, pc_in, ps_in, d_ref, gg_out, ug_out, wg_ref, wu_ref, pt_ref, x_own, c_own, wd_ref,
+                x_other, c_other, qf_ref, pc_ref, ps_ref, sx, sc, gs, us, hs, hid, gg, ug, rg, ru, rd,
+                sums_ref, diffs_ref, mids_ref, flat, in_sem, out_sem):
     core = lax.axis_index("mp")
     db = 8
     per = db // 2
@@ -149,25 +148,24 @@
         (wg_in, wg_ref), (wu_in, wu_ref), (pt_in, pt_ref), (x_own_in, x_own), (c_own_in, c_own),
         (wd_own_in, wd_ref.at[pl.ds(core * per, per)]), (wd_other_in, wd_ref.at[pl.ds((1 - core) * per, per)]),
         (x_other_in, x_other), (c_other_in, c_other),
-        (qc_in, qc_ref), (qs_in, qs_ref), (pc_in, pc_ref), (ps_in, ps_ref),
+        (qf_in, qf_ref), (pc_in, pc_ref), (ps_in, ps_ref),
     )
     copies = [pltpu.make_async_copy(src, dst, in_sem.at[n]) for n, (src, dst) in enumerate(arrays)]
     for copy in copies:
         copy.start()
 
     def to_spectra(source, target, first):
+        rows = jnp.concatenate([source[:, j * block : (j + 1) * block] for j in range(per)], axis=0)
+        result = nt_dot(pt_ref[...], rows).reshape(pairs, 2, 2, F, per * LANES)
         for j in range(0, per, 2):
-            pair = jnp.concatenate(
-                [source[:, j * block : (j + 1) * block], source[:, (j + 1) * block : (j + 2) * block]], axis=0
-            )
-            result = nt_dot(pt_ref[...], pair).reshape(pairs, 2, 2, F, 2 * LANES)
-            target[:, :, :, first // 2 + j // 2] = side_by_side(result).astype(jnp.bfloat16)
+            two = side_by_side(result[..., j * LANES : (j + 2) * LANES])
+            target[:, :, :, first // 2 + j // 2] = two.astype(jnp.bfloat16)
 
     for copy in copies[:5]:
         copy.wait()
     to_spectra(x_own, sx, core * per)
     to_spectra(c_own, sc, core * per)
-    for n, (source, target, adjoint) in enumerate(((wg_ref, rg, ra), (wu_ref, ru, rb))):
+    for n, (source, target) in enumerate(((wg_ref, rg), (wu_ref, ru))):
         for tile in range(block // LANES):
             for o in range(fb):
                 flat[n, tile, o * db : (o + 1) * db] = source[o, :, tile * LANES : (tile + 1) * LANES].astype(jnp.float32)
@@ -180,17 +178,6 @@
             target[at : at + fb, :] = rows
 
         weight_rows(read, write, False, half)
-
-        def read_adjoint(o, at, n=n):
-            if o >= fb:
-                return jnp.zeros((db, LANES), jnp.float32)
-            return flat[n, at // LANES, o * db : (o + 1) * db, :]
-
-        def write_adjoint(group, ri, tile, rows, adjoint=adjoint):
-            at = (group * 2 + ri) * db
-            adjoint[tile, at : at + db, :] = rows
-
-        adjoint_rows(read_adjoint, write_adjoint, half)
 
     for copy in copies[5:9]:
         copy.wait()
@@ -214,12 +201,11 @@
     def both_groups(ref, g):
         return blocks(*(ref[g, :, h].reshape(LANES, LANES) for h in range(2)))
 
-    @pl.loop(0, pairs)
-    def _(g):
+    def mix(g):
         for source, weights in ((sx, ((rg, gs), (ru, us))), (sc, ((rd, hs),))):
             spectrum = both_groups(source, g)
             for rows, target in weights:
-                left = jnp.concatenate(
+                wide = jnp.concatenate(
                     [
                         jnp.concatenate(
                             [
@@ -238,60 +224,78 @@
                     ],
                     axis=0,
                 )
-                result = side_by_side(dot(left, spectrum).reshape(2, fb, F, 2 * LANES)).astype(jnp.bfloat16)
+                result = side_by_side(dot(wide, spectrum).reshape(2, fb, F, 2 * LANES)).astype(jnp.bfloat16)
                 for ri in range(2):
                     target[:, g, ri] = result[ri]
+
+    @pl.loop(0, pairs // 4)
+    def _(n):
+        for u in range(4):
+            mix(4 * n + u)
 
     for copy in copies[9:]:
         copy.wait()
     top = lax.broadcasted_iota(jnp.int32, (F, LANES), 0)
-    signed = jnp.where(top % 2 == 0, norm, -norm)
+    wide_top = lax.broadcasted_iota(jnp.int32, (F, 2 * LANES), 0)
+    signed = jnp.where(wide_top % 2 == 0, norm, -norm)
+    inner = jnp.where(lax.broadcasted_iota(jnp.int32, (PAIR, 2 * LANES), 0) == 0, 0.0, 1.0).astype(jnp.bfloat16)
 
     def set_row(values, row):
-        return jnp.concatenate([jnp.where(top == 0, row, values[:F]), values[F:]], axis=0)
+        return jnp.concatenate([jnp.where(wide_top == 0, row, values[:F]), values[F:]], axis=0)
 
     def add_tile(values, tile):
-        return (values.reshape(-1, F, LANES) + tile[None]).reshape(values.shape)
-
-    @pl.loop(0, fb // 2)
-    def _(pair):
-        sources = [(ref, 2 * pair + u) for u in range(2) for ref in (gs, us, hs)]
-        re = jnp.concatenate([ref[o, :, 0].reshape(half, LANES) for ref, o in sources], axis=1)
-        im = jnp.concatenate([ref[o, :, 1].reshape(half, LANES) for ref, o in sources], axis=1)
-        even = dot(qc_ref[...], re)
-        odd = dot(qs_ref[...], im)
-        near, far = [], []
-        for v in range(len(sources)):
-            lanes = slice(v * LANES, (v + 1) * LANES)
-            last = im[:PAIR, lanes].astype(jnp.float32)[:1]
-            shared = add_tile(even[:half, lanes], last * signed)
-            near.append(shared + odd[:, lanes])
-            far.append(set_row(shared - odd[:, lanes], even[half : half + 1, lanes] + last * norm))
-        sums, differences, middles = [], [], []
+        return (values.reshape(-1, F, 2 * LANES) + tile[None]).reshape(values.shape)
+
+    def to_values(pair):
+        spectra = jnp.concatenate(
+            [ref[2 * pair + u].reshape(block, LANES) for ref in (gs, us, hs) for u in range(2)], axis=1
+        )
+        return dot(qf_ref[...], spectra)
+
+    def to_grads(values, slot):
+        gate, up, grad = (values[:, v * 2 * LANES : (v + 1) * 2 * LANES] for v in range(3))
+        for v, side in enumerate(swiglu_back(gate, up, grad)):
+            near, far = side[:half], side[half:]
+            mids_ref[slot, v] = far[:PAIR].astype(jnp.float32)[:F]
+            sums_ref[slot, v, :PAIR] = near[:PAIR] + far[:PAIR] * inner
+            sums_ref[slot, v, PAIR:] = near[PAIR:] + far[PAIR:]
+            diffs_ref[slot, v] = near - far
+
+    def to_grad_spectra(pair, slot):
+        re = dot(pc_ref[...], jnp.concatenate([sums_ref[slot, v] for v in range(3)], axis=1))
+        im = dot(ps_ref[...], jnp.concatenate([diffs_ref[slot, v] for v in range(3)], axis=1))
+        for v, target in enumerate((hid, gg, ug)):
+            lanes = slice(v * 2 * LANES, (v + 1) * 2 * LANES)
+            middle = mids_ref[slot, v][:1]
+            real = add_tile(re[:half, lanes], middle * signed)
+            imag = set_row(im[:, lanes], re[half : half + 1, lanes] + middle * norm)
+            for ri, both in enumerate((real, imag)):
+                target[:, ri, :, pair] = side_by_side(both.reshape(pairs, 2, F, 2 * LANES)).astype(jnp.bfloat16)
+
+    steps = fb // 2
+    to_grads(to_values(0), 0)
+
+    @pl.loop(0, (steps - 1) // 2)
+    def _(n):
         for u in range(2):
-            for a, b in zip(swiglu_back(*near[3 * u : 3 * u + 3]), swiglu_back(*far[3 * u : 3 * u + 3])):
-                a, b = a.astype(jnp.float32), b.astype(jnp.float32)
-                middles.append(b[:1])
-                sums.append(set_row(a + b, a[:1]).astype(jnp.bfloat16))
-                differences.append((a - b).astype(jnp.bfloat16))
-        re = dot(pc_ref[...], jnp.concatenate(sums, axis=1))
-        im = dot(ps_ref[...], jnp.concatenate(differences, axis=1))
-        for v, target in enumerate((hid, gg, ug)):
-            real, imag = [], []
-            for u in range(2):
-                at = (3 * u + v) * LANES
-                middle = middles[3 * u + v]
-                real.append(add_tile(re[:half, at : at + LANES], middle * signed))
-                imag.append(set_row(im[:, at : at + LANES], re[half : half + 1, at : at + LANES] + middle * norm))
-            for ri, two in enumerate((real, imag)):
-                two = [values.reshape(pairs, 2, F, LANES) for values in two]
-                target[:, ri, :, pair] = jnp.concatenate(two, axis=2).astype(jnp.bfloat16)
-
+            values = to_values(2 * n + u + 1)
+            to_grad_spectra(2 * n + u, u)
+            to_grads(values, 1 - u)
+
+    if steps % 2 == 0:
+        to_grad_spectra(steps - 2, 0)
+        to_grads(to_values(steps - 1), 1)
+    to_grad_spectra(steps - 1, 1 - steps % 2)
+
+    stores = [
+        pltpu.make_async_copy(src, dst, out_sem.at[n]) for n, (src, dst) in enumerate(((gg, gg_out), (ug, ug_out)))
+    ]
+    for copy in stores:
+        copy.start()
     lane = lax.broadcasted_iota(jnp.int32, (F, LANES), 1)
     left = lane < LANES // 2
 
-    @pl.loop(0, pairs)
-    def _(g):
+    def weight_sums(g):
         for w, (rows, cols, sign) in enumerate(((gg, sx, 1), (ug, sx, 1), (hid, sc, -1))):
             two = jnp.concatenate([rows[g, :, h, : fb // 2].reshape(2 * fb * F, LANES) for h in range(2)], axis=1)
             m = nt_dot(two, both_groups(cols, g))
@@ -317,13 +321,59 @@
                 d_ref[g, w * ROWS : (w + 1) * ROWS, h * LANES : (h + 1) * LANES] = jnp.concatenate(
                     result, axis=0
                 ).astype(jnp.bfloat16)
+
+    @pl.loop(0, pairs // 4)
+    def _(n):
+        for u in range(4):
+            weight_sums(4 * n + u)
+
+    for copy in stores:
+        copy.wait()
+
+
+def adjoint_kernel(fb, wg_in, wu_in, gg_in, ug_in, own_ref, other_ref, wg_ref, wu_ref, gg, ug, ra, rb, part, in_sem,
+                   g_sem):
+    core = lax.axis_index("mp")
+    db = 8
+    per = db // 2
+    pairs = gg.shape[0]
+    half = pairs * PAIR
+    weights = [
+        pltpu.make_async_copy(src, dst, in_sem.at[n]) for n, (src, dst) in enumerate(((wg_in, wg_ref), (wu_in, wu_ref)))
+    ]
+
+    def group_copies(g):
+        return [
+            pltpu.make_async_copy(src.at[g], dst.at[g], g_sem.at[n, g])
+            for n, (src, dst) in enumerate(((gg_in, gg), (ug_in, ug)))
+        ]
+
+    for copy in weights:
+        copy.start()
+    for g in range(pairs):
+        for copy in group_copies(g):
+            copy.start()
+    for copy in weights:
+        copy.wait()
+    for source, adjoint in ((wg_ref, ra), (wu_ref, rb)):
+        def read(o, at, source=source):
+            if o >= fb:
+                return jnp.zeros((db, LANES), jnp.float32)
+            return source[o, :, at : at + LANES].astype(jnp.float32)
+
+        def write(group, ri, tile, rows, adjoint=adjoint):
+            at = (group * 2 + ri) * db
+            adjoint[tile, at : at + db, :] = rows
+
+        adjoint_rows(read, write, half)
+    mask = diagonal()
+
+    def mix(g, slot):
         spectrum = jnp.concatenate([blocks(*(ref[g, :, h].reshape(2 * LANES, LANES) for h in range(2))) for ref in (gg, ug)])
-        weights = jnp.concatenate(
+        wide = jnp.concatenate(
             [
                 spread(
-                    lambda r, h=h, tile=tile, ref=ref: ref[
-                        tile, pl.ds((2 * g + h) * 2 * db + r, F, stride=0), :
-                    ],
+                    lambda r, h=h, tile=tile, ref=ref: ref[tile, pl.ds((2 * g + h) * 2 * db + r, F, stride=0), :],
                     2 * db,
                     mask,
                 )
@@ -333,10 +383,18 @@
             ],
             axis=1,
         )
-        part[...] = side_by_side(dot(weights, spectrum).reshape(2, db, F, 2 * LANES))
+        part[slot] = side_by_side(dot(wide, spectrum).reshape(2, db, F, 2 * LANES))
         for ri in range(2):
-            own_ref[g, ri] = part[ri, pl.ds(core * per, per)]
-            other_ref[g, ri] = part[ri, pl.ds((1 - core) * per, per)].astype(jnp.bfloat16)
+            own_ref[g, ri] = part[slot, ri, pl.ds(core * per, per)]
+            other_ref[g, ri] = part[slot, ri, pl.ds((1 - core) * per, per)].astype(jnp.bfloat16)
+
+    @pl.loop(0, pairs // 2)
+    def _(n):
+        for u in range(2):
+            for copy in group_copies(2 * n + u):
+                copy.wait()
+        for u in range(2):
+            mix(2 * n + u, u)
 
 
 def input_kernel(own_ref, got_ref, qt_ref, out_ref):
@@ -345,15 +403,6 @@
         spectrum = (own_ref[:, :, j] + got_ref[:, :, j].astype(jnp.float32)).astype(jnp.bfloat16)
         values = dot(qt_ref[...], spectrum.reshape(block, LANES))
         out_ref[:, j * block : (j + 1) * block] = values.T.astype(jnp.bfloat16)
-
-
-def reduce_kernel(r_ref, out_ref):
-    total = r_ref[0].astype(jnp.float32)
-    for d in range(1, r_ref.shape[0]):
-        total = total + r_ref[d].astype(jnp.float32)
-    total = total.astype(jnp.bfloat16)
-    for d in range(out_ref.shape[0]):
-        out_ref[d] = total
 
 
 def straight(tile):
@@ -367,11 +416,22 @@
     return jnp.concatenate(halves, axis=0)
 
 
+def reduce_kernel(r_ref, out_ref):
+    for g in range(r_ref.shape[1]):
+        for lanes in (slice(0, LANES), slice(LANES, 2 * LANES)):
+            total = r_ref[0, g, :, lanes].astype(jnp.float32)
+            for d in range(1, r_ref.shape[0]):
+                total = total + r_ref[d, g, :, lanes].astype(jnp.float32)
+            total = straight(total).astype(jnp.bfloat16)
+            for d in range(out_ref.shape[0]):
+                out_ref[d, g, :, lanes] = total
+
+
 def entries(source, rows, part):
     tiles = []
     for i in range(16):
         lanes = slice((i % 2) * LANES, (i % 2 + 1) * LANES)
-        tiles.append(straight(source[part * 8 + i // 2, rows, lanes].astype(jnp.float32)))
+        tiles.append(source[part * 8 + i // 2, rows, lanes].astype(jnp.float32))
     return swap_blocks(tiles)
 
 
@@ -438,7 +498,7 @@
     per = db // 2
     bf16, f32 = jnp.bfloat16, jnp.float32
     shape = jax.ShapeDtypeStruct
-    pt, qt, qc, qs, pc, ps = transform_tables(block)
+    pt, qt, qf, pc, ps = transform_tables(block)
     norm = float(np.asarray(1.0 / math.sqrt(block), jnp.bfloat16))
 
     tokens_other = lax.ppermute(tokens, "mp", swap)
@@ -448,29 +508,27 @@
     down_got = lax.ppermute(jnp.where(core == 0, down[:, 1], down[:, 0]), "mp", swap)
 
     inputs = (
-        gate_spectra, up_spectra, pt, tokens, cotangent, down_own, down_got, tokens_other, cotangent_other, qc, qs, pc, ps
+        gate_spectra, up_spectra, pt, tokens, cotangent, down_own, down_got, tokens_other, cotangent_other, qf, pc, ps
     )
     buffers = [shape((db, fb, block), bf16) if n == 5 else a for n, a in enumerate(inputs) if n != 6]
-    d_all, own, other = call(
+    spec = shape((pairs, 2, 2, ROWS // 2, PAIR, LANES), bf16)
+    d_all, gg, ug = call(
         functools.partial(main_kernel, fb, norm),
-        (
-            shape((pairs, 3 * ROWS, 2 * LANES), bf16),
-            shape((pairs, 2, per, PAIR, LANES), f32),
-            shape((pairs, 2, per, PAIR, LANES), bf16),
-        ),
+        (shape((pairs, 3 * ROWS, 2 * LANES), bf16), spec, spec),
         inputs,
         [pltpu.VMEM(a.shape, bf16) for a in buffers]
         + [pltpu.VMEM((pairs, 2, 2, db // 2, PAIR, LANES), bf16)] * 2
         + [pltpu.VMEM((fb, pairs, 2, PAIR, LANES), bf16)] * 3
-        + [pltpu.VMEM((pairs, 2, 2, ROWS // 2, PAIR, LANES), bf16)] * 3
+        + [pltpu.VMEM(spec.shape, bf16)] * 3
         + [pltpu.VMEM((groups * 2 * ROWS, LANES), f32)] * 3
-        + [pltpu.VMEM((2, groups * 2 * db, LANES), f32)] * 2
-        + [pltpu.VMEM((2, block // LANES, fb * db, LANES), f32), pltpu.VMEM((2, db, PAIR, LANES), f32)]
-        + [pltpu.SemaphoreType.DMA((len(inputs),))],
+        + [pltpu.VMEM((2, 3, half, 2 * LANES), bf16)] * 2
+        + [pltpu.VMEM((2, 3, F, 2 * LANES), f32), pltpu.VMEM((2, block // LANES, fb * db, LANES), f32)]
+        + [pltpu.SemaphoreType.DMA((len(inputs),)), pltpu.SemaphoreType.DMA((2,))],
         mib=63,
         flops=10**10,
         moved=10**7,
         in_specs=[HBM] * len(inputs),
+        out_specs=(VMEM, HBM, HBM),
     )
 
     direct = pairs % n_dp == 0
@@ -480,13 +538,26 @@
     else:
         share = pairs
         got = lax.psum(d_all.astype(f32), "dp")[None]
+    own, other = call(
+        functools.partial(adjoint_kernel, fb),
+        (shape((pairs, 2, per, PAIR, LANES), f32), shape((pairs, 2, per, PAIR, LANES), bf16)),
+        (gate_spectra, up_spectra, gg, ug),
+        [pltpu.VMEM(gate_spectra.shape, bf16)] * 2
+        + [pltpu.VMEM(spec.shape, bf16)] * 2
+        + [pltpu.VMEM((2, groups * 2 * db, LANES), f32)] * 2
+        + [pltpu.VMEM((2, 2, db, PAIR, LANES), f32)]
+        + [pltpu.SemaphoreType.DMA((2,)), pltpu.SemaphoreType.DMA((2, pairs))],
+        mib=63,
+        flops=2 * 10**9,
+        moved=10**7,
+        in_specs=[HBM] * 4,
+    )
+    total = call(reduce_kernel, shape((n_dp if direct else 1, share, 3 * ROWS, 2 * LANES), bf16), (got,), moved=10**6)
+    total, own, other = lax.optimization_barrier((total, own, other))
     partner = lax.ppermute(other, "mp", swap)
     grad_tokens = call(
         input_kernel, shape(tokens.shape, bf16), (own, partner, qt), flops=5 * 10**8, moved=4 * 10**6
     )
-
-    total = call(reduce_kernel, shape((n_dp if direct else 1, share, 3 * ROWS, 2 * LANES), bf16), (got,), moved=10**6)
-    total, grad_tokens = lax.optimization_barrier((total, grad_tokens))
     if direct:
         total = lax.all_to_all(total, "dp", 0, 0, tiled=True)
     total = total.reshape(pairs, 3 * ROWS, 2 * LANES)

time: 67.7 us -> 60.6 us (0.90)
  blocking collectives: 15.7 us -> 0 us
  waiting for transfers between devices: 10 us -> 17.7 us
  starting transfers between devices: 8.46 us -> 11.9 us
  Pallas kernels: 28.9 us -> 27.5 us
  local copies, waits for them, and re-layouts: 2.93 us -> 1.71 us
    all_to_all x1 -> x0, blocking collectives: 15.7 us -> none  [shards(): total = lax.all_to_all(total, 'dp', 0, 0, tiled=True)]
    all_to_all x0 -> x1, waiting for transfers between devices: none -> 11.9 us  [shards(): total = lax.all_to_all(total, 'dp', 0, 0, tiled=True)]
    all_to_all x0 -> x1, starting transfers between devices: none -> 3.64 us  [shards(): total = lax.all_to_all(total, 'dp', 0, 0, tiled=True)]
    ppermute x1, waiting for transfers between devices: 2.11 us -> 0.01 us  [shards(): partner = lax.ppermute(other, 'mp', swap)]
    all_to_all x1, waiting for transfers between devices: 7 us -> 4.95 us  [shards(): lax.all_to_all(d_all.reshape(n_dp, share, 3 * ROWS, 2 * LANES), 'dp', 0,...]
    pallas_call x5 -> x6, Pallas kernels: 28.9 us -> 27.5 us  [call(): pl.pallas_call(kernel, out_shape=out_shape, in_specs=in_specs or [VMEM] *...]
    unnamed x8, local copies, waits for them, and re-layouts: 2.04 us -> 0.81 us
  transfers between devices with their start and end apart: 6 -> 7, of which waited for: 3 -> 3; matrix products, arithmetic and copies ran while one was open for 2% -> 3% of each run, Pallas kernels for 4% -> 17%
where the time goes in v5:
time: 60.6 us; the launch traced here: 60.2 us
  Pallas kernels  27.5 us (45%)
  waiting for transfers between devices  17.7 us (29%)
  starting transfers between devices  11.9 us (20%)
  local copies, waits for them, and re-layouts  1.71 us (3%)
  between operations  0.72 us (1%)
  other arithmetic  0.66 us (1%)
    pallas_call x6, Pallas kernels, call(): pl.pallas_call(kernel, out_shape=out_shape, in_specs=in_specs or [VMEM] *...  27.5 us
    all_to_all x1, waiting for transfers between devices, shards(): total = lax.all_to_all(total, 'dp', 0, 0, tiled=True)  11.9 us
    all_to_all x1, starting transfers between devices, shards(): lax.all_to_all(d_all.reshape(n_dp, share, 3 * ROWS, 2 * LANES), 'dp', 0,...  7.16 us
    all_to_all x1, waiting for transfers between devices, shards(): lax.all_to_all(d_all.reshape(n_dp, share, 3 * ROWS, 2 * LANES), 'dp', 0,...  4.95 us
    all_to_all x1, starting transfers between devices, shards(): total = lax.all_to_all(total, 'dp', 0, 0, tiled=True)  3.64 us
  transfers between devices with their start and end apart: 7, of which 3 were waited for; matrix products, arithmetic and copies ran while one was open for 3% of the time, Pallas kernels for 17%

profile of v5, /device:TPU:0, one launch (start us, length us, event | category | flops | bytes accessed | tf_op | source)
XLA Modules:
  0.0 60.2 jit_solution(7354643769084093459)
XLA Ops:
  0.6 0.6 collective-permute-start.1
  1.2 0.1 collective-permute-start.2
  1.3 0.9 %fusion = (bf16[4,1,14,512]{3,0,2,1:T(4,128)(2,1)S(1)}, bf16[4,1,14,512]{3,0,2,1:T(4,128)(2,1)S(1)}) fusion(bf16[4,2,14,512]{3,0,2,1:T(4,128)(2,1)} %bitcast.14), kind=kLoop, calls=%fused_computation.2 | loop fusion | bytes 229376 | tf_op jit(solution)/shard_map/slice | solution.py:507
  2.2 0.7 %select_bitcast_fusion = (bf16[4,14,512]{2,1,0:T(8,128)(2,1)S(1)}, bf16[4,14,512]{2,1,0:T(8,128)(2,1)}) fusion(pred[]{:T(512)S(6)} %eq.4, bf16[4,1,14,512]{3,0,2,1:T(4,128)(2,1)S(1)} %get-tuple-element.27, bf16[4,1,14,512]{3,0,2,1:T(4,128)(2,1)S(1)} %get-tuple-element.26), kind=kLoop, calls=%fused_computation | loop fusion | flops 57344 | bytes 229377 | tf_op jit(solution)/shard_map/jit(_where)/select_n | solution.py:508
  2.8 0.4 collective-permute-start
  3.2 0.9 %collective-permute-done.wd_other_in = bf16[4,14,512]{2,1,0:T(8,128)(2,1)S(1)} collective-permute-done((bf16[4,14,512]{2,1,0:T(8,128)(2,1)S(1)}, bf16[4,14,512]{2,1,0:T(8,128)(2,1)S(1)}, u32[]{:S(2)}, u32[]{:S(2)}) %collective-permute-start) | collective-permute-done | bytes 57376 | tf_op jit(solution)/shard_map/ppermute | solution.py:508
  4.2 0.0 collective-permute-done.1.x_other_in
  4.2 0.0 collective-permute-done.2.c_other_in
  4.2 0.6 %copy-done.3 = bf16[4,14,512]{2,1,0:T(8,128)(2,1)} copy-done((bf16[4,14,512]{2,1,0:T(8,128)(2,1)}, bf16[4,14,512]{2,1,0:T(8,128)(2,1)S(1)}, u32[]{:S(2)}) %copy-start.3) | copy-done | bytes 57368
  4.8 0.2 copy-done.2
  5.0 15.2 %shard_map.129 = (bf16[16,48,256]{2,1,0:T(8,128)(2,1)}, bf16[16,2,2,8,16,128]{5,4,3,2,1,0:T(8,128)(2,1)}, bf16[16,2,2,8,16,128]{5,4,3,2,1,0:T(8,128)(2,1)}) custom-call(bf16[14,8,512]{2,1,0:T(8,128)(2,1)} %wg_in.3, bf16[14,8,512]{2,1,0:T(8,128)(2,1)} %wu_in.3, bf16[512,512]{1,0:T(8,128)(2,1)} %constant.16.clone.pt_in, bf16[128,2048]{1,0:T(8,128)(2,1)} %x_own_in.1, ...), custom_call_target="tpu_custom_call" | custom-call | flops 10000000000 | bytes 10000000 | tf_op jit(solution)/shard_map/pallas_call | solution.py:478
  20.2 7.2 %all-to-all-start = ((bf16[8,2,48,256]{3,2,1,0:T(8,128)(2,1)}), bf16[8,2,48,256]{3,2,1,0:T(8,128)(2,1)S(1)}, u32[]{:S(2)}, u32[]{:S(2)}) async-start(bf16[8,2,48,256]{3,2,1,0:T(8,128)(2,1)} %bitcast.12), calls=%async_computation | async-start | bytes 786432 | tf_op jit(solution)/shard_map/all_to_all | solution.py:537
  27.4 7.0 %shard_map.131 = (f32[16,2,4,16,128]{4,3,2,1,0:T(8,128)}, bf16[16,2,4,16,128]{4,3,2,1,0:T(8,128)(2,1)}) custom-call(bf16[14,8,512]{2,1,0:T(8,128)(2,1)} %wg_in.3, bf16[14,8,512]{2,1,0:T(8,128)(2,1)} %wu_in.3, bf16[16,2,2,8,16,128]{5,4,3,2,1,0:T(8,128)(2,1)} %get-tuple-element.15.gg_in, bf16[16,2,2,8,16,128]{5,4,3,2,1,0:T(8,128)(2,1)} %get-tuple-element.16.ug_in), custom_call_target="tpu_custom_call" | custom-call | flops 2000000000 | bytes 10000000 | tf_op jit(solution)/shard_map/pallas_call | solution.py:478
  34.4 0.0 copy-start.1
  34.4 5.0 %all-to-all-done.r_ref = bf16[8,2,48,256]{3,2,1,0:T(8,128)(2,1)S(1)} async-done(((bf16[8,2,48,256]{3,2,1,0:T(8,128)(2,1)}), bf16[8,2,48,256]{3,2,1,0:T(8,128)(2,1)S(1)}, u32[]{:S(2)}, u32[]{:S(2)}) %all-to-all-start) | async-done | bytes 393248 | tf_op jit(solution)/shard_map/all_to_all | solution.py:537
  39.4 0.8 %shard_map.130 = bf16[8,2,48,256]{3,2,1,0:T(8,128)(2,1)} custom-call(bf16[8,2,48,256]{3,2,1,0:T(8,128)(2,1)S(1)} %all-to-all-done.r_ref), custom_call_target="tpu_custom_call" | custom-call | bytes 1000000 | tf_op jit(solution)/shard_map/pallas_call | solution.py:478
  40.2 3.6 %all-to-all-start.1 = ((bf16[8,2,48,256]{3,2,1,0:T(8,128)(2,1)}), bf16[8,2,48,256]{3,2,1,0:T(8,128)(2,1)S(1)}, u32[]{:S(2)}, u32[]{:S(2)}) async-start(bf16[8,2,48,256]{3,2,1,0:T(8,128)(2,1)} %shard_map.130), calls=%async_computation.1 | async-start | bytes 786432 | tf_op jit(solution)/shard_map/all_to_all | solution.py:562
  43.8 0.0 collective-permute-start.3
  43.8 11.9 %all-to-all-done.1 = bf16[8,2,48,256]{3,2,1,0:T(8,128)(2,1)S(1)} async-done(((bf16[8,2,48,256]{3,2,1,0:T(8,128)(2,1)}), bf16[8,2,48,256]{3,2,1,0:T(8,128)(2,1)S(1)}, u32[]{:S(2)}, u32[]{:S(2)}) %all-to-all-start.1) | async-done | bytes 393248 | tf_op jit(solution)/shard_map/all_to_all | solution.py:562
  55.7 0.1 collective-permute-start.4
  55.8 0.0 collective-permute-done.3.got_ref
  55.8 1.6 %shard_map.132 = bf16[128,2048]{1,0:T(8,128)(2,1)} custom-call(f32[16,2,4,16,128]{4,3,2,1,0:T(8,128)S(1)} %copy-done, bf16[16,2,4,16,128]{4,3,2,1,0:T(8,128)(2,1)S(1)} %collective-permute-done.3.got_ref, bf16[512,512]{1,0:T(8,128)(2,1)S(1)} %copy-done.1), custom_call_target="tpu_custom_call" | custom-call | flops 500000000 | bytes 4000000 | tf_op jit(solution)/shard_map/pallas_call | solution.py:478
  57.4 1.4 %shard_map.133 = (f32[112,512]{1,0:T(8,128)}, f32[112,512]{1,0:T(8,128)}) custom-call(bf16[16,48,256]{2,1,0:T(8,128)(2,1)S(1)} %bitcast.11), custom_call_target="tpu_custom_call" | custom-call | bytes 1000000 | tf_op jit(solution)/shard_map/pallas_call | solution.py:478
  58.8 1.4 %shard_map.134 = f32[28,4,512]{2,1,0:T(4,128)} custom-call(bf16[16,16,256]{2,1,0:T(8,128)(2,1)S(1)} %slice.16.own_ref, bf16[16,16,256]{2,1,0:T(8,128)(2,1)S(1)} %collective-permute-done.4.got_ref), custom_call_target="tpu_custom_call" | custom-call | bytes 1000000 | tf_op jit(solution)/shard_map/pallas_call | solution.py:478
  (7 shorter events, 0.0 us)
Async XLA Ops:
  0.6 3.5 %collective-permute-start.1 = (bf16[128,2048]{1,0:T(8,128)(2,1)}, bf16[128,2048]{1,0:T(8,128)(2,1)S(1)}, u32[]{:S(2)}, u32[]{:S(2)}) collective-permute-start(bf16[128,2048]{1,0:T(8,128)(2,1)} %x_own_in.1), channel_id=1, source_target_pairs={{0,1},{1,0},{2,3},{3,2},{4,5},{5,4},{6,7},{7,6},{8,9},{9,8},{10,11... | collective-permute-start | bytes 1572872 | tf_op jit(solution)/shard_map/ppermute | solution.py:504
  1.2 3.0 %collective-permute-start.2 = (bf16[128,2048]{1,0:T(8,128)(2,1)}, bf16[128,2048]{1,0:T(8,128)(2,1)}, u32[]{:S(2)}, u32[]{:S(2)}) collective-permute-start(bf16[128,2048]{1,0:T(8,128)(2,1)} %c_own_in.1), channel_id=1, source_target_pairs={{0,1},{1,0},{2,3},{3,2},{4,5},{5,4},{6,7},{7,6},{8,9},{9,8},{10,11... | collective-permute-start | bytes 1572872 | tf_op jit(solution)/shard_map/ppermute | solution.py:505
  2.8 1.3 %collective-permute-start = (bf16[4,14,512]{2,1,0:T(8,128)(2,1)S(1)}, bf16[4,14,512]{2,1,0:T(8,128)(2,1)S(1)}, u32[]{:S(2)}, u32[]{:S(2)}) collective-permute-start(bf16[4,14,512]{2,1,0:T(8,128)(2,1)S(1)} %get-tuple-element.24), channel_id=1, source_target_pairs={{0,1},{1,0},{2,3},{3,2},{4,5},{5,4},{6,7},{7,6},{8,9},{9,8},{10,11... | collective-permute-start | bytes 172040 | tf_op jit(solution)/shard_map/ppermute | solution.py:508
  4.2 0.6 %copy-start.3 = (bf16[4,14,512]{2,1,0:T(8,128)(2,1)}, bf16[4,14,512]{2,1,0:T(8,128)(2,1)S(1)}, u32[]{:S(2)}) copy-start(bf16[4,14,512]{2,1,0:T(8,128)(2,1)S(1)} %collective-permute-done.wd_other_in) | copy-start | bytes 172036
  4.2 0.8 %copy-start.2 = (bf16[128,2048]{1,0:T(8,128)(2,1)}, bf16[128,2048]{1,0:T(8,128)(2,1)S(1)}, u32[]{:S(2)}) copy-start(bf16[128,2048]{1,0:T(8,128)(2,1)S(1)} %collective-permute-done.1.x_other_in) | copy-start | bytes 1572868
  20.2 19.2 %all-to-all-start = ((bf16[8,2,48,256]{3,2,1,0:T(8,128)(2,1)}), bf16[8,2,48,256]{3,2,1,0:T(8,128)(2,1)S(1)}, u32[]{:S(2)}, u32[]{:S(2)}) async-start(bf16[8,2,48,256]{3,2,1,0:T(8,128)(2,1)} %bitcast.12), calls=%async_computation | async-start | bytes 786432 | tf_op jit(solution)/shard_map/all_to_all | solution.py:537
  34.4 21.4 %copy-start = (f32[16,2,4,16,128]{4,3,2,1,0:T(8,128)S(1)}, f32[16,2,4,16,128]{4,3,2,1,0:T(8,128)}, u32[]{:S(2)}) copy-start(f32[16,2,4,16,128]{4,3,2,1,0:T(8,128)} %get-tuple-element.19.own_ref) | copy-start | bytes 3145732
  34.4 21.4 %copy-start.1 = (bf16[512,512]{1,0:T(8,128)(2,1)S(1)}, bf16[512,512]{1,0:T(8,128)(2,1)}, u32[]{:S(2)}) copy-start(bf16[512,512]{1,0:T(8,128)(2,1)} %constant.17.clone.qt_ref) | copy-start | bytes 1572868
  40.2 15.5 %all-to-all-start.1 = ((bf16[8,2,48,256]{3,2,1,0:T(8,128)(2,1)}), bf16[8,2,48,256]{3,2,1,0:T(8,128)(2,1)S(1)}, u32[]{:S(2)}, u32[]{:S(2)}) async-start(bf16[8,2,48,256]{3,2,1,0:T(8,128)(2,1)} %shard_map.130), calls=%async_computation.1 | async-start | bytes 786432 | tf_op jit(solution)/shard_map/all_to_all | solution.py:562
  43.8 12.0 %collective-permute-start.3 = (bf16[16,2,4,16,128]{4,3,2,1,0:T(8,128)(2,1)}, bf16[16,2,4,16,128]{4,3,2,1,0:T(8,128)(2,1)S(1)}, u32[]{:S(2)}, u32[]{:S(2)}) collective-permute-start(bf16[16,2,4,16,128]{4,3,2,1,0:T(8,128)(2,1)} %get-tuple-element.20), channel_id=1, source_target_pairs={{0,1},{1,0},{2,3},{3,2},{4,5},{5,4},{6,7},{7,6},{8,9},{9,8},{10,11... | collective-permute-start | bytes 1572872 | tf_op jit(solution)/shard_map/ppermute | solution.py:557
  55.7 3.1 %collective-permute-start.4 = (bf16[16,16,256]{2,1,0:T(8,128)(2,1)S(1)}, bf16[16,16,256]{2,1,0:T(8,128)(2,1)S(1)}, u32[]{:S(2)}, u32[]{:S(2)}) collective-permute-start(bf16[16,16,256]{2,1,0:T(8,128)(2,1)S(1)} %slice.16.own_ref), channel_id=1, source_target_pairs={{0,1},{1,0},{2,3},{3,2},{4,5},{5,4},{6,7},{7,6},{8,9},{9,8},{10,11... | collective-permute-start | bytes 393224 | tf_op jit(solution)/shard_map/ppermute | solution.py:565
